TPU v7x, 32 devices: a whole 2x2x4 slice. The times are simulated.
32 devices in a mesh: tile: 8 (over y, x, core), sec: 4 (over z).
Axes of the slice: x: 2, y: 2, z: 4, core: 2. Of those that a mesh axis runs over, the one named last changes fastest.
Arguments:
- pixels: bfloat16 [8, 64, 1024, 256], P('sec', 'tile'), may hold values from -6 to 6
- pred_features: bfloat16 [64, 1024, 128], P('tile'), may hold values from -6 to 6
- offsets: int32 [8, 2, 64, 1024], P('sec', None, 'tile'), may hold values from -1 to 1
- valid_mask: int32 [8, 64, 1024], P('sec', 'tile'), may hold values 0 or 1
- base_shift: float32 [2, 64, 1024], P(None, 'tile'), may hold values from -6 to 6
- w_hidden: bfloat16 [256, 512], replicated, may hold values from -0.375 to 0.375
- w_feature: bfloat16 [512, 128], replicated, may hold values from -0.25 to 0.25
- feat_gain: float32 [128], replicated, may hold values from 0.25 to 1.75
Outputs:
- displacement: float32 [8, 2, 64, 1024], P('sec', None, 'tile')
All inputs are finite; a program needn't handle non-finite values. No bound on the sum of `valid_mask` on one device may be relied on, other than what follows from the above.
Results may differ from a plain program's by a relative error of at most 0.0024.
Values may be sent and summed in bfloat16 or wider, within the bound.
No kernel may reach another device: no remote copies, remote signals or barrier semaphores. Data moves between devices by JAX's collectives and lax.ppermute only.
A program may use at most 128 MiB of HBM per device.

v0:
```python
import functools

import jax
import jax.numpy as jnp
from jax import lax
from jax.experimental import pallas as pl
from jax.experimental.pallas import tpu as pltpu
from jax.sharding import PartitionSpec as P


ITERS = 8
REACH = 2
LANES = 128
BASE = 16
PAD = LANES
SEG = 16
EDGE = 16

epsilon = 1e-05
step_size = 0.2
stiffness = 0.5

F32 = jnp.float32
BF16 = jnp.bfloat16
HBM = pl.BlockSpec(memory_space=pl.ANY)
VMEM = pl.BlockSpec(memory_space=pltpu.VMEM)


def hop(value, axis, steps):
    count = lax.axis_size(axis)
    pairs = [(i, i + steps) for i in range(count) if 0 <= i + steps < count]
    return lax.ppermute(value, axis, pairs)


def hop_plane(value, steps):
    tiles = lax.axis_size("tile")
    secs = lax.axis_size("sec")
    pairs = [(i * secs, (i + steps) * secs) for i in range(tiles) if 0 <= i + steps < tiles]
    return lax.ppermute(value, ("tile", "sec"), pairs)


def params(limit=48):
    return pltpu.CompilerParams(vmem_limit_bytes=limit * 1024 * 1024)


def matmuls(pix, wh, wf):
    hidden = jnp.maximum(jnp.dot(pix, wh, preferred_element_type=F32), 0.0).astype(BF16)
    return jnp.dot(hidden, wf, preferred_element_type=F32)


def normed(pre, gain):
    mean = jnp.mean(pre * pre, axis=-1, keepdims=True)
    return (pre * lax.rsqrt(mean + epsilon) * gain).astype(BF16)


def encode_rows(pieces, store, pix_ref, wh_ref, wf_ref, gain_ref, pix_s, pre_s, sem):
    width = pix_s.shape[1]
    copies = []
    for n, (sec, row, col0) in enumerate(pieces):
        copy = pltpu.make_async_copy(
            pix_ref.at[sec, row, col0 : col0 + width, :], pix_s.at[n], sem.at[n]
        )
        copy.start()
        copies.append(copy)
    steps = len(pieces) // 2

    def finish(n):
        value = normed(pre_s[n % 2], gain_ref[...])
        store(2 * n, value[:width])
        store(2 * n + 1, value[width:])

    for n in range(steps):
        copies[2 * n].wait()
        copies[2 * n + 1].wait()
        pix = pix_s[2 * n : 2 * n + 2].reshape(2 * width, pix_s.shape[2])
        pre_s[n % 2] = matmuls(pix, wh_ref[...], wf_ref[...])
        if n:
            finish(n - 1)
    finish(steps - 1)


def encode_front_kernel(half, pix_ref, wh_ref, wf_ref, gain_ref, fwd_ref, pix_s, pre_s, sem):
    rows = pix_ref.shape[1]

    def store(n, value):
        fwd_ref[n] = value

    pieces = [(1, r, 0) for r in range(rows)]
    encode_rows(pieces, store, pix_ref, wh_ref, wf_ref, gain_ref, pix_s, pre_s, sem)


def encode_back_kernel(
    half, pix_ref, wh_ref, wf_ref, gain_ref, off_ref, mask_ref, bwd_ref, pix_s, pre_s, sem
):
    rows, cols = pix_ref.shape[1:3]
    width = pix_s.shape[1]
    first = half // LANES - 1
    for tile in range(cols // LANES - first):
        lanes = slice((first + tile) * LANES, (first + tile + 1) * LANES)
        extra = jnp.concatenate(
            [off_ref[0, 0, :, lanes], off_ref[0, 1, :, lanes], mask_ref[0, :, lanes], mask_ref[0, :, lanes]], 0
        )
        at = rows * width + tile * 4 * rows
        bwd_ref[at : at + 4 * rows, :] = extra.astype(F32).astype(BF16)

    def store(n, value):
        bwd_ref[n * width : (n + 1) * width, :] = value

    pieces = [(0, r, cols - width) for r in range(rows)]
    encode_rows(pieces, store, pix_ref, wh_ref, wf_ref, gain_ref, pix_s, pre_s, sem)


def border_rows(rows):
    return list(range(REACH)) + list(range(rows - REACH, rows))


def encode_border_kernel(
    half, pix_ref, wh_ref, wf_ref, gain_ref, fwd_ref, bwd_ref,
    border_ref, up_ref, down_ref, pix_s, pre_s, sem, csem,
):
    rows, cols = pix_ref.shape[1:3]
    width = fwd_ref.shape[1]
    copies = []

    def copy(src, dst):
        c = pltpu.make_async_copy(src, dst, csem.at[len(copies)])
        c.start()
        copies.append(c)

    for pack, row0 in ((up_ref, rows - REACH), (down_ref, 0)):
        for r in range(REACH):
            copy(
                bwd_ref.at[pl.ds((row0 + r + 1) * width - half, half), :],
                pack.at[r, half:cols, :],
            )
            copy(
                fwd_ref.at[row0 + r, half - 2 * EDGE : half, :],
                pack.at[r, cols : cols + 2 * EDGE, :],
            )

    def store(n, value):
        border_ref[n] = value
        lead = 0 if n < 2 * REACH else cols + 2 * EDGE
        pack = down_ref if n % (2 * REACH) < REACH else up_ref
        pack[n % REACH, lead : lead + half, :] = value

    pieces = [(0, r, 0) for r in border_rows(rows)] + [(1, r, half) for r in border_rows(rows)]
    encode_rows(pieces, store, pix_ref, wh_ref, wf_ref, gain_ref, pix_s, pre_s, sem)
    for c in copies:
        c.wait()


def encode_inner_kernel(half, pix_ref, wh_ref, wf_ref, gain_ref, inner_ref, pix_s, pre_s, sem):
    rows = pix_ref.shape[1]

    def store(n, value):
        inner_ref[n] = value

    inside = range(REACH, rows - REACH)
    pieces = [(0, r, 0) for r in inside] + [(1, r, half) for r in inside]
    encode_rows(pieces, store, pix_ref, wh_ref, wf_ref, gain_ref, pix_s, pre_s, sem)


def flops_of(nodes, patch, hid, feat):
    return pl.CostEstimate(
        flops=2 * nodes * hid * (patch + feat), bytes_accessed=nodes * 2 * (patch + feat), transcendentals=nodes
    )


def align(band, first, lift, row):
    band = pltpu.roll(band, (2 * LANES - first - BASE + 2 + lift) % LANES, 1)
    for shift in (1, 2, 4):
        band = jnp.where((row & shift) != 0, pltpu.roll(band, LANES - shift, 1), band)
    return band


def score_columns(q_s, ref_s, m_s, s_s, k, low):
    rows = q_s.shape[0]
    span = 2 * REACH + 1
    tall = LANES - low
    lane = lax.broadcasted_iota(jnp.int32, (8, LANES), 1)
    cols = pl.ds(pl.multiple_of(k * LANES + low, 16), tall)
    for rp in range(rows + 2 * REACH):
        j = rp % span
        start = pl.multiple_of(k * LANES + (PAD - BASE - SEG * j), 16)
        window = ref_s[rp, pl.ds(start, 2 * LANES), :]
        first = max(rp - 2 * REACH, 0)
        last = min(rp, rows - 1)
        query = q_s[first : last + 1, cols, :].reshape((last + 1 - first) * tall, q_s.shape[2])
        product = lax.dot_general(
            query, window, (((1,), (1,)), ((), ())), preferred_element_type=F32
        )
        for r in range(first, last + 1):
            for i in range(low // 8, LANES // 8):
                at = (r - first) * tall + 8 * i - low
                s = 8 * i + BASE - 4 + SEG * j
                near = product[at : at + 8, :LANES]
                far = product[at : at + 8, LANES:]
                if s + SEG <= LANES:
                    value, mask = near, (lane >= s) & (lane < s + SEG)
                elif s >= LANES:
                    value, mask = far, (lane >= s - LANES) & (lane < s + SEG - LANES)
                else:
                    value = jnp.where(lane >= s, near, far)
                    mask = (lane >= s) | (lane < s + SEG - LANES)
                dst = m_s.at[r, 8 * i : 8 * i + 8, :]
                if rp == r:
                    dst[...] = value
                else:
                    pltpu.store(dst, value, mask=mask)
        if rp > 2 * REACH and rp % 2:
            score_turn(m_s, s_s, rp - 2 * REACH - 1, k, low)


def score_turn(m_s, s_s, r, k, low):
    span = 2 * REACH + 1
    lane = lax.broadcasted_iota(jnp.int32, (8, LANES), 1)
    row = lax.broadcasted_iota(jnp.int32, (8, LANES), 0)
    groups = [jnp.zeros((8, LANES), F32)] * (low // 8)
    for i in range(low // 8, LANES // 8):
        one = align(m_s[r, 8 * i : 8 * i + 8, :], 8 * i, 0, row)
        two = align(m_s[r + 1, 8 * i : 8 * i + 8, :], 8 * i, 8, row)
        groups.append(jnp.where((lane & 8) != 0, two, one))
    turned = jnp.concatenate(groups, 0).T
    lanes = pl.ds(pl.multiple_of(k * LANES, LANES), LANES)
    for n in range(2):
        for j in range(span):
            a = (j - r - n) % span
            at = SEG * j + 8 * n
            s_s[r + n, SEG * a : SEG * a + 8, lanes] = turned[at : at + 8]


def score_job(q_s, ref_s, m_s, s_s, tiles, low=0):
    first = 1 if low else 0
    if low:
        score_columns(q_s, ref_s, m_s.at[0], s_s, 0, low)
    pairs, odd = (tiles - first) // 2, (tiles - first) % 2

    def body(n, carry):
        for m in range(2):
            score_columns(q_s, ref_s, m_s.at[m], s_s, 2 * n + m + first, 0)
        return carry

    lax.fori_loop(0, pairs, body, 0)
    if odd:
        score_columns(q_s, ref_s, m_s.at[0], s_s, tiles - 1, 0)


def flow_tile(s_s, oy, ox, lanes):
    y_low, y_high, x_low, x_high = oy < 0, oy > 0, ox < 0, ox > 0
    feat = F32(1.0 / LANES)
    by_row = {}
    for i in range(3):
        for b in range(5):
            v = [s_s[:, SEG * (i + d) + b, lanes] for d in range(3)]
            by_row[i, b] = jnp.where(y_low, v[0], jnp.where(y_high, v[2], v[1]))
    total = jnp.ones_like(oy)
    sum_y = jnp.zeros_like(oy)
    sum_x = jnp.zeros_like(oy)
    for i in range(3):
        for j in range(3):
            near = jnp.where(
                x_low, by_row[i, j], jnp.where(x_high, by_row[i, j + 2], by_row[i, j + 1])
            )
            near = near * feat
            weight = near * near
            total = total + weight
            if i != 1:
                sum_y = sum_y + weight * (i - 1)
            if j != 1:
                sum_x = sum_x + weight * (j - 1)
    return oy + sum_y / total, ox + sum_x / total


def flows_of(s_s, off_ref, flow_ref, tiles):
    def body(k, carry):
        lanes = pl.ds(pl.multiple_of(k * LANES, LANES), LANES)
        fy, fx = flow_tile(s_s, off_ref[0, :, lanes].astype(F32), off_ref[1, :, lanes].astype(F32), lanes)
        flow_ref[0, :, lanes] = fy
        flow_ref[1, :, lanes] = fx
        return carry

    lax.fori_loop(0, tiles, body, 0)


class Loads:
    def __init__(self, sem, first=0):
        self.sem, self.next, self.open = sem, first, []

    def __call__(self, src, dst):
        copy = pltpu.make_async_copy(src, dst, self.sem.at[self.next])
        copy.start()
        self.next += 1
        self.open.append(copy)

    def wait(self):
        for copy in self.open:
            copy.wait()
        self.open = []


def zero_sides(ref_s, cols):
    side = jnp.zeros((ref_s.shape[0], EDGE, ref_s.shape[2]), BF16)
    ref_s[:, PAD - EDGE : PAD, :] = side
    ref_s[:, PAD + cols : PAD + cols + EDGE, :] = side


def load_left(loads, border_ref, inner_ref, ref, row0, lanes, section):
    inner = inner_ref.shape[0] // 2
    at = section * 2 * REACH
    loads(border_ref.at[at : at + REACH], ref.at[row0 : row0 + REACH, lanes, :])
    loads(
        inner_ref.at[section * inner : (section + 1) * inner],
        ref.at[row0 + REACH : row0 + REACH + inner, lanes, :],
    )
    loads(
        border_ref.at[at + REACH : at + 2 * REACH],
        ref.at[row0 + REACH + inner : row0 + 2 * REACH + inner, lanes, :],
    )


def own_scores_kernel(
    half, fwd_ref, bwd_ref, border_ref, inner_ref, up_ref, down_ref,
    pred_ref, pup_ref, pdown_ref, off_ref, flow_ref, flow0_ref,
    q_s, ref_s, s_s, q0_s, ref0_s, m_s, sem,
):
    rows, cols = q_s.shape[:2]
    width = fwd_ref.shape[1]
    is_first = lax.axis_index("sec") == 0
    base0 = half - LANES
    loads = Loads(sem)
    loads(fwd_ref.at[:, 0:half, :], q_s.at[:, 0:half, :])
    load_left(loads, border_ref, inner_ref, q_s, 0, slice(half, cols), 1)
    load_left(loads, border_ref, inner_ref, ref_s, REACH, slice(PAD, PAD + half), 0)
    for r in range(rows):
        loads(
            bwd_ref.at[pl.ds((r + 1) * width - half, half), :],
            ref_s.at[r + REACH, PAD + half : PAD + cols, :],
        )
    loads(up_ref.at[:, 0:cols, :], ref_s.at[0:REACH, PAD : PAD + cols, :])
    loads(down_ref.at[:, 0:cols, :], ref_s.at[rows + REACH : rows + 2 * REACH, PAD : PAD + cols, :])
    zero_sides(ref_s, cols)
    at = loads.next
    loads.wait()
    flow0_ref[...] = jnp.zeros_like(flow0_ref)

    @pl.when(is_first)
    def _():
        loads0 = Loads(sem, at)
        for r in range(rows):
            loads0(
                bwd_ref.at[pl.ds(r * width, width), :],
                q0_s.at[r, LANES + half - width : LANES + half, :],
            )
        span = slice(base0, cols)
        to = slice(PAD, PAD + cols - base0)
        loads0(pred_ref.at[:, span, :], ref0_s.at[REACH : rows + REACH, to, :])
        loads0(pup_ref.at[:, span, :], ref0_s.at[0:REACH, to, :])
        loads0(pdown_ref.at[:, span, :], ref0_s.at[rows + REACH : rows + 2 * REACH, to, :])
        zero_sides(ref0_s, cols - base0)
        tiles = (cols - base0) // LANES
        loads0.wait()
        score_job(q0_s, ref0_s, m_s, s_s, tiles, LANES - EDGE)
        flows_of(s_s, off_ref.at[0, :, :, base0:cols], flow0_ref, tiles)

    score_job(q_s, ref_s, m_s, s_s, cols // LANES)
    flows_of(s_s, off_ref.at[1], flow_ref, cols // LANES)


def back_scores_kernel(
    half, q_ref, fwd_ref, border_ref, inner_ref, up_ref, down_ref, flow_ref,
    q_s, ref_s, s_s, off_s, m_s, sem,
):
    rows, span = q_s.shape[:2]
    width = fwd_ref.shape[1]
    cols = 2 * half
    lead = PAD + LANES
    gap = 2 * EDGE
    loads = Loads(sem)
    for r in range(rows):
        loads(q_ref.at[pl.ds(r * width, width), :], q_s.at[r, span - width : span, :])
    loads(fwd_ref.at[:, half - gap : half, :], ref_s.at[REACH : rows + REACH, lead - gap : lead, :])
    load_left(loads, border_ref, inner_ref, ref_s, REACH, slice(lead, lead + half), 1)
    pack = slice(cols, cols + gap + half)
    to = slice(lead - gap, lead + half)
    loads(up_ref.at[:, pack, :], ref_s.at[0:REACH, to, :])
    loads(down_ref.at[:, pack, :], ref_s.at[rows + REACH : rows + 2 * REACH, to, :])
    loads(q_ref.at[rows * width :, :], off_s)
    ref_s[:, lead + half : lead + half + EDGE, :] = jnp.zeros((rows + 2 * REACH, EDGE, LANES), BF16)
    loads.wait()
    tiles = span // LANES
    score_job(q_s, ref_s, m_s, s_s, tiles, LANES - EDGE)

    def body(k, carry):
        lanes = pl.ds(pl.multiple_of(k * LANES, LANES), LANES)
        extra = off_s[pl.ds(pl.multiple_of(k * 4 * rows, 4 * rows), 4 * rows), :].astype(F32)
        fy, fx = flow_tile(s_s, extra[:rows], extra[rows : 2 * rows], lanes)
        flow_ref[0, :, lanes] = fy
        flow_ref[1, :, lanes] = fx
        flow_ref[2, :, lanes] = extra[2 * rows : 3 * rows]
        return carry

    lax.fori_loop(0, tiles, body, 0)


def pairs_out(pack_ref, at, tops, bottoms):
    for n, (top, bottom) in enumerate(zip(tops, bottoms)):
        pack_ref[at + 16 * n : at + 16 * n + 16, :] = jnp.concatenate([top, bottom], 0).astype(BF16)
    return at + 16 * len(tops)


def front_scores_kernel(
    half, fwd_ref, up_ref, down_ref, pred_ref, pup_ref, pdown_ref, border_ref, inner_ref,
    off_ref, mask_ref, flow1_ref, flow0_ref, flow2_ref, flow_ref, pack_ref,
    q_s, ref_s, s_s, m_s, sem,
):
    rows = q_s.shape[0]
    cols = off_ref.shape[3]
    width = fwd_ref.shape[1]
    is_first = lax.axis_index("sec") == 0
    loads = Loads(sem)
    load_left(loads, border_ref, inner_ref, q_s, 0, slice(0, half), 0)
    at = loads.next
    span = slice(PAD, PAD + width)
    below = slice(rows + REACH, rows + 2 * REACH)

    @pl.when(is_first)
    def _():
        mine = Loads(sem, at)
        mine(pred_ref.at[:, 0:width, :], ref_s.at[REACH : rows + REACH, span, :])
        mine(pup_ref.at[:, 0:width, :], ref_s.at[0:REACH, span, :])
        mine(pdown_ref.at[:, 0:width, :], ref_s.at[below, span, :])
        mine.wait()

    @pl.when(jnp.logical_not(is_first))
    def _():
        mine = Loads(sem, at)
        mine(fwd_ref, ref_s.at[REACH : rows + REACH, span, :])
        mine(up_ref, ref_s.at[0:REACH, span, :])
        mine(down_ref, ref_s.at[below, span, :])
        mine.wait()

    loads.wait()
    ref_s[:, PAD - EDGE : PAD, :] = jnp.zeros((rows + 2 * REACH, EDGE, LANES), BF16)
    tiles = half // LANES
    score_job(q_s, ref_s, m_s, s_s, tiles)
    flow_ref[:, :, half:cols] = flow0_ref[:, :, LANES:]
    flows_of(s_s, off_ref.at[0], flow_ref, tiles)

    def tiles_of(ref, count):
        return [ref[:, n * LANES : (n + 1) * LANES] for n in range(count)]

    n = 0
    for ref, count in ((flow1_ref, cols // LANES), (flow_ref, cols // LANES), (flow2_ref, flow2_ref.shape[2] // LANES)):
        n = pairs_out(pack_ref, n, tiles_of(ref.at[0], count), tiles_of(ref.at[1], count))
    masks = []
    for ref, count in ((mask_ref.at[1], cols // LANES), (mask_ref.at[0], cols // LANES), (flow2_ref.at[2], flow2_ref.shape[2] // LANES)):
        masks += [m.astype(F32) for m in tiles_of(ref, count)]
    if len(masks) % 2:
        masks.append(masks[-1])
    pairs_out(pack_ref, n, masks[0::2], masks[1::2])


def relax_kernel(
    half, up_ref, down_ref, flow1_ref, flow3_ref, flow2_ref, mask_ref, f1_ref, f3_ref, msg_ref,
    field_s, pull_s, keep_s,
):
    rows, cols = flow1_ref.shape[1:]
    deep = rows + 2 * ITERS
    place = lax.axis_index("tile")
    count = lax.axis_size("tile")
    glob = place * rows + lax.broadcasted_iota(jnp.int32, (deep, LANES), 0) - ITERS
    inside = ((glob >= 0) & (glob < rows * count)).astype(F32)
    widths = (cols, cols, flow2_ref.shape[2])
    tiles = [w // LANES for w in widths]
    flows = (flow1_ref, flow3_ref, flow2_ref)
    own_masks = (mask_ref.at[1], mask_ref.at[0], flow2_ref.at[2])
    starts = [0, tiles[0], tiles[0] + tiles[1]]
    mask_at = 16 * sum(tiles)
    for job in range(3):
        for k in range(tiles[job]):
            lanes = slice(k * LANES, (k + 1) * LANES)
            at = 16 * (starts[job] + k)
            m_at = mask_at + 8 * (starts[job] + k)
            half_at = m_at // 16 * 16
            sub = slice(m_at - half_at, m_at - half_at + 8)
            upper = up_ref[at : at + 16, :].astype(F32)
            lower = down_ref[at : at + 16, :].astype(F32)
            m_up = up_ref[half_at : half_at + 16, :].astype(F32)[sub]
            m_down = down_ref[half_at : half_at + 16, :].astype(F32)[sub]
            weight = stiffness * jnp.concatenate(
                [m_up, own_masks[job][:, lanes].astype(F32), m_down], 0
            )
            keep_s[job, :, lanes] = (step_size - step_size * weight) * inside
            for c in range(2):
                flow = jnp.concatenate(
                    [upper[8 * c : 8 * c + 8], flows[job][c, :, lanes], lower[8 * c : 8 * c + 8]], 0
                )
                pull = step_size * weight * flow * inside
                pull_s[job, c, :, lanes] = pull
                field_s[job, c, :, lanes] = pull
    step = step_size * inside

    def body(n, carry):
        for job in range(3):
            for c in range(2):
                old = [field_s[job, c, :, k * LANES : (k + 1) * LANES] for k in range(tiles[job])]
                lane = lax.broadcasted_iota(jnp.int32, (deep, LANES), 1)
                nxt = [pltpu.roll(x, LANES - 1, 1) for x in old]
                prv = [pltpu.roll(x, 1, 1) for x in old]
                zero = jnp.zeros_like(old[0])
                for k in range(tiles[job]):
                    lanes = slice(k * LANES, (k + 1) * LANES)
                    right = jnp.where(lane == LANES - 1, nxt[k + 1] if k + 1 < tiles[job] else zero, nxt[k])
                    left = jnp.where(lane == 0, prv[k - 1] if k else zero, prv[k])
                    around = pltpu.roll(old[k], 1, 0) + pltpu.roll(old[k], deep - 1, 0) + left + right
                    field_s[job, c, :, lanes] = (
                        keep_s[job, :, lanes] * old[k] + step * around + pull_s[job, c, :, lanes]
                    )
        return carry

    lax.fori_loop(0, ITERS - 1, body, 0)
    is_first = lax.axis_index("sec") == 0
    seam = half - EDGE // 2
    mine = slice(ITERS, ITERS + rows)
    lead = half - LANES
    for c in range(2):
        for k in range(tiles[0]):
            lanes = slice(k * LANES, (k + 1) * LANES)
            col = lax.broadcasted_iota(jnp.int32, (rows, LANES), 1) + k * LANES
            one = field_s[0, c, mine, lanes]
            front = field_s[1, c, mine, lanes]
            if (k + 1) * LANES > seam:
                front = jnp.where((col < seam) | is_first, front, 0.0)
            total = one + front
            if k * LANES >= lead:
                back = field_s[2, c, mine, k * LANES - lead : (k + 1) * LANES - lead]
                total = total + jnp.where(col >= seam, back, 0.0)
            f1_ref[c, :, lanes] = one
            f3_ref[c, :, lanes] = front
            msg_ref[c, :, lanes] = total.astype(msg_ref.dtype)


def shards(pixels, pred, offsets, mask, base_shift, w_hidden, w_feature, feat_gain):
    secs, rows, cols, patch = pixels.shape
    hid, feat = w_feature.shape
    assert secs == 2 and rows == ITERS and feat == LANES and cols % (2 * LANES) == 0
    half = cols // 2
    width = half + EDGE
    inner = rows - 2 * REACH
    span = half + LANES
    deep = rows + 2 * REACH
    tail = 4 * rows * (span // LANES)
    gain = feat_gain.reshape(1, feat)
    shape = jax.ShapeDtypeStruct
    weights = (w_hidden, w_feature, gain)

    def encode(kernel, outs, extra, extra_specs, wide, more=()):
        return pl.pallas_call(
            functools.partial(kernel, half),
            out_shape=outs,
            in_specs=[HBM, VMEM, VMEM, VMEM] + extra_specs,
            out_specs=jax.tree.map(lambda _: VMEM, outs),
            scratch_shapes=[
                pltpu.VMEM((rows, wide, patch), BF16),
                pltpu.VMEM((2, 2 * wide, feat), F32),
                pltpu.SemaphoreType.DMA((rows,)),
                *more,
            ],
            compiler_params=params(),
            cost_estimate=flops_of(rows * wide, patch, hid, feat),
        )(pixels, *weights, *extra)

    pup = hop_plane(pred[rows - REACH :], 1)
    pdown = hop_plane(pred[:REACH], -1)
    fwd = encode(encode_front_kernel, shape((rows, width, feat), BF16), (), [], width)
    fwd_in = hop(fwd, "sec", 1)
    bwd = encode(
        encode_back_kernel, shape((rows * width + tail, feat), BF16),
        (offsets, mask), [VMEM, VMEM], width,
    )
    bwd_in = hop(bwd, "sec", -1)
    pack_cols = cols + 2 * EDGE + half
    border, up, down = encode(
        encode_border_kernel,
        (
            shape((4 * REACH, half, feat), BF16),
            shape((REACH, pack_cols, feat), BF16),
            shape((REACH, pack_cols, feat), BF16),
        ),
        (fwd, bwd), [HBM, HBM], half, (pltpu.SemaphoreType.DMA((4 * REACH,)),),
    )
    up_in = hop(up, "tile", 1)
    down_in = hop(down, "tile", -1)
    inside = encode(encode_inner_kernel, shape((2 * inner, half, feat), BF16), (), [], half)
    fup_in = hop(fwd_in[rows - REACH :], "tile", 1)
    fdown_in = hop(fwd_in[:REACH], "tile", -1)

    bands = SEG * (2 * REACH + 1)
    nodes = rows * cols

    def score_cost(part):
        return pl.CostEstimate(flops=int(part * nodes * 12 * 2 * 256 * 128), bytes_accessed=int(part * nodes * 512), transcendentals=0)

    flow1, flow0 = pl.pallas_call(
        functools.partial(own_scores_kernel, half),
        out_shape=(shape((2, rows, cols), F32), shape((2, rows, span), F32)),
        in_specs=[HBM] * 9 + [VMEM],
        out_specs=(VMEM, VMEM),
        scratch_shapes=[
            pltpu.VMEM((rows, cols, feat), BF16),
            pltpu.VMEM((deep, cols + 2 * PAD, feat), BF16),
            pltpu.VMEM((rows, bands, cols), F32),
            pltpu.VMEM((rows, span, feat), BF16),
            pltpu.VMEM((deep, span + 2 * PAD, feat), BF16),
            pltpu.VMEM((2, rows, LANES, LANES), F32),
            pltpu.SemaphoreType.DMA((32,)),
        ],
        compiler_params=params(),
        cost_estimate=score_cost(1.0),
        name="own_scores",
    )(fwd, bwd, border, inside, up_in, down_in, pred, pup, pdown, offsets)

    flow2 = pl.pallas_call(
        functools.partial(back_scores_kernel, half),
        out_shape=shape((3, rows, span), F32),
        in_specs=[HBM] * 6,
        out_specs=VMEM,
        scratch_shapes=[
            pltpu.VMEM((rows, span, feat), BF16),
            pltpu.VMEM((deep, span + 2 * PAD, feat), BF16),
            pltpu.VMEM((rows, bands, span), F32),
            pltpu.VMEM((tail, feat), BF16),
            pltpu.VMEM((2, rows, LANES, LANES), F32),
            pltpu.SemaphoreType.DMA((20,)),
        ],
        compiler_params=params(),
        cost_estimate=score_cost(0.55),
        name="back_scores",
    )(bwd_in, fwd, border, inside, up_in, down_in)

    tiles = 2 * (cols // LANES) + span // LANES
    pack_rows = 16 * tiles + 16 * ((tiles + 1) // 2)
    flow3, pack = pl.pallas_call(
        functools.partial(front_scores_kernel, half),
        out_shape=(shape((2, rows, cols), F32), shape((pack_rows, LANES), BF16)),
        in_specs=[HBM] * 8 + [VMEM] * 5,
        out_specs=(VMEM, VMEM),
        scratch_shapes=[
            pltpu.VMEM((rows, half, feat), BF16),
            pltpu.VMEM((deep, half + 3 * PAD, feat), BF16),
            pltpu.VMEM((rows, bands, half), F32),
            pltpu.VMEM((2, rows, LANES, LANES), F32),
            pltpu.SemaphoreType.DMA((12,)),
        ],
        compiler_params=params(),
        cost_estimate=score_cost(0.5),
        name="front_scores",
    )(fwd_in, fup_in, fdown_in, pred, pup, pdown, border, inside, offsets, mask, flow1, flow0, flow2)
    pack_up = hop(pack, "tile", 1)
    pack_down = hop(pack, "tile", -1)

    wide = rows + 2 * ITERS
    f1, f3, msg = pl.pallas_call(
        functools.partial(relax_kernel, half),
        out_shape=(shape((2, rows, cols), F32), shape((2, rows, cols), F32), shape((2, rows, cols), BF16)),
        in_specs=[VMEM] * 6,
        out_specs=(VMEM,) * 3,
        scratch_shapes=[
            pltpu.VMEM((3, 2, wide, cols), F32),
            pltpu.VMEM((3, 2, wide, cols), F32),
            pltpu.VMEM((3, wide, cols), F32),
        ],
        compiler_params=params(),
        cost_estimate=pl.CostEstimate(flops=nodes * 24 * 12 * 8, bytes_accessed=nodes * 40, transcendentals=0),
        name="relax",
    )(pack_up, pack_down, flow1, flow3, flow2, mask)

    prefix = base_shift
    for steps in range(1, lax.axis_size("sec")):
        prefix = prefix + hop(msg, "sec", steps).astype(F32)
    first = prefix + f3
    return jnp.stack([first, first + f1], axis=0)


def solution(mesh):
    in_specs = (
        P("sec", "tile", None, None),
        P("tile", None, None),
        P("sec", None, "tile", None),
        P("sec", "tile", None),
        P(None, "tile", None),
        P(),
        P(),
        P(),
    )
    out_specs = P("sec", None, "tile", None)
    return jax.shard_map(shards, mesh=mesh, in_specs=in_specs, out_specs=out_specs, check_vma=False)
```

profile of v0, /device:TPU:4, one launch (start us, length us, event | category | flops | bytes accessed | tf_op | source)
XLA Modules:
  0.0 111.7 jit_solution(18293696393565530176)
XLA Ops:
  0.0 0.9 copy-done.1
  1.0 0.9 copy-done.2
  1.9 0.7 copy-done.5
  2.5 4.6 %shard_map.82.fwd_ref = bf16[8,528,128]{2,1,0:T(8,128)(2,1)S(1)} custom-call(bf16[2,8,1024,256]{3,2,1,0:T(8,128)(2,1)} %pix_ref.7, bf16[256,512]{1,0:T(8,128)(2,1)S(1)} %copy-done.1, bf16[512,128]{1,0:T(8,128)(2,1)S(1)} %copy-done.2, f32[1,128]{1,0:T(1,128)S(1)} %bitcast.4), custom_call_target="tpu_custom_call" | custom-call | flops 1660944384 | bytes 3244032 | tf_op jit(solution)/shard_map/pallas_call | solution.py:559
  7.1 4.5 %shard_map.83.bwd_ref = bf16[4384,128]{1,0:T(8,128)(2,1)S(1)} custom-call(bf16[2,8,1024,256]{3,2,1,0:T(8,128)(2,1)} %pix_ref.7, bf16[256,512]{1,0:T(8,128)(2,1)S(1)} %copy-done.1, bf16[512,128]{1,0:T(8,128)(2,1)S(1)} %copy-done.2, f32[1,128]{1,0:T(1,128)S(1)} %bitcast.5, s32[2,2,8,1024]{3,2,1,0:T(8,128)S(1)} %copy-done.4, s32[2,8,1024]{2,1,0:T(8,128)S(1)} %copy-done.3), custom_call_target="tpu_custom_call" | custom-call | flops 1660944384 | bytes 3244032 | tf_op jit(solution)/shard_map/pallas_call | solution.py:559
  11.7 0.0 copy-start.7
  11.7 5.6 %shard_map.84 = (bf16[8,512,128]{2,1,0:T(8,128)(2,1)S(1)}, bf16[2,1568,128]{2,1,0:T(8,128)(2,1)S(1)}, bf16[2,1568,128]{2,1,0:T(8,128)(2,1)S(1)}) custom-call(bf16[2,8,1024,256]{3,2,1,0:T(8,128)(2,1)} %pix_ref.7, bf16[256,512]{1,0:T(8,128)(2,1)S(1)} %copy-done.1, bf16[512,128]{1,0:T(8,128)(2,1)S(1)} %copy-done.2, f32[1,128]{1,0:T(1,128)S(1)} %bitcast.6, ...), custom_call_target="tpu_custom_call" | custom-call | flops 1610612736 | bytes 3145728 | tf_op jit(solution)/shard_map/pallas_call | solution.py:559
  17.3 1.9 %collective-permute-start.5 = (bf16[2,1568,128]{2,1,0:T(8,128)(2,1)S(1)}, bf16[2,1568,128]{2,1,0:T(8,128)(2,1)S(1)}, u32[]{:S(2)}, u32[]{:S(2)}) collective-permute-start(bf16[2,1568,128]{2,1,0:T(8,128)(2,1)S(1)} %get-tuple-element.16), channel_id=1, source_target_pairs={{0,4},{4,8},{8,12},{12,16},{16,20},{20,24},{24,28},{1,5},{5,9},{9,... | collective-permute-start | bytes 2408456 | tf_op jit(solution)/shard_map/ppermute | solution.py:32
  19.2 4.5 %collective-permute-start.6 = (bf16[2,1568,128]{2,1,0:T(8,128)(2,1)S(1)}, bf16[2,1568,128]{2,1,0:T(8,128)(2,1)S(1)}, u32[]{:S(2)}, u32[]{:S(2)}) collective-permute-start(bf16[2,1568,128]{2,1,0:T(8,128)(2,1)S(1)} %get-tuple-element.17), channel_id=1, source_target_pairs={{4,0},{8,4},{12,8},{16,12},{20,16},{24,20},{28,24},{5,1},{9,5},{13... | collective-permute-start | bytes 2408456 | tf_op jit(solution)/shard_map/ppermute | solution.py:32
  23.8 0.1 fusion
  23.8 1.9 %collective-permute-start.3 = (bf16[2,1024,128]{2,1,0:T(8,128)(2,1)S(1)}, bf16[2,1024,128]{2,1,0:T(8,128)(2,1)S(1)}, u32[]{:S(2)}, u32[]{:S(2)}) collective-permute-start(bf16[2,1024,128]{2,1,0:T(8,128)(2,1)S(1)} %get-tuple-element.28), channel_id=1, source_target_pairs={{0,4},{4,8},{8,12},{12,16},{16,20},{20,24},{24,28}} | collective-permute-start | bytes 1572872 | tf_op jit(solution)/shard_map/ppermute | solution.py:39
  25.8 4.5 %collective-permute-start.4 = (bf16[2,1024,128]{2,1,0:T(8,128)(2,1)S(1)}, bf16[2,1024,128]{2,1,0:T(8,128)(2,1)S(1)}, u32[]{:S(2)}, u32[]{:S(2)}) collective-permute-start(bf16[2,1024,128]{2,1,0:T(8,128)(2,1)S(1)} %get-tuple-element.27), channel_id=1, source_target_pairs={{4,0},{8,4},{12,8},{16,12},{20,16},{24,20},{28,24}} | collective-permute-start | bytes 1572872 | tf_op jit(solution)/shard_map/ppermute | solution.py:39
  30.3 1.4 %collective-permute-start = (bf16[8,528,128]{2,1,0:T(8,128)(2,1)S(1)}, bf16[8,528,128]{2,1,0:T(8,128)(2,1)S(1)}, u32[]{:S(2)}, u32[]{:S(2)}) collective-permute-start(bf16[8,528,128]{2,1,0:T(8,128)(2,1)S(1)} %shard_map.82.fwd_ref), channel_id=1, source_target_pairs={{0,1},{1,2},{2,3},{4,5},{5,6},{6,7},{8,9},{9,10},{10,11},{12,13},{... | collective-permute-start | bytes 3244040 | tf_op jit(solution)/shard_map/ppermute | solution.py:32
  31.7 17.1 %collective-permute-done.3.pup_ref = bf16[2,1024,128]{2,1,0:T(8,128)(2,1)S(1)} collective-permute-done((bf16[2,1024,128]{2,1,0:T(8,128)(2,1)S(1)}, bf16[2,1024,128]{2,1,0:T(8,128)(2,1)S(1)}, u32[]{:S(2)}, u32[]{:S(2)}) %collective-permute-start.3) | collective-permute-done | bytes 524320 | tf_op jit(solution)/shard_map/ppermute | solution.py:39
  48.7 1.5 %collective-permute-start.7 = (bf16[4384,128]{1,0:T(8,128)(2,1)S(1)}, bf16[4384,128]{1,0:T(8,128)(2,1)S(1)}, u32[]{:S(2)}, u32[]{:S(2)}) collective-permute-start(bf16[4384,128]{1,0:T(8,128)(2,1)S(1)} %shard_map.83.bwd_ref), channel_id=1, source_target_pairs={{1,0},{2,1},{3,2},{5,4},{6,5},{7,6},{9,8},{10,9},{11,10},{13,12},{... | collective-permute-start | bytes 3366920 | tf_op jit(solution)/shard_map/ppermute | solution.py:32
  50.2 4.5 %shard_map.85.inner_ref = bf16[8,512,128]{2,1,0:T(8,128)(2,1)S(1)} custom-call(bf16[2,8,1024,256]{3,2,1,0:T(8,128)(2,1)} %pix_ref.7, bf16[256,512]{1,0:T(8,128)(2,1)S(1)} %copy-done.1, bf16[512,128]{1,0:T(8,128)(2,1)S(1)} %copy-done.2, f32[1,128]{1,0:T(1,128)S(1)} %bitcast.7), custom_call_target="tpu_custom_call" | custom-call | flops 1610612736 | bytes 3145728 | tf_op jit(solution)/shard_map/pallas_call | solution.py:559
  54.7 18.9 %own_scores.1 = (f32[2,8,1024]{2,1,0:T(8,128)S(1)}, f32[2,8,640]{2,1,0:T(8,128)S(1)}) custom-call(bf16[8,528,128]{2,1,0:T(8,128)(2,1)S(1)} %shard_map.82.fwd_ref, bf16[4384,128]{1,0:T(8,128)(2,1)} %copy-done, bf16[8,512,128]{2,1,0:T(8,128)(2,1)S(1)} %get-tuple-element.15.border_ref, bf16[8,512,128]{2,1,0:T(8,128)(2,1)S(1)} %shard_map.85.inner_ref, ...), custom_call_target="tpu_custom_call" | custom-call | flops 6442450944 | bytes 4194304 | tf_op jit(solution)/shard_map/own_scores/pallas_call | solution.py:605
  73.7 1.9 %collective-permute-start.1 = (bf16[2,528,128]{2,1,0:T(8,128)(2,1)S(1)}, bf16[2,528,128]{2,1,0:T(8,128)(2,1)S(1)}, u32[]{:S(2)}, u32[]{:S(2)}) collective-permute-start(bf16[2,528,128]{2,1,0:T(8,128)(2,1)S(1)} %get-tuple-element.30), channel_id=1, source_target_pairs={{0,4},{4,8},{8,12},{12,16},{16,20},{20,24},{24,28},{1,5},{5,9},{9,... | collective-permute-start | bytes 811016 | tf_op jit(solution)/shard_map/ppermute | solution.py:32
  75.6 4.5 %collective-permute-start.2 = (bf16[2,528,128]{2,1,0:T(8,128)(2,1)S(1)}, bf16[2,528,128]{2,1,0:T(8,128)(2,1)S(1)}, u32[]{:S(2)}, u32[]{:S(2)}) collective-permute-start(bf16[2,528,128]{2,1,0:T(8,128)(2,1)S(1)} %get-tuple-element.29), channel_id=1, source_target_pairs={{4,0},{8,4},{12,8},{16,12},{20,16},{24,20},{28,24},{5,1},{9,5},{13... | collective-permute-start | bytes 811016 | tf_op jit(solution)/shard_map/ppermute | solution.py:32
  80.2 7.5 %back_scores.1.flow2_ref = f32[3,8,640]{2,1,0:T(8,128)S(1)} custom-call(bf16[4384,128]{1,0:T(8,128)(2,1)S(1)} %collective-permute-done.7.q_ref, bf16[8,528,128]{2,1,0:T(8,128)(2,1)S(1)} %shard_map.82.fwd_ref, bf16[8,512,128]{2,1,0:T(8,128)(2,1)S(1)} %get-tuple-element.15.border_ref, bf16[8,512,128]{2,1,0:T(8,128)(2,1)S(1)} %shard_map.85.inner_ref, ...), custom_call_target="tpu_custom_call" | custom-call | flops 3543347968 | bytes 2306867 | tf_op jit(solution)/shard_map/back_scores/pallas_call | solution.py:624
  87.7 6.3 %front_scores.1 = (f32[2,8,1024]{2,1,0:T(8,128)S(1)}, bf16[512,128]{1,0:T(8,128)(2,1)S(1)}) custom-call(bf16[8,528,128]{2,1,0:T(8,128)(2,1)S(1)} %collective-permute-done.fwd_ref, bf16[2,528,128]{2,1,0:T(8,128)(2,1)S(1)} %collective-permute-done.1.up_ref, bf16[2,528,128]{2,1,0:T(8,128)(2,1)S(1)} %collective-permute-done.2.down_ref, ...), custom_call_target="tpu_custom_call" | custom-call | flops 3221225472 | bytes 2097152 | tf_op jit(solution)/shard_map/front_scores/pallas_call | solution.py:644
  94.0 1.9 %collective-permute-start.8 = (bf16[512,128]{1,0:T(8,128)(2,1)S(1)}, bf16[512,128]{1,0:T(8,128)(2,1)S(1)}, u32[]{:S(2)}, u32[]{:S(2)}) collective-permute-start(bf16[512,128]{1,0:T(8,128)(2,1)S(1)} %get-tuple-element.20), channel_id=1, source_target_pairs={{0,4},{4,8},{8,12},{12,16},{16,20},{20,24},{24,28},{1,5},{5,9},{9,... | collective-permute-start | bytes 393224 | tf_op jit(solution)/shard_map/ppermute | solution.py:32
  95.9 4.5 %collective-permute-start.9 = (bf16[512,128]{1,0:T(8,128)(2,1)S(1)}, bf16[512,128]{1,0:T(8,128)(2,1)S(1)}, u32[]{:S(2)}, u32[]{:S(2)}) collective-permute-start(bf16[512,128]{1,0:T(8,128)(2,1)S(1)} %get-tuple-element.20), channel_id=1, source_target_pairs={{4,0},{8,4},{12,8},{16,12},{20,16},{24,20},{28,24},{5,1},{9,5},{13... | collective-permute-start | bytes 393224 | tf_op jit(solution)/shard_map/ppermute | solution.py:32
  100.5 2.1 %collective-permute-done.8.up_ref = bf16[512,128]{1,0:T(8,128)(2,1)S(1)} collective-permute-done((bf16[512,128]{1,0:T(8,128)(2,1)S(1)}, bf16[512,128]{1,0:T(8,128)(2,1)S(1)}, u32[]{:S(2)}, u32[]{:S(2)}) %collective-permute-start.8) | collective-permute-done | bytes 131104 | tf_op jit(solution)/shard_map/ppermute | solution.py:32
  102.6 0.4 collective-permute-done.9.down_ref
  103.0 2.6 %relax.1 = (f32[2,8,1024]{2,1,0:T(8,128)S(1)}, f32[2,8,1024]{2,1,0:T(8,128)S(1)}, bf16[2,8,1024]{2,1,0:T(8,128)(2,1)S(1)}) custom-call(bf16[512,128]{1,0:T(8,128)(2,1)S(1)} %collective-permute-done.8.up_ref, bf16[512,128]{1,0:T(8,128)(2,1)S(1)} %collective-permute-done.9.down_ref, f32[2,8,1024]{2,1,0:T(8,128)S(1)} %get-tuple-element.18.flow1_ref, ...), custom_call_target="tpu_custom_call" | custom-call | flops 18874368 | bytes 327680 | tf_op jit(solution)/shard_map/relax/pallas_call | solution.py:664
  105.6 1.3 %collective-permute-start.10 = (bf16[2,8,1024]{2,1,0:T(8,128)(2,1)S(1)}, bf16[2,8,1024]{2,1,0:T(8,128)(2,1)S(1)}, u32[]{:S(2)}, u32[]{:S(2)}) collective-permute-start(bf16[2,8,1024]{2,1,0:T(8,128)(2,1)S(1)} %get-tuple-element.22), channel_id=1, source_target_pairs={{0,1},{1,2},{2,3},{4,5},{5,6},{6,7},{8,9},{9,10},{10,11},{12,13},{... | collective-permute-start | bytes 98312 | tf_op jit(solution)/shard_map/ppermute | solution.py:32
  106.9 1.3 %collective-permute-start.11 = (bf16[2,8,1024]{2,1,0:T(8,128)(2,1)S(1)}, bf16[2,8,1024]{2,1,0:T(8,128)(2,1)S(1)}, u32[]{:S(2)}, u32[]{:S(2)}) collective-permute-start(bf16[2,8,1024]{2,1,0:T(8,128)(2,1)S(1)} %get-tuple-element.22), channel_id=1, source_target_pairs={{0,2},{1,3},{4,6},{5,7},{8,10},{9,11},{12,14},{13,15},{16,18},{17,... | collective-permute-start | bytes 98312 | tf_op jit(solution)/shard_map/ppermute | solution.py:32
  108.2 1.3 %collective-permute-start.12 = (bf16[2,8,1024]{2,1,0:T(8,128)(2,1)S(1)}, bf16[2,8,1024]{2,1,0:T(8,128)(2,1)S(1)}, u32[]{:S(2)}, u32[]{:S(2)}) collective-permute-start(bf16[2,8,1024]{2,1,0:T(8,128)(2,1)S(1)} %get-tuple-element.22), channel_id=1, source_target_pairs={{0,3},{4,7},{8,11},{12,15},{16,19},{20,23},{24,27},{28,31}} | collective-permute-start | bytes 98312 | tf_op jit(solution)/shard_map/ppermute | solution.py:32
  109.5 0.3 collective-permute-done.11
  109.7 1.3 %collective-permute-done.12 = bf16[2,8,1024]{2,1,0:T(8,128)(2,1)S(1)} collective-permute-done((bf16[2,8,1024]{2,1,0:T(8,128)(2,1)S(1)}, bf16[2,8,1024]{2,1,0:T(8,128)(2,1)S(1)}, u32[]{:S(2)}, u32[]{:S(2)}) %collective-permute-start.12) | collective-permute-done | bytes 32800 | tf_op jit(solution)/shard_map/ppermute | solution.py:32
  111.1 0.7 pad_maximum_fusion
  (24 shorter events, 0.1 us)
Async XLA Ops:
  0.0 0.9 copy-start.1
  1.0 0.9 copy-start.2
  1.9 0.7 copy-start.5
  2.5 4.6 %copy-start.3 = (s32[2,8,1024]{2,1,0:T(8,128)S(1)}, s32[2,8,1024]{2,1,0:T(8,128)}, u32[]{:S(2)}) copy-start(s32[2,8,1024]{2,1,0:T(8,128)} %mask_ref.5) | copy-start | bytes 196612
  2.5 4.6 %copy-start.4 = (s32[2,2,8,1024]{3,2,1,0:T(8,128)S(1)}, s32[2,2,8,1024]{3,2,1,0:T(8,128)}, u32[]{:S(2)}) copy-start(s32[2,2,8,1024]{3,2,1,0:T(8,128)} %off_ref.5) | copy-start | bytes 393220
  11.7 37.1 %copy-start = (bf16[4384,128]{1,0:T(8,128)(2,1)}, bf16[4384,128]{1,0:T(8,128)(2,1)S(1)}, u32[]{:S(2)}) copy-start(bf16[4384,128]{1,0:T(8,128)(2,1)S(1)} %shard_map.83.bwd_ref) | copy-start | bytes 3366916
  11.7 12.1 %copy-start.7 = (bf16[8,1024,128]{2,1,0:T(8,128)(2,1)S(1)}, bf16[8,1024,128]{2,1,0:T(8,128)(2,1)}, u32[]{:S(2)}) copy-start(bf16[8,1024,128]{2,1,0:T(8,128)(2,1)} %pred_ref.3) | copy-start | bytes 6291460
  17.3 33.0 %copy-start.6 = (f32[128]{0:T(128)S(1)}, f32[128]{0:T(128)}, u32[]{:S(2)}) copy-start(f32[128]{0:T(128)} %param.15) | copy-start | bytes 1540
  17.3 37.4 %collective-permute-start.5 = (bf16[2,1568,128]{2,1,0:T(8,128)(2,1)S(1)}, bf16[2,1568,128]{2,1,0:T(8,128)(2,1)S(1)}, u32[]{:S(2)}, u32[]{:S(2)}) collective-permute-start(bf16[2,1568,128]{2,1,0:T(8,128)(2,1)S(1)} %get-tuple-element.16), channel_id=1, source_target_pairs={{0,4},{4,8},{8,12},{12,16},{16,20},{20,24},{24,28},{1,5},{5,9},{9,... | collective-permute-start | bytes 2408456 | tf_op jit(solution)/shard_map/ppermute | solution.py:32
  19.2 35.5 %collective-permute-start.6 = (bf16[2,1568,128]{2,1,0:T(8,128)(2,1)S(1)}, bf16[2,1568,128]{2,1,0:T(8,128)(2,1)S(1)}, u32[]{:S(2)}, u32[]{:S(2)}) collective-permute-start(bf16[2,1568,128]{2,1,0:T(8,128)(2,1)S(1)} %get-tuple-element.17), channel_id=1, source_target_pairs={{4,0},{8,4},{12,8},{16,12},{20,16},{24,20},{28,24},{5,1},{9,5},{13... | collective-permute-start | bytes 2408456 | tf_op jit(solution)/shard_map/ppermute | solution.py:32
  23.8 24.9 %collective-permute-start.3 = (bf16[2,1024,128]{2,1,0:T(8,128)(2,1)S(1)}, bf16[2,1024,128]{2,1,0:T(8,128)(2,1)S(1)}, u32[]{:S(2)}, u32[]{:S(2)}) collective-permute-start(bf16[2,1024,128]{2,1,0:T(8,128)(2,1)S(1)} %get-tuple-element.28), channel_id=1, source_target_pairs={{0,4},{4,8},{8,12},{12,16},{16,20},{20,24},{24,28}} | collective-permute-start | bytes 1572872 | tf_op jit(solution)/shard_map/ppermute | solution.py:39
  25.8 28.9 %collective-permute-start.4 = (bf16[2,1024,128]{2,1,0:T(8,128)(2,1)S(1)}, bf16[2,1024,128]{2,1,0:T(8,128)(2,1)S(1)}, u32[]{:S(2)}, u32[]{:S(2)}) collective-permute-start(bf16[2,1024,128]{2,1,0:T(8,128)(2,1)S(1)} %get-tuple-element.27), channel_id=1, source_target_pairs={{4,0},{8,4},{12,8},{16,12},{20,16},{24,20},{28,24}} | collective-permute-start | bytes 1572872 | tf_op jit(solution)/shard_map/ppermute | solution.py:39
  30.3 43.3 %collective-permute-start = (bf16[8,528,128]{2,1,0:T(8,128)(2,1)S(1)}, bf16[8,528,128]{2,1,0:T(8,128)(2,1)S(1)}, u32[]{:S(2)}, u32[]{:S(2)}) collective-permute-start(bf16[8,528,128]{2,1,0:T(8,128)(2,1)S(1)} %shard_map.82.fwd_ref), channel_id=1, source_target_pairs={{0,1},{1,2},{2,3},{4,5},{5,6},{6,7},{8,9},{9,10},{10,11},{12,13},{... | collective-permute-start | bytes 3244040 | tf_op jit(solution)/shard_map/ppermute | solution.py:32
  48.7 31.4 %collective-permute-start.7 = (bf16[4384,128]{1,0:T(8,128)(2,1)S(1)}, bf16[4384,128]{1,0:T(8,128)(2,1)S(1)}, u32[]{:S(2)}, u32[]{:S(2)}) collective-permute-start(bf16[4384,128]{1,0:T(8,128)(2,1)S(1)} %shard_map.83.bwd_ref), channel_id=1, source_target_pairs={{1,0},{2,1},{3,2},{5,4},{6,5},{7,6},{9,8},{10,9},{11,10},{13,12},{... | collective-permute-start | bytes 3366920 | tf_op jit(solution)/shard_map/ppermute | solution.py:32
  73.7 13.9 %collective-permute-start.1 = (bf16[2,528,128]{2,1,0:T(8,128)(2,1)S(1)}, bf16[2,528,128]{2,1,0:T(8,128)(2,1)S(1)}, u32[]{:S(2)}, u32[]{:S(2)}) collective-permute-start(bf16[2,528,128]{2,1,0:T(8,128)(2,1)S(1)} %get-tuple-element.30), channel_id=1, source_target_pairs={{0,4},{4,8},{8,12},{12,16},{16,20},{20,24},{24,28},{1,5},{5,9},{9,... | collective-permute-start | bytes 811016 | tf_op jit(solution)/shard_map/ppermute | solution.py:32
  75.6 12.0 %collective-permute-start.2 = (bf16[2,528,128]{2,1,0:T(8,128)(2,1)S(1)}, bf16[2,528,128]{2,1,0:T(8,128)(2,1)S(1)}, u32[]{:S(2)}, u32[]{:S(2)}) collective-permute-start(bf16[2,528,128]{2,1,0:T(8,128)(2,1)S(1)} %get-tuple-element.29), channel_id=1, source_target_pairs={{4,0},{8,4},{12,8},{16,12},{20,16},{24,20},{28,24},{5,1},{9,5},{13... | collective-permute-start | bytes 811016 | tf_op jit(solution)/shard_map/ppermute | solution.py:32
  87.7 23.4 %copy-start.8 = (f32[2,8,1024]{2,1,0:T(8,128)S(1)}, f32[2,8,1024]{2,1,0:T(8,128)}, u32[]{:S(2)}) copy-start(f32[2,8,1024]{2,1,0:T(8,128)} %param.12) | copy-start | bytes 196612
  94.0 8.6 %collective-permute-start.8 = (bf16[512,128]{1,0:T(8,128)(2,1)S(1)}, bf16[512,128]{1,0:T(8,128)(2,1)S(1)}, u32[]{:S(2)}, u32[]{:S(2)}) collective-permute-start(bf16[512,128]{1,0:T(8,128)(2,1)S(1)} %get-tuple-element.20), channel_id=1, source_target_pairs={{0,4},{4,8},{8,12},{12,16},{16,20},{20,24},{24,28},{1,5},{5,9},{9,... | collective-permute-start | bytes 393224 | tf_op jit(solution)/shard_map/ppermute | solution.py:32
  95.9 7.0 %collective-permute-start.9 = (bf16[512,128]{1,0:T(8,128)(2,1)S(1)}, bf16[512,128]{1,0:T(8,128)(2,1)S(1)}, u32[]{:S(2)}, u32[]{:S(2)}) collective-permute-start(bf16[512,128]{1,0:T(8,128)(2,1)S(1)} %get-tuple-element.20), channel_id=1, source_target_pairs={{4,0},{8,4},{12,8},{16,12},{20,16},{24,20},{28,24},{5,1},{9,5},{13... | collective-permute-start | bytes 393224 | tf_op jit(solution)/shard_map/ppermute | solution.py:32
  105.6 3.9 %collective-permute-start.10 = (bf16[2,8,1024]{2,1,0:T(8,128)(2,1)S(1)}, bf16[2,8,1024]{2,1,0:T(8,128)(2,1)S(1)}, u32[]{:S(2)}, u32[]{:S(2)}) collective-permute-start(bf16[2,8,1024]{2,1,0:T(8,128)(2,1)S(1)} %get-tuple-element.22), channel_id=1, source_target_pairs={{0,1},{1,2},{2,3},{4,5},{5,6},{6,7},{8,9},{9,10},{10,11},{12,13},{... | collective-permute-start | bytes 98312 | tf_op jit(solution)/shard_map/ppermute | solution.py:32
  106.9 2.9 %collective-permute-start.11 = (bf16[2,8,1024]{2,1,0:T(8,128)(2,1)S(1)}, bf16[2,8,1024]{2,1,0:T(8,128)(2,1)S(1)}, u32[]{:S(2)}, u32[]{:S(2)}) collective-permute-start(bf16[2,8,1024]{2,1,0:T(8,128)(2,1)S(1)} %get-tuple-element.22), channel_id=1, source_target_pairs={{0,2},{1,3},{4,6},{5,7},{8,10},{9,11},{12,14},{13,15},{16,18},{17,... | collective-permute-start | bytes 98312 | tf_op jit(solution)/shard_map/ppermute | solution.py:32
  108.2 2.9 %collective-permute-start.12 = (bf16[2,8,1024]{2,1,0:T(8,128)(2,1)S(1)}, bf16[2,8,1024]{2,1,0:T(8,128)(2,1)S(1)}, u32[]{:S(2)}, u32[]{:S(2)}) collective-permute-start(bf16[2,8,1024]{2,1,0:T(8,128)(2,1)S(1)} %get-tuple-element.22), channel_id=1, source_target_pairs={{0,3},{4,7},{8,11},{12,15},{16,19},{20,23},{24,27},{28,31}} | collective-permute-start | bytes 98312 | tf_op jit(solution)/shard_map/ppermute | solution.py:32
where the time goes:
time: 114 us; the launch traced here: 112 us
  Pallas kernels  54.4 us (48%)
  starting transfers between devices  32.5 us (29%)
  waiting for transfers between devices  21.2 us (19%)
  local copies, waits for them, and re-layouts  2.65 us (2%)
    ppermute x11, starting transfers between devices, hop(): return lax.ppermute(value, axis, pairs)  26.1 us
    pallas_call x4, Pallas kernels, encode(): pl.pallas_call(functools.partial(kernel, half), out_shape=outs, in_specs=...  19.1 us
    pallas_call x1, Pallas kernels, shards(): pl.pallas_call(functools.partial(own_scores_kernel, half), out_shape=(sha...  18.9 us
    ppermute x2, waiting for transfers between devices, hop_plane(): return lax.ppermute(value, ('tile', 'sec'), pairs)  17.1 us
    pallas_call x1, Pallas kernels, shards(): pl.pallas_call(functools.partial(back_scores_kernel, half), out_shape=sha...  7.45 us
    ppermute x2, starting transfers between devices, hop_plane(): return lax.ppermute(value, ('tile', 'sec'), pairs)  6.46 us
    pallas_call x1, Pallas kernels, shards(): pl.pallas_call(functools.partial(front_scores_kernel, half), out_shape=(s...  6.3 us
    ppermute x11, waiting for transfers between devices, hop(): return lax.ppermute(value, axis, pairs)  4.08 us
  transfers between devices with their start and end apart: 13, of which 5 were waited for; matrix products, arithmetic and copies ran while one was open for 0% of the time, Pallas kernels for 28%

commit v1 on v0

v1 whole, which is shorter than its diff:
```python
import functools

import jax
import jax.numpy as jnp
from jax import lax
from jax.experimental import pallas as pl
from jax.experimental.pallas import tpu as pltpu
from jax.sharding import PartitionSpec as P


ITERS = 8
REACH = 2
LANES = 128
BASE = 16
PAD = LANES
SEG = 16
EDGE = 16

epsilon = 1e-05
step_size = 0.2
stiffness = 0.5

F32 = jnp.float32
BF16 = jnp.bfloat16
HBM = pl.BlockSpec(memory_space=pltpu.HBM)
VMEM = pl.BlockSpec(memory_space=pltpu.VMEM)


def hop(value, axis, steps):
    count = lax.axis_size(axis)
    pairs = [(i, i + steps) for i in range(count) if 0 <= i + steps < count]
    return lax.ppermute(value, axis, pairs)


def hop_plane(value, steps):
    tiles = lax.axis_size("tile")
    secs = lax.axis_size("sec")
    pairs = [(i * secs, (i + steps) * secs) for i in range(tiles) if 0 <= i + steps < tiles]
    return lax.ppermute(value, ("tile", "sec"), pairs)


def params(limit):
    return pltpu.CompilerParams(vmem_limit_bytes=limit * 1024 * 1024)


def matmuls(pix, wh, wf):
    hidden = jnp.maximum(jnp.dot(pix, wh, preferred_element_type=F32), 0.0).astype(BF16)
    return jnp.dot(hidden, wf, preferred_element_type=F32)


def normed(pre, gain):
    mean = jnp.mean(pre * pre, axis=-1, keepdims=True)
    return (pre * lax.rsqrt(mean + epsilon) * gain).astype(BF16)


def encode_steps(pix_of, count, width, store, wh_ref, wf_ref, gain_ref, pre_s):
    steps = count // 2

    def finish(n):
        value = normed(pre_s[n % 2], gain_ref[...])
        store(2 * n, value[:width])
        store(2 * n + 1, value[width:])

    for n in range(steps):
        pre_s[n % 2] = matmuls(pix_of(2 * n), wh_ref[...], wf_ref[...])
        if n:
            finish(n - 1)
    finish(steps - 1)


def border_rows(rows):
    return list(range(REACH)) + list(range(rows - REACH, rows))


def inner_rows(rows):
    return list(range(REACH, rows - REACH))


def pieces_of(kind, rows, far):
    border, inner = border_rows(rows), inner_rows(rows)
    if kind == "front":
        return [(1, r, 0) for r in range(rows)]
    if kind == "border":
        return [(0, r, far) for r in border] + [(0, r, 0) for r in border] + [(1, r, far) for r in border]
    if kind == "back":
        return [(0, r, far) for r in inner]
    return [(0, r, 0) for r in inner] + [(1, r, far) for r in inner]


def fetch(pieces, pix_ref, dst_ref, sem):
    width = dst_ref.shape[1]
    copies = []
    for n, (sec, row, col0) in enumerate(pieces):
        copy = pltpu.make_async_copy(
            pix_ref.at[sec, row, col0 : col0 + width, :], dst_ref.at[n], sem.at[n]
        )
        copy.start()
        copies.append(copy)
    return copies


def pair_of(ref, n):
    width, patch = ref.shape[1:]
    return ref[n : n + 2].reshape(2 * width, patch)


def zero_sides(ref, cols):
    side = jnp.zeros((ref.shape[0], EDGE, ref.shape[2]), BF16)
    ref[:, PAD - EDGE : PAD, :] = side
    ref[:, PAD + cols : PAD + cols + EDGE, :] = side


def put_left(ref, row, value, half):
    ref[row + REACH, PAD : PAD + half, :] = value[:half]


def put_right(ref, row, value, half):
    ref[row + REACH, PAD + half : PAD + 2 * half, :] = value[value.shape[0] - half :]


def encode_front_kernel(
    half, pix_ref, wh_in, wf_in, gain_in, pred_ref,
    front_ref, odd_ref, next_ref, wh_ref, wf_ref, gain_ref, top_ref, bottom_ref,
    pix_s, pre_s, sem, next_sem, more_sem,
):
    rows, cols = pix_ref.shape[1:3]
    width = front_ref.shape[1]
    far = cols - width
    constants = [(wh_in, wh_ref), (wf_in, wf_ref), (gain_in, gain_ref)]
    start_all(constants, more_sem)
    copies = fetch(pieces_of("front", rows, far), pix_ref, pix_s, sem)
    edges = [(pred_ref.at[0:REACH], top_ref), (pred_ref.at[rows - REACH : rows], bottom_ref)]
    start_all(edges, more_sem.at[len(constants) :])
    following = fetch(pieces_of("border", rows, far), pix_ref, next_ref, next_sem)
    zero_sides(odd_ref, cols)
    wait_all(constants, more_sem)

    def pix_of(n):
        copies[n].wait()
        copies[n + 1].wait()
        return pair_of(pix_s, n)

    def store(n, value):
        front_ref[n] = value
        put_left(odd_ref, n, value, half)

    encode_steps(pix_of, len(copies), width, store, wh_ref, wf_ref, gain_ref, pre_s)
    wait_all(edges, more_sem.at[len(constants) :])
    for copy in following:
        copy.wait()


def encode_border_kernel(
    half, pix_ref, wh_ref, wf_ref, gain_ref, own_ref, odd_in, off_ref, mask_ref,
    odd_ref, even_ref, back_ref, up_ref, down_ref, next_ref, pre_s, next_sem,
):
    rows, cols = pix_ref.shape[1:3]
    width = own_ref.shape[1]
    border = border_rows(rows)
    following = fetch(pieces_of("back", rows, cols - width), pix_ref, next_ref, next_sem)
    zero_sides(even_ref, cols)
    first = half // LANES - 1
    for tile in range(cols // LANES - first):
        lanes = slice((first + tile) * LANES, (first + tile + 1) * LANES)
        extra = jnp.concatenate(
            [off_ref[0, 0, :, lanes], off_ref[0, 1, :, lanes], mask_ref[0, :, lanes], mask_ref[0, :, lanes]], 0
        )
        at = rows * width + tile * 4 * rows
        back_ref[at : at + 4 * rows, :] = extra.astype(F32).astype(BF16)

    def store(n, value):
        part, m = divmod(n, len(border))
        row = border[m]
        pack = down_ref if m < REACH else up_ref
        if part == 0:
            back_ref[row * width : (row + 1) * width, :] = value
            put_right(even_ref, row, value, half)
            pack[m % REACH, half:cols, :] = value[width - half :]
        elif part == 1:
            put_left(even_ref, row, value, half)
            pack[m % REACH, 0:half, :] = value[:half]
        else:
            put_right(odd_ref, row, value, half)
            pack[m % REACH, cols : cols + width, :] = value

    encode_steps(lambda n: pair_of(own_ref, n), own_ref.shape[0], width, store, wh_ref, wf_ref, gain_ref, pre_s)
    for copy in following:
        copy.wait()


def encode_back_kernel(
    half, pix_ref, wh_ref, wf_ref, gain_ref, own_ref, even_in, back_in,
    even_ref, back_ref, next_ref, pre_s, next_sem,
):
    rows, cols = pix_ref.shape[1:3]
    width = own_ref.shape[1]
    inner = inner_rows(rows)
    following = fetch(pieces_of("inner", rows, cols - width), pix_ref, next_ref, next_sem)

    def store(n, value):
        back_ref[inner[n] * width : (inner[n] + 1) * width, :] = value
        put_right(even_ref, inner[n], value, half)

    encode_steps(lambda n: pair_of(own_ref, n), own_ref.shape[0], width, store, wh_ref, wf_ref, gain_ref, pre_s)
    for copy in following:
        copy.wait()


def encode_inner_kernel(
    half, wh_ref, wf_ref, gain_ref, own_ref, odd_in, even_in, odd_ref, even_ref, pre_s
):
    width = own_ref.shape[1]
    rows = odd_ref.shape[0] - 2 * REACH
    inner = inner_rows(rows)

    def store(n, value):
        part, m = divmod(n, len(inner))
        if part == 0:
            put_left(even_ref, inner[m], value, half)
        else:
            put_right(odd_ref, inner[m], value, half)

    encode_steps(lambda n: pair_of(own_ref, n), own_ref.shape[0], width, store, wh_ref, wf_ref, gain_ref, pre_s)


def flops_of(nodes, patch, hid, feat):
    return pl.CostEstimate(
        flops=2 * nodes * hid * (patch + feat), bytes_accessed=nodes * 2 * (patch + feat), transcendentals=nodes
    )


def align(band, first, lift, row):
    band = pltpu.roll(band, (2 * LANES - first - BASE + 2 + lift) % LANES, 1)
    for shift in (1, 2, 4):
        band = jnp.where((row & shift) != 0, pltpu.roll(band, LANES - shift, 1), band)
    return band


def score_columns(query_of, window_of, rows, m_s, s_s, k, low):
    span = 2 * REACH + 1
    tall = LANES - low
    lane = lax.broadcasted_iota(jnp.int32, (8, LANES), 1)
    for rp in range(rows[0], rows[1] + 2 * REACH):
        j = rp % span
        window = window_of(rp, k, SEG * j)
        first = max(rp - 2 * REACH, rows[0])
        last = min(rp, rows[1] - 1)
        parts = [query_of(r, k, low) for r in range(first, last + 1)]
        query = jnp.concatenate(parts, 0) if len(parts) > 1 else parts[0]
        product = lax.dot_general(
            query, window, (((1,), (1,)), ((), ())), preferred_element_type=F32
        )
        for r in range(first, last + 1):
            for i in range(low // 8, LANES // 8):
                at = (r - first) * tall + 8 * i - low
                s = 8 * i + BASE - 4 + SEG * j
                near = product[at : at + 8, :LANES]
                far = product[at : at + 8, LANES:]
                if s + SEG <= LANES:
                    value, mask = near, (lane >= s) & (lane < s + SEG)
                elif s >= LANES:
                    value, mask = far, (lane >= s - LANES) & (lane < s + SEG - LANES)
                else:
                    value = jnp.where(lane >= s, near, far)
                    mask = (lane >= s) | (lane < s + SEG - LANES)
                dst = m_s.at[r, 8 * i : 8 * i + 8, :]
                if rp == r:
                    dst[...] = value
                else:
                    pltpu.store(dst, value, mask=mask)
        if rp > rows[0] + 2 * REACH and rp % 2:
            score_turn(m_s, s_s, rp - 2 * REACH - 1, k, low)


def score_turn(m_s, s_s, r, k, low):
    span = 2 * REACH + 1
    lane = lax.broadcasted_iota(jnp.int32, (8, LANES), 1)
    row = lax.broadcasted_iota(jnp.int32, (8, LANES), 0)
    groups = [jnp.zeros((8, LANES), F32)] * (low // 8)
    for i in range(low // 8, LANES // 8):
        one = align(m_s[r, 8 * i : 8 * i + 8, :], 8 * i, 0, row)
        two = align(m_s[r + 1, 8 * i : 8 * i + 8, :], 8 * i, 8, row)
        groups.append(jnp.where((lane & 8) != 0, two, one))
    turned = jnp.concatenate(groups, 0).T
    lanes = pl.ds(pl.multiple_of(k * LANES, LANES), LANES)
    for n in range(2):
        for j in range(span):
            a = (j - r - n) % span
            at = SEG * j + 8 * n
            s_s[r + n, SEG * a : SEG * a + 8, lanes] = turned[at : at + 8]


def score_job(query_of, window_of, m_s, s_s, tiles, low=0, blocks=None):
    blocks = blocks or ((0, s_s.shape[0]),)
    first = 1 if low else 0

    def columns(m, k, low):
        for rows in blocks:
            score_columns(query_of, window_of, rows, m_s.at[m], s_s, k, low)

    if low:
        columns(0, 0, low)
    pairs, odd = (tiles - first) // 2, (tiles - first) % 2

    def body(n, carry):
        for m in range(2):
            columns(m, 2 * n + m + first, 0)
        return carry

    lax.fori_loop(0, pairs, body, 0)
    if odd:
        columns(0, tiles - 1, 0)


def padded_query(ref, tile0=0):
    def query_of(r, k, low):
        at = pl.multiple_of((k + tile0) * LANES + PAD + low, 16)
        return ref[r + REACH, pl.ds(at, LANES - low), :]

    return query_of


def padded_window(ref, halo=None, tile0=0):
    rows = ref.shape[0] - 2 * REACH

    def window_of(rp, k, shift):
        at = pl.multiple_of((k + tile0) * LANES + (PAD - BASE) - shift, 16)
        if halo is not None and rp < REACH:
            return halo[rp, pl.ds(at, 2 * LANES), :]
        if halo is not None and rp >= rows + REACH:
            return halo[rp - rows, pl.ds(at, 2 * LANES), :]
        return ref[rp, pl.ds(at, 2 * LANES), :]

    return window_of


def flow_tile(s_s, oy, ox, lanes):
    y_low, y_high, x_low, x_high = oy < 0, oy > 0, ox < 0, ox > 0
    feat = F32(1.0 / LANES)
    by_row = {}
    for i in range(3):
        for b in range(5):
            v = [s_s[:, SEG * (i + d) + b, lanes] for d in range(3)]
            by_row[i, b] = jnp.where(y_low, v[0], jnp.where(y_high, v[2], v[1]))
    total = jnp.ones_like(oy)
    sum_y = jnp.zeros_like(oy)
    sum_x = jnp.zeros_like(oy)
    for i in range(3):
        for j in range(3):
            near = jnp.where(
                x_low, by_row[i, j], jnp.where(x_high, by_row[i, j + 2], by_row[i, j + 1])
            )
            near = near * feat
            weight = near * near
            total = total + weight
            if i != 1:
                sum_y = sum_y + weight * (i - 1)
            if j != 1:
                sum_x = sum_x + weight * (j - 1)
    return oy + sum_y / total, ox + sum_x / total


def flows_of(s_s, off_ref, flow_ref, tiles):
    def body(k, carry):
        lanes = pl.ds(pl.multiple_of(k * LANES, LANES), LANES)
        fy, fx = flow_tile(s_s, off_ref[0, :, lanes].astype(F32), off_ref[1, :, lanes].astype(F32), lanes)
        flow_ref[0, :, lanes] = fy
        flow_ref[1, :, lanes] = fx
        return carry

    lax.fori_loop(0, tiles, body, 0)


def copies_of(pairs, sem):
    return [pltpu.make_async_copy(src, dst, sem.at[n]) for n, (src, dst) in enumerate(pairs)]


def start_all(pairs, sem):
    for copy in copies_of(pairs, sem):
        copy.start()


def wait_all(pairs, sem):
    for copy in copies_of(pairs, sem):
        copy.wait()


def near_scores_kernel(
    half, even_ref, odd_ref, pred_ref, pup_ref, pdown_ref, off_ref,
    s_s, flow0_ref, ref0_s, s0_s, m_s, sem,
):
    rows = odd_ref.shape[0] - 2 * REACH
    cols = 2 * half
    far = half - 2 * EDGE
    is_first = lax.axis_index("sec") == 0
    tile0 = half // LANES - 1
    tiles = cols // LANES - tile0
    to = slice(PAD + far, PAD + cols)
    before = [
        (pred_ref.at[:, far:cols, :], ref0_s.at[REACH : rows + REACH, to, :]),
        (pup_ref.at[:, far:cols, :], ref0_s.at[0:REACH, to, :]),
        (pdown_ref.at[:, far:cols, :], ref0_s.at[rows + REACH : rows + 2 * REACH, to, :]),
    ]

    @pl.when(is_first)
    def _():
        start_all(before, sem)

    flow0_ref[...] = jnp.zeros_like(flow0_ref)
    score_job(
        padded_query(odd_ref), padded_window(even_ref), m_s, s_s, cols // LANES, 0, ((REACH, rows - REACH),)
    )

    @pl.when(is_first)
    def _():
        zero_sides(ref0_s, cols)
        wait_all(before, sem)
        score_job(
            padded_query(even_ref, tile0), padded_window(ref0_s, None, tile0), m_s, s0_s, tiles, LANES - EDGE
        )
        flows_of(s0_s, off_ref.at[0, :, :, tile0 * LANES : cols], flow0_ref, tiles)


def own_scores_kernel(
    half, even_ref, odd_ref, up_ref, down_ref, off_ref, s_in, s_s, flow_ref, halo_s, m_s, sem
):
    rows = odd_ref.shape[0] - 2 * REACH
    cols = 2 * half
    halos = [
        (up_ref.at[:, 0:cols, :], halo_s.at[0:REACH, PAD : PAD + cols, :]),
        (down_ref.at[:, 0:cols, :], halo_s.at[REACH : 2 * REACH, PAD : PAD + cols, :]),
    ]
    start_all(halos, sem)
    zero_sides(halo_s, cols)
    wait_all(halos, sem)
    score_job(
        padded_query(odd_ref), padded_window(even_ref, halo_s), m_s, s_s, cols // LANES, 0,
        ((0, REACH), (rows - REACH, rows)),
    )
    flows_of(s_s, off_ref.at[1], flow_ref, cols // LANES)


def pairs_out(pack_ref, at, tops, bottoms):
    for n, (top, bottom) in enumerate(zip(tops, bottoms)):
        pack_ref[at + 16 * n : at + 16 * n + 16, :] = jnp.concatenate([top, bottom], 0).astype(BF16)
    return at + 16 * len(tops)


def cross_scores_kernel(
    half, back_ref, odd_ref, up_ref, down_ref, front_ref, fup_ref, fdown_ref,
    pred_ref, pup_ref, pdown_ref, even_ref, off_ref, mask_ref, flow1_ref, flow0_ref,
    flow2_ref, flow_ref, pack_ref, halo_s, ref_s, s_s, m_s, sem, sem0,
):
    rows = odd_ref.shape[0] - 2 * REACH
    cols = 2 * half
    width = front_ref.shape[1]
    far = cols - width
    is_first = lax.axis_index("sec") == 0
    tile0 = half // LANES - 1
    tiles = cols // LANES - tile0
    pack = slice(cols, cols + width)
    to = slice(PAD + far, PAD + cols)
    span = slice(PAD, PAD + width)
    above, below = slice(0, REACH), slice(rows + REACH, rows + 2 * REACH)
    halos = [
        (up_ref.at[:, pack, :], halo_s.at[0:REACH, to, :]),
        (down_ref.at[:, pack, :], halo_s.at[REACH : 2 * REACH, to, :]),
    ]
    before = [
        (pred_ref.at[:, 0:width, :], ref_s.at[REACH : rows + REACH, span, :]),
        (pup_ref.at[:, 0:width, :], ref_s.at[above, span, :]),
        (pdown_ref.at[:, 0:width, :], ref_s.at[below, span, :]),
    ]
    passed = [
        (front_ref, ref_s.at[REACH : rows + REACH, span, :]),
        (fup_ref, ref_s.at[above, span, :]),
        (fdown_ref, ref_s.at[below, span, :]),
    ]
    start_all(halos, sem)

    @pl.when(is_first)
    def _():
        start_all(before, sem0)

    @pl.when(jnp.logical_not(is_first))
    def _():
        start_all(passed, sem0)

    zero_sides(halo_s, cols)
    wait_all(halos, sem)

    def query_of(r, k, low):
        at = (k + tile0) * LANES + low - far
        size = LANES - low
        return back_ref[pl.ds(pl.multiple_of(at + r * width, 16), size), :]

    score_job(query_of, padded_window(odd_ref, halo_s, tile0), m_s, s_s, tiles, LANES - EDGE)

    def body(k, carry):
        lanes = pl.ds(pl.multiple_of(k * LANES, LANES), LANES)
        extra = back_ref[pl.ds(pl.multiple_of(k * 4 * rows + rows * width, 4 * rows), 4 * rows), :].astype(F32)
        fy, fx = flow_tile(s_s, extra[:rows], extra[rows : 2 * rows], lanes)
        flow2_ref[0, :, lanes] = fy
        flow2_ref[1, :, lanes] = fx
        flow2_ref[2, :, lanes] = extra[2 * rows : 3 * rows]
        return carry

    lax.fori_loop(0, tiles, body, 0)

    @pl.when(is_first)
    def _():
        wait_all(before, sem0)

    @pl.when(jnp.logical_not(is_first))
    def _():
        wait_all(passed, sem0)

    ref_s[:, PAD - EDGE : PAD, :] = jnp.zeros((rows + 2 * REACH, EDGE, LANES), BF16)
    tiles = half // LANES
    score_job(padded_query(even_ref), padded_window(ref_s), m_s, s_s, tiles)
    flow_ref[:, :, half:cols] = flow0_ref[:, :, LANES:]
    flows_of(s_s, off_ref.at[0], flow_ref, tiles)

    def tiles_of(ref, count):
        return [ref[:, n * LANES : (n + 1) * LANES] for n in range(count)]

    n = 0
    for ref, count in ((flow1_ref, cols // LANES), (flow_ref, cols // LANES), (flow2_ref, flow2_ref.shape[2] // LANES)):
        n = pairs_out(pack_ref, n, tiles_of(ref.at[0], count), tiles_of(ref.at[1], count))
    masks = []
    for ref, count in ((mask_ref.at[1], cols // LANES), (mask_ref.at[0], cols // LANES), (flow2_ref.at[2], flow2_ref.shape[2] // LANES)):
        masks += [m.astype(F32) for m in tiles_of(ref, count)]
    if len(masks) % 2:
        masks.append(masks[-1])
    pairs_out(pack_ref, n, masks[0::2], masks[1::2])


def relax_kernel(
    half, up_ref, down_ref, flow1_ref, flow3_ref, flow2_ref, mask_ref, f1_ref, f3_ref, msg_ref,
    field_s, pull_s, keep_s,
):
    rows, cols = flow1_ref.shape[1:]
    deep = rows + 2 * ITERS
    place = lax.axis_index("tile")
    count = lax.axis_size("tile")
    glob = place * rows + lax.broadcasted_iota(jnp.int32, (deep, LANES), 0) - ITERS
    inside = ((glob >= 0) & (glob < rows * count)).astype(F32)
    widths = (cols, cols, flow2_ref.shape[2])
    tiles = [w // LANES for w in widths]
    flows = (flow1_ref, flow3_ref, flow2_ref)
    own_masks = (mask_ref.at[1], mask_ref.at[0], flow2_ref.at[2])
    starts = [0, tiles[0], tiles[0] + tiles[1]]
    mask_at = 16 * sum(tiles)
    for job in range(3):
        for k in range(tiles[job]):
            lanes = slice(k * LANES, (k + 1) * LANES)
            at = 16 * (starts[job] + k)
            m_at = mask_at + 8 * (starts[job] + k)
            half_at = m_at // 16 * 16
            sub = slice(m_at - half_at, m_at - half_at + 8)
            upper = up_ref[at : at + 16, :].astype(F32)
            lower = down_ref[at : at + 16, :].astype(F32)
            m_up = up_ref[half_at : half_at + 16, :].astype(F32)[sub]
            m_down = down_ref[half_at : half_at + 16, :].astype(F32)[sub]
            weight = stiffness * jnp.concatenate(
                [m_up, own_masks[job][:, lanes].astype(F32), m_down], 0
            )
            keep_s[job, :, lanes] = (step_size - step_size * weight) * inside
            for c in range(2):
                flow = jnp.concatenate(
                    [upper[8 * c : 8 * c + 8], flows[job][c, :, lanes], lower[8 * c : 8 * c + 8]], 0
                )
                pull = step_size * weight * flow * inside
                pull_s[job, c, :, lanes] = pull
                field_s[job, c, :, lanes] = pull
    step = step_size * inside

    def body(n, carry):
        for job in range(3):
            for c in range(2):
                old = [field_s[job, c, :, k * LANES : (k + 1) * LANES] for k in range(tiles[job])]
                lane = lax.broadcasted_iota(jnp.int32, (deep, LANES), 1)
                nxt = [pltpu.roll(x, LANES - 1, 1) for x in old]
                prv = [pltpu.roll(x, 1, 1) for x in old]
                zero = jnp.zeros_like(old[0])
                for k in range(tiles[job]):
                    lanes = slice(k * LANES, (k + 1) * LANES)
                    right = jnp.where(lane == LANES - 1, nxt[k + 1] if k + 1 < tiles[job] else zero, nxt[k])
                    left = jnp.where(lane == 0, prv[k - 1] if k else zero, prv[k])
                    around = pltpu.roll(old[k], 1, 0) + pltpu.roll(old[k], deep - 1, 0) + left + right
                    field_s[job, c, :, lanes] = (
                        keep_s[job, :, lanes] * old[k] + step * around + pull_s[job, c, :, lanes]
                    )
        return carry

    lax.fori_loop(0, ITERS - 1, body, 0)
    is_first = lax.axis_index("sec") == 0
    seam = half - EDGE // 2
    mine = slice(ITERS, ITERS + rows)
    lead = half - LANES
    for c in range(2):
        for k in range(tiles[0]):
            lanes = slice(k * LANES, (k + 1) * LANES)
            col = lax.broadcasted_iota(jnp.int32, (rows, LANES), 1) + k * LANES
            one = field_s[0, c, mine, lanes]
            front = field_s[1, c, mine, lanes]
            if (k + 1) * LANES > seam:
                front = jnp.where((col < seam) | is_first, front, 0.0)
            total = one + front
            if k * LANES >= lead:
                back = field_s[2, c, mine, k * LANES - lead : (k + 1) * LANES - lead]
                total = total + jnp.where(col >= seam, back, 0.0)
            f1_ref[c, :, lanes] = one
            f3_ref[c, :, lanes] = front
            msg_ref[c, :, lanes] = total.astype(msg_ref.dtype)


def shards(pixels, pred, offsets, mask, base_shift, w_hidden, w_feature, feat_gain):
    secs, rows, cols, patch = pixels.shape
    hid, feat = w_feature.shape
    assert secs == 2 and rows == ITERS and feat == LANES and cols % (2 * LANES) == 0
    half = cols // 2
    width = half + 2 * EDGE
    inner = rows - 2 * REACH
    span = half + LANES
    deep = rows + 2 * REACH
    tail = 4 * rows * (span // LANES)
    full = cols + 2 * PAD
    gain = feat_gain.reshape(1, feat)
    shape = jax.ShapeDtypeStruct
    padded = shape((deep, full, feat), BF16)
    pre = pltpu.VMEM((2, 2 * width, feat), F32)

    dma = pltpu.SemaphoreType.DMA

    def call(kernel, ins, in_specs, outs, scratch, cost, limit, aliases=None):
        return pl.pallas_call(
            functools.partial(kernel, half),
            out_shape=outs,
            in_specs=in_specs,
            out_specs=tuple(VMEM for _ in outs),
            scratch_shapes=scratch,
            input_output_aliases=aliases or {},
            compiler_params=params(limit),
            cost_estimate=cost,
        )(*ins)

    def pixels_for(kind):
        return shape((len(pieces_of(kind, rows, 0)), width, patch), BF16)

    def encode_cost(kind):
        return flops_of(len(pieces_of(kind, rows, 0)) * width, patch, hid, feat)

    pixels, w_hidden, w_feature, gain, pred = (
        pltpu.with_memory_space_constraint(x, pltpu.HBM) for x in (pixels, w_hidden, w_feature, gain, pred)
    )
    edges = shape((REACH, cols, feat), BF16)
    front, odd, pix, wh, wf, gain, top, bottom = call(
        encode_front_kernel,
        (pixels, w_hidden, w_feature, gain, pred), [HBM] * 5,
        (
            shape((rows, width, feat), BF16), padded, pixels_for("border"),
            shape(w_hidden.shape, BF16), shape(w_feature.shape, BF16), shape(gain.shape, F32), edges, edges,
        ),
        [pltpu.VMEM((rows, width, patch), BF16), pre, dma((rows,)), dma((6 * REACH,)), dma((5,))],
        encode_cost("front"), 12,
    )
    weights = (wh, wf, gain)
    front_in = hop(front, "sec", 1)
    pup = hop_plane(bottom, 1)
    pdown = hop_plane(top, -1)
    pack = shape((REACH, cols + width, feat), BF16)
    odd, even, back, up, down, pix = call(
        encode_border_kernel,
        (pixels, *weights, pix, odd, offsets, mask), [HBM] + [VMEM] * 7,
        (padded, padded, shape((rows * width + tail, feat), BF16), pack, pack, pixels_for("back")),
        [pre, dma((inner,))], encode_cost("border"), 12, {5: 0},
    )
    up_in = hop(up, "tile", 1)
    down_in = hop(down, "tile", -1)
    even, back, pix = call(
        encode_back_kernel,
        (pixels, *weights, pix, even, back), [HBM] + [VMEM] * 6,
        (padded, shape(back.shape, BF16), pixels_for("inner")),
        [pre, dma((2 * inner,))], encode_cost("back"), 12, {5: 0, 6: 1},
    )
    back_in = hop(back, "sec", -1)
    odd, even = call(
        encode_inner_kernel, (*weights, pix, odd, even), [VMEM] * 6,
        (padded, padded), [pre], encode_cost("inner"), 12, {4: 0, 5: 1},
    )

    bands = SEG * (2 * REACH + 1)
    nodes = rows * cols

    def score_cost(part):
        return pl.CostEstimate(
            flops=int(part * nodes * 2560 * LANES), bytes_accessed=int(part * nodes * 512), transcendentals=0
        )

    halo = pltpu.VMEM((2 * REACH, full, feat), BF16)
    grids = pltpu.VMEM((rows, bands, cols), F32)
    turning = pltpu.VMEM((2, rows, LANES, LANES), F32)
    whole = pltpu.VMEM((deep, full, feat), BF16)
    flow0_shape = shape((2, rows, span), F32)
    scores, flow0 = call(
        near_scores_kernel, (even, odd, pred, pup, pdown, offsets),
        [VMEM] * 2 + [HBM] + [VMEM] * 3, (shape((rows, bands, cols), F32), flow0_shape),
        [whole, pltpu.VMEM((rows, bands, span), F32), turning, dma((3,))], score_cost(0.5), 16,
    )
    fup_in = hop(front_in[rows - REACH :], "tile", 1)
    fdown_in = hop(front_in[:REACH], "tile", -1)
    _, flow1 = call(
        own_scores_kernel, (even, odd, up_in, down_in, offsets, scores), [VMEM] * 6,
        (shape(scores.shape, F32), shape((2, rows, cols), F32)),
        [halo, turning, dma((2,))], score_cost(0.5), 12, {5: 0},
    )

    tiles = 2 * (cols // LANES) + span // LANES
    pack_rows = 16 * tiles + 16 * ((tiles + 1) // 2)
    flow2, flow3, pack = call(
        cross_scores_kernel,
        (
            back_in, odd, up_in, down_in, front_in, fup_in, fdown_in,
            pred, pup, pdown, even, offsets, mask, flow1, flow0,
        ),
        [VMEM] * 7 + [HBM] + [VMEM] * 7,
        (shape((3, rows, span), F32), shape((2, rows, cols), F32), shape((pack_rows, LANES), BF16)),
        [halo, whole, grids, turning, dma((2,)), dma((3,))], score_cost(1.0), 20,
    )
    pack_up = hop(pack, "tile", 1)
    pack_down = hop(pack, "tile", -1)

    wide = rows + 2 * ITERS
    f1, f3, msg = pl.pallas_call(
        functools.partial(relax_kernel, half),
        out_shape=(shape((2, rows, cols), F32), shape((2, rows, cols), F32), shape((2, rows, cols), BF16)),
        in_specs=[VMEM] * 6,
        out_specs=(VMEM,) * 3,
        scratch_shapes=[
            pltpu.VMEM((3, 2, wide, cols), F32),
            pltpu.VMEM((3, 2, wide, cols), F32),
            pltpu.VMEM((3, wide, cols), F32),
        ],
        compiler_params=params(12),
        cost_estimate=pl.CostEstimate(flops=nodes * 24 * 12 * 8, bytes_accessed=nodes * 40, transcendentals=0),
        name="relax",
    )(pack_up, pack_down, flow1, flow3, flow2, mask)

    prefix = base_shift
    for steps in range(1, lax.axis_size("sec")):
        prefix = prefix + hop(msg, "sec", steps).astype(F32)
    first = prefix + f3
    return jnp.stack([first, first + f1], axis=0)


def solution(mesh):
    in_specs = (
        P("sec", "tile", None, None),
        P("tile", None, None),
        P("sec", None, "tile", None),
        P("sec", "tile", None),
        P(None, "tile", None),
        P(),
        P(),
        P(),
    )
    out_specs = P("sec", None, "tile", None)
    return jax.shard_map(shards, mesh=mesh, in_specs=in_specs, out_specs=out_specs, check_vma=False)
```

time: 114 us -> 93.1 us (0.82)
  waiting for transfers between devices: 21.2 us -> 10.9 us
  Pallas kernels: 54.4 us -> 46.7 us
  local copies, waits for them, and re-layouts: 2.65 us -> 0.05 us
    ppermute x2, waiting for transfers between devices: 17.1 us -> 0.01 us  [hop_plane(): return lax.ppermute(value, ('tile', 'sec'), pairs)]
    pallas_call x7, Pallas kernels: 51.8 us -> 44.1 us  [call(): pl.pallas_call(functools.partial(kernel, half), out_shape=outs, in_specs=...]
    ppermute x11, waiting for transfers between devices: 4.08 us -> 10.9 us  [hop(): return lax.ppermute(value, axis, pairs)]
    unnamed x18 -> x6, local copies, waits for them, and re-layouts: 2.54 us -> 0.01 us
  transfers between devices with their start and end apart: 13 -> 13, of which waited for: 5 -> 4; matrix products, arithmetic and copies ran while one was open for 0% -> 0% of each run, Pallas kernels for 28% -> 30%
where the time goes in v1:
time: 93.1 us; the launch traced here: 91.4 us
  Pallas kernels  46.7 us (50%)
  starting transfers between devices  32.8 us (35%)
  waiting for transfers between devices  10.9 us (12%)
    pallas_call x7, Pallas kernels, call(): pl.pallas_call(functools.partial(kernel, half), out_shape=outs, in_specs=...  44.1 us
    ppermute x11, starting transfers between devices, hop(): return lax.ppermute(value, axis, pairs)  26.3 us
    ppermute x11, waiting for transfers between devices, hop(): return lax.ppermute(value, axis, pairs)  10.9 us
    ppermute x2, starting transfers between devices, hop_plane(): return lax.ppermute(value, ('tile', 'sec'), pairs)  6.46 us
    pallas_call x1, Pallas kernels, shards(): pl.pallas_call(functools.partial(relax_kernel, half), out_shape=(shape((2...  2.6 us
  transfers between devices with their start and end apart: 13, of which 4 were waited for; matrix products, arithmetic and copies ran while one was open for 0% of the time, Pallas kernels for 30%

profile of v1, /device:TPU:4, one launch (start us, length us, event | category | flops | bytes accessed | tf_op | source)
XLA Modules:
  0.0 91.4 jit_solution(15926908840164626947)
XLA Ops:
  0.0 5.8 %shard_map.82 = (bf16[8,544,128]{2,1,0:T(8,128)(2,1)S(1)}, bf16[12,1280,128]{2,1,0:T(8,128)(2,1)S(1)}, bf16[12,544,256]{2,1,0:T(8,128)(2,1)S(1)}, bf16[256,512]{...) custom-call(bf16[2,8,1024,256]{3,2,1,0:T(8,128)(2,1)} %pix_ref.5, ...), custom_call_target="tpu_custom_call" | custom-call | flops 1711276032 | bytes 3342336 | tf_op jit(solution)/shard_map/pallas_call | solution.py:637
  5.8 3.6 %collective-permute-start.3 = (bf16[8,544,128]{2,1,0:T(8,128)(2,1)S(1)}, bf16[8,544,128]{2,1,0:T(8,128)(2,1)S(1)}, u32[]{:S(2)}, u32[]{:S(2)}) collective-permute-start(bf16[8,544,128]{2,1,0:T(8,128)(2,1)S(1)} %get-tuple-element.48), channel_id=1, source_target_pairs={{0,1},{1,2},{2,3},{4,5},{5,6},{6,7},{8,9},{9,10},{10,11},{12,13},{... | collective-permute-start | bytes 3342344 | tf_op jit(solution)/shard_map/ppermute | solution.py:32
  9.4 4.9 %shard_map.83 = (bf16[12,1280,128]{2,1,0:T(8,128)(2,1)S(1)}, bf16[12,1280,128]{2,1,0:T(8,128)(2,1)S(1)}, bf16[4512,128]{1,0:T(8,128)(2,1)S(1)}, bf16[2,1568,128]...) custom-call(bf16[2,8,1024,256]{3,2,1,0:T(8,128)(2,1)} %pix_ref.5, ...), custom_call_target="tpu_custom_call", output_to_operand_aliasing={{0}: (5, {})} | custom-call | flops 2566914048 | bytes 5013504 | tf_op jit(solution)/shard_map/pallas_call | solution.py:637
  14.2 2.3 %shard_map.84 = (bf16[12,1280,128]{2,1,0:T(8,128)(2,1)S(1)}, bf16[4512,128]{1,0:T(8,128)(2,1)S(1)}, bf16[8,544,256]{2,1,0:T(8,128)(2,1)S(1)}) custom-call(bf16[2,8,1024,256]{3,2,1,0:T(8,128)(2,1)} %pix_ref.5, bf16[256,512]{1,0:T(8,128)(2,1)S(1)} %get-tuple-element.33.wh_ref, ...), custom_call_target="tpu_custom_call", output_to_operand_aliasing={{0}: (5, {}), {1}: (6, {})} | custom-call | flops 855638016 | bytes 1671168 | tf_op jit(solution)/shard_map/pallas_call | solution.py:637
  16.5 1.3 %collective-permute-start = (bf16[4512,128]{1,0:T(8,128)(2,1)S(1)}, bf16[4512,128]{1,0:T(8,128)(2,1)S(1)}, u32[]{:S(2)}, u32[]{:S(2)}) collective-permute-start(bf16[4512,128]{1,0:T(8,128)(2,1)S(1)} %get-tuple-element.41), channel_id=1, source_target_pairs={{1,0},{2,1},{3,2},{5,4},{6,5},{7,6},{9,8},{10,9},{11,10},{13,12},{... | collective-permute-start | bytes 3465224 | tf_op jit(solution)/shard_map/ppermute | solution.py:32
  17.8 1.9 %collective-permute-start.6 = (bf16[2,1024,128]{2,1,0:T(8,128)(2,1)S(1)}, bf16[2,1024,128]{2,1,0:T(8,128)(2,1)S(1)}, u32[]{:S(2)}, u32[]{:S(2)}) collective-permute-start(bf16[2,1024,128]{2,1,0:T(8,128)(2,1)S(1)} %get-tuple-element.49), channel_id=1, source_target_pairs={{0,4},{4,8},{8,12},{12,16},{16,20},{20,24},{24,28}} | collective-permute-start | bytes 1572872 | tf_op jit(solution)/shard_map/ppermute | solution.py:39
  19.8 4.5 %collective-permute-start.7 = (bf16[2,1024,128]{2,1,0:T(8,128)(2,1)S(1)}, bf16[2,1024,128]{2,1,0:T(8,128)(2,1)S(1)}, u32[]{:S(2)}, u32[]{:S(2)}) collective-permute-start(bf16[2,1024,128]{2,1,0:T(8,128)(2,1)S(1)} %get-tuple-element.50), channel_id=1, source_target_pairs={{4,0},{8,4},{12,8},{16,12},{20,16},{24,20},{28,24}} | collective-permute-start | bytes 1572872 | tf_op jit(solution)/shard_map/ppermute | solution.py:39
  24.3 1.9 %collective-permute-start.1 = (bf16[2,1568,128]{2,1,0:T(8,128)(2,1)S(1)}, bf16[2,1568,128]{2,1,0:T(8,128)(2,1)S(1)}, u32[]{:S(2)}, u32[]{:S(2)}) collective-permute-start(bf16[2,1568,128]{2,1,0:T(8,128)(2,1)S(1)} %get-tuple-element.46), channel_id=1, source_target_pairs={{0,4},{4,8},{8,12},{12,16},{16,20},{20,24},{24,28},{1,5},{5,9},{9,... | collective-permute-start | bytes 2408456 | tf_op jit(solution)/shard_map/ppermute | solution.py:32
  26.3 6.8 %collective-permute-done.3.front_ref = bf16[8,544,128]{2,1,0:T(8,128)(2,1)S(1)} collective-permute-done((bf16[8,544,128]{2,1,0:T(8,128)(2,1)S(1)}, bf16[8,544,128]{2,1,0:T(8,128)(2,1)S(1)}, u32[]{:S(2)}, u32[]{:S(2)}) %collective-permute-start.3) | collective-permute-done | bytes 1114144 | tf_op jit(solution)/shard_map/ppermute | solution.py:32
  33.1 1.9 %collective-permute-start.2 = (bf16[2,1568,128]{2,1,0:T(8,128)(2,1)S(1)}, bf16[2,1568,128]{2,1,0:T(8,128)(2,1)S(1)}, u32[]{:S(2)}, u32[]{:S(2)}) collective-permute-start(bf16[2,1568,128]{2,1,0:T(8,128)(2,1)S(1)} %get-tuple-element.47), channel_id=1, source_target_pairs={{4,0},{8,4},{12,8},{16,12},{20,16},{24,20},{28,24},{5,1},{9,5},{13... | collective-permute-start | bytes 2408456 | tf_op jit(solution)/shard_map/ppermute | solution.py:32
  35.0 0.0 collective-permute-done.6.pup_ref
  35.1 2.4 %collective-permute-start.4 = (bf16[2,544,128]{2,1,0:T(8,128)(2,1)S(1)}, bf16[2,544,128]{2,1,0:T(8,128)(2,1)S(1)}, u32[]{:S(2)}, u32[]{:S(2)}) collective-permute-start(bf16[2,544,128]{2,1,0:T(8,128)(2,1)S(1)} %get-tuple-element.64), channel_id=1, source_target_pairs={{0,4},{4,8},{8,12},{12,16},{16,20},{20,24},{24,28},{1,5},{5,9},{9,... | collective-permute-start | bytes 835592 | tf_op jit(solution)/shard_map/ppermute | solution.py:32
  37.5 0.0 collective-permute-done.7.pdown_ref
  37.5 4.2 %collective-permute-start.5 = (bf16[2,544,128]{2,1,0:T(8,128)(2,1)S(1)}, bf16[2,544,128]{2,1,0:T(8,128)(2,1)S(1)}, u32[]{:S(2)}, u32[]{:S(2)}) collective-permute-start(bf16[2,544,128]{2,1,0:T(8,128)(2,1)S(1)} %get-tuple-element.63), channel_id=1, source_target_pairs={{4,0},{8,4},{12,8},{16,12},{20,16},{24,20},{28,24},{5,1},{9,5},{13... | collective-permute-start | bytes 835592 | tf_op jit(solution)/shard_map/ppermute | solution.py:32
  41.7 2.7 %shard_map.85 = (bf16[12,1280,128]{2,1,0:T(8,128)(2,1)S(1)}, bf16[12,1280,128]{2,1,0:T(8,128)(2,1)S(1)}) custom-call(bf16[256,512]{1,0:T(8,128)(2,1)S(1)} %get-tuple-element.33.wh_ref, bf16[512,128]{1,0:T(8,128)(2,1)S(1)} %get-tuple-element.34.wf_ref, f32[1,128]{1,0:T(1,128)S(1)} %get-tuple-element.35.gain_ref, ...), custom_call_target="tpu_custom_call", output_to_operand_aliasing={{0}: (4, {}), {1}: (5, {})} | custom-call | flops 1711276032 | bytes 3342336 | tf_op jit(solution)/shard_map/pallas_call | solution.py:637
  44.4 11.1 %shard_map.86 = (f32[8,80,1024]{2,1,0:T(8,128)S(1)}, f32[2,8,640]{2,1,0:T(8,128)S(1)}) custom-call(bf16[12,1280,128]{2,1,0:T(8,128)(2,1)S(1)} %get-tuple-element.51.even_ref, bf16[12,1280,128]{2,1,0:T(8,128)(2,1)S(1)} %get-tuple-element.45.odd_ref, bf16[8,1024,128]{2,1,0:T(8,128)(2,1)} %pred_ref.5, bf16[2,1024,128]{2,1,0:T(8,128)(2,1)S(1)} %collective-permute-done.6.pup_ref, ...), custom_call_target="tpu_custom_call" | custom-call | flops 1342177280 | bytes 2097152 | tf_op jit(solution)/shard_map/pallas_call | solution.py:637
  55.5 0.0 collective-permute-done.2.down_ref
  55.5 6.3 %shard_map.87 = (f32[8,80,1024]{2,1,0:T(8,128)S(1)}, f32[2,8,1024]{2,1,0:T(8,128)S(1)}) custom-call(bf16[12,1280,128]{2,1,0:T(8,128)(2,1)S(1)} %get-tuple-element.51.even_ref, bf16[12,1280,128]{2,1,0:T(8,128)(2,1)S(1)} %get-tuple-element.45.odd_ref, bf16[2,1568,128]{2,1,0:T(8,128)(2,1)S(1)} %collective-permute-done.1.up_ref, ...), custom_call_target="tpu_custom_call", output_to_operand_aliasing={{0}: (5, {})} | custom-call | flops 1342177280 | bytes 2097152 | tf_op jit(solution)/shard_map/pallas_call | solution.py:637
  61.9 0.0 collective-permute-done.5.fdown_ref
  61.9 0.0 copy-start.2
  61.9 11.1 %shard_map.88 = (f32[3,8,640]{2,1,0:T(8,128)S(1)}, f32[2,8,1024]{2,1,0:T(8,128)S(1)}, bf16[512,128]{1,0:T(8,128)(2,1)S(1)}) custom-call(bf16[4512,128]{1,0:T(8,128)(2,1)S(1)} %collective-permute-done.back_ref, bf16[12,1280,128]{2,1,0:T(8,128)(2,1)S(1)} %get-tuple-element.45.odd_ref, bf16[2,1568,128]{2,1,0:T(8,128)(2,1)S(1)} %collective-permute-done.1.up_ref, ...), custom_call_target="tpu_custom_call" | custom-call | flops 2684354560 | bytes 4194304 | tf_op jit(solution)/shard_map/pallas_call | solution.py:637
  73.0 1.9 %collective-permute-start.8 = (bf16[512,128]{1,0:T(8,128)(2,1)S(1)}, bf16[512,128]{1,0:T(8,128)(2,1)S(1)}, u32[]{:S(2)}, u32[]{:S(2)}) collective-permute-start(bf16[512,128]{1,0:T(8,128)(2,1)S(1)} %get-tuple-element.55), channel_id=1, source_target_pairs={{0,4},{4,8},{8,12},{12,16},{16,20},{20,24},{24,28},{1,5},{5,9},{9,... | collective-permute-start | bytes 393224 | tf_op jit(solution)/shard_map/ppermute | solution.py:32
  74.9 4.5 %collective-permute-start.9 = (bf16[512,128]{1,0:T(8,128)(2,1)S(1)}, bf16[512,128]{1,0:T(8,128)(2,1)S(1)}, u32[]{:S(2)}, u32[]{:S(2)}) collective-permute-start(bf16[512,128]{1,0:T(8,128)(2,1)S(1)} %get-tuple-element.55), channel_id=1, source_target_pairs={{4,0},{8,4},{12,8},{16,12},{20,16},{24,20},{28,24},{5,1},{9,5},{13... | collective-permute-start | bytes 393224 | tf_op jit(solution)/shard_map/ppermute | solution.py:32
  79.5 0.7 collective-permute-done.8.up_ref
  80.2 1.8 %collective-permute-done.9.down_ref = bf16[512,128]{1,0:T(8,128)(2,1)S(1)} collective-permute-done((bf16[512,128]{1,0:T(8,128)(2,1)S(1)}, bf16[512,128]{1,0:T(8,128)(2,1)S(1)}, u32[]{:S(2)}, u32[]{:S(2)}) %collective-permute-start.9) | collective-permute-done | bytes 131104 | tf_op jit(solution)/shard_map/ppermute | solution.py:32
  82.0 2.6 %relax.1 = (f32[2,8,1024]{2,1,0:T(8,128)S(1)}, f32[2,8,1024]{2,1,0:T(8,128)S(1)}, bf16[2,8,1024]{2,1,0:T(8,128)(2,1)S(1)}) custom-call(bf16[512,128]{1,0:T(8,128)(2,1)S(1)} %collective-permute-done.8.up_ref, bf16[512,128]{1,0:T(8,128)(2,1)S(1)} %collective-permute-done.9.down_ref, f32[2,8,1024]{2,1,0:T(8,128)S(1)} %get-tuple-element.53.flow1_ref, ...), custom_call_target="tpu_custom_call" | custom-call | flops 18874368 | bytes 327680 | tf_op jit(solution)/shard_map/relax/pallas_call | solution.py:735
  84.6 1.3 %collective-permute-start.12 = (bf16[2,8,1024]{2,1,0:T(8,128)(2,1)S(1)}, bf16[2,8,1024]{2,1,0:T(8,128)(2,1)S(1)}, u32[]{:S(2)}, u32[]{:S(2)}) collective-permute-start(bf16[2,8,1024]{2,1,0:T(8,128)(2,1)S(1)} %get-tuple-element.58), channel_id=1, source_target_pairs={{0,3},{4,7},{8,11},{12,15},{16,19},{20,23},{24,27},{28,31}} | collective-permute-start | bytes 98312 | tf_op jit(solution)/shard_map/ppermute | solution.py:32
  85.9 1.3 %collective-permute-start.11 = (bf16[2,8,1024]{2,1,0:T(8,128)(2,1)S(1)}, bf16[2,8,1024]{2,1,0:T(8,128)(2,1)S(1)}, u32[]{:S(2)}, u32[]{:S(2)}) collective-permute-start(bf16[2,8,1024]{2,1,0:T(8,128)(2,1)S(1)} %get-tuple-element.58), channel_id=1, source_target_pairs={{0,2},{1,3},{4,6},{5,7},{8,10},{9,11},{12,14},{13,15},{16,18},{17,... | collective-permute-start | bytes 98312 | tf_op jit(solution)/shard_map/ppermute | solution.py:32
  87.2 2.0 %collective-permute-start.10 = (bf16[2,8,1024]{2,1,0:T(8,128)(2,1)S(1)}, bf16[2,8,1024]{2,1,0:T(8,128)(2,1)S(1)}, u32[]{:S(2)}, u32[]{:S(2)}) collective-permute-start(bf16[2,8,1024]{2,1,0:T(8,128)(2,1)S(1)} %get-tuple-element.58), channel_id=1, source_target_pairs={{0,1},{1,2},{2,3},{4,5},{5,6},{6,7},{8,9},{9,10},{10,11},{12,13},{... | collective-permute-start | bytes 98312 | tf_op jit(solution)/shard_map/ppermute | solution.py:32
  89.2 0.0 collective-permute-done.12
  89.2 1.6 %collective-permute-done.10 = bf16[2,8,1024]{2,1,0:T(8,128)(2,1)S(1)} collective-permute-done((bf16[2,8,1024]{2,1,0:T(8,128)(2,1)S(1)}, bf16[2,8,1024]{2,1,0:T(8,128)(2,1)S(1)}, u32[]{:S(2)}, u32[]{:S(2)}) %collective-permute-start.10) | collective-permute-done | bytes 32800 | tf_op jit(solution)/shard_map/ppermute | solution.py:32
  90.8 0.7 pad_maximum_fusion
  (11 shorter events, 0.1 us)
Async XLA Ops:
  0.0 9.3 %copy-start = (s32[2,2,8,1024]{3,2,1,0:T(8,128)S(1)}, s32[2,2,8,1024]{3,2,1,0:T(8,128)}, u32[]{:S(2)}) copy-start(s32[2,2,8,1024]{3,2,1,0:T(8,128)} %off_ref.7) | copy-start | bytes 393220
  0.0 9.4 %copy-start.1 = (s32[2,8,1024]{2,1,0:T(8,128)S(1)}, s32[2,8,1024]{2,1,0:T(8,128)}, u32[]{:S(2)}) copy-start(s32[2,8,1024]{2,1,0:T(8,128)} %mask_ref.5) | copy-start | bytes 196612
  5.8 27.3 %collective-permute-start.3 = (bf16[8,544,128]{2,1,0:T(8,128)(2,1)S(1)}, bf16[8,544,128]{2,1,0:T(8,128)(2,1)S(1)}, u32[]{:S(2)}, u32[]{:S(2)}) collective-permute-start(bf16[8,544,128]{2,1,0:T(8,128)(2,1)S(1)} %get-tuple-element.48), channel_id=1, source_target_pairs={{0,1},{1,2},{2,3},{4,5},{5,6},{6,7},{8,9},{9,10},{10,11},{12,13},{... | collective-permute-start | bytes 3342344 | tf_op jit(solution)/shard_map/ppermute | solution.py:32
  16.5 45.3 %collective-permute-start = (bf16[4512,128]{1,0:T(8,128)(2,1)S(1)}, bf16[4512,128]{1,0:T(8,128)(2,1)S(1)}, u32[]{:S(2)}, u32[]{:S(2)}) collective-permute-start(bf16[4512,128]{1,0:T(8,128)(2,1)S(1)} %get-tuple-element.41), channel_id=1, source_target_pairs={{1,0},{2,1},{3,2},{5,4},{6,5},{7,6},{9,8},{10,9},{11,10},{13,12},{... | collective-permute-start | bytes 3465224 | tf_op jit(solution)/shard_map/ppermute | solution.py:32
  17.8 17.2 %collective-permute-start.6 = (bf16[2,1024,128]{2,1,0:T(8,128)(2,1)S(1)}, bf16[2,1024,128]{2,1,0:T(8,128)(2,1)S(1)}, u32[]{:S(2)}, u32[]{:S(2)}) collective-permute-start(bf16[2,1024,128]{2,1,0:T(8,128)(2,1)S(1)} %get-tuple-element.49), channel_id=1, source_target_pairs={{0,4},{4,8},{8,12},{12,16},{16,20},{20,24},{24,28}} | collective-permute-start | bytes 1572872 | tf_op jit(solution)/shard_map/ppermute | solution.py:39
  19.8 17.7 %collective-permute-start.7 = (bf16[2,1024,128]{2,1,0:T(8,128)(2,1)S(1)}, bf16[2,1024,128]{2,1,0:T(8,128)(2,1)S(1)}, u32[]{:S(2)}, u32[]{:S(2)}) collective-permute-start(bf16[2,1024,128]{2,1,0:T(8,128)(2,1)S(1)} %get-tuple-element.50), channel_id=1, source_target_pairs={{4,0},{8,4},{12,8},{16,12},{20,16},{24,20},{28,24}} | collective-permute-start | bytes 1572872 | tf_op jit(solution)/shard_map/ppermute | solution.py:39
  24.3 31.2 %collective-permute-start.1 = (bf16[2,1568,128]{2,1,0:T(8,128)(2,1)S(1)}, bf16[2,1568,128]{2,1,0:T(8,128)(2,1)S(1)}, u32[]{:S(2)}, u32[]{:S(2)}) collective-permute-start(bf16[2,1568,128]{2,1,0:T(8,128)(2,1)S(1)} %get-tuple-element.46), channel_id=1, source_target_pairs={{0,4},{4,8},{8,12},{12,16},{16,20},{20,24},{24,28},{1,5},{5,9},{9,... | collective-permute-start | bytes 2408456 | tf_op jit(solution)/shard_map/ppermute | solution.py:32
  33.1 22.5 %collective-permute-start.2 = (bf16[2,1568,128]{2,1,0:T(8,128)(2,1)S(1)}, bf16[2,1568,128]{2,1,0:T(8,128)(2,1)S(1)}, u32[]{:S(2)}, u32[]{:S(2)}) collective-permute-start(bf16[2,1568,128]{2,1,0:T(8,128)(2,1)S(1)} %get-tuple-element.47), channel_id=1, source_target_pairs={{4,0},{8,4},{12,8},{16,12},{20,16},{24,20},{28,24},{5,1},{9,5},{13... | collective-permute-start | bytes 2408456 | tf_op jit(solution)/shard_map/ppermute | solution.py:32
  35.1 26.8 %collective-permute-start.4 = (bf16[2,544,128]{2,1,0:T(8,128)(2,1)S(1)}, bf16[2,544,128]{2,1,0:T(8,128)(2,1)S(1)}, u32[]{:S(2)}, u32[]{:S(2)}) collective-permute-start(bf16[2,544,128]{2,1,0:T(8,128)(2,1)S(1)} %get-tuple-element.64), channel_id=1, source_target_pairs={{0,4},{4,8},{8,12},{12,16},{16,20},{20,24},{24,28},{1,5},{5,9},{9,... | collective-permute-start | bytes 835592 | tf_op jit(solution)/shard_map/ppermute | solution.py:32
  37.5 24.4 %collective-permute-start.5 = (bf16[2,544,128]{2,1,0:T(8,128)(2,1)S(1)}, bf16[2,544,128]{2,1,0:T(8,128)(2,1)S(1)}, u32[]{:S(2)}, u32[]{:S(2)}) collective-permute-start(bf16[2,544,128]{2,1,0:T(8,128)(2,1)S(1)} %get-tuple-element.63), channel_id=1, source_target_pairs={{4,0},{8,4},{12,8},{16,12},{20,16},{24,20},{28,24},{5,1},{9,5},{13... | collective-permute-start | bytes 835592 | tf_op jit(solution)/shard_map/ppermute | solution.py:32
  61.9 28.9 %copy-start.2 = (f32[2,8,1024]{2,1,0:T(8,128)S(1)}, f32[2,8,1024]{2,1,0:T(8,128)}, u32[]{:S(2)}) copy-start(f32[2,8,1024]{2,1,0:T(8,128)} %param.12) | copy-start | bytes 196612
  73.0 7.2 %collective-permute-start.8 = (bf16[512,128]{1,0:T(8,128)(2,1)S(1)}, bf16[512,128]{1,0:T(8,128)(2,1)S(1)}, u32[]{:S(2)}, u32[]{:S(2)}) collective-permute-start(bf16[512,128]{1,0:T(8,128)(2,1)S(1)} %get-tuple-element.55), channel_id=1, source_target_pairs={{0,4},{4,8},{8,12},{12,16},{16,20},{20,24},{24,28},{1,5},{5,9},{9,... | collective-permute-start | bytes 393224 | tf_op jit(solution)/shard_map/ppermute | solution.py:32
  74.9 7.0 %collective-permute-start.9 = (bf16[512,128]{1,0:T(8,128)(2,1)S(1)}, bf16[512,128]{1,0:T(8,128)(2,1)S(1)}, u32[]{:S(2)}, u32[]{:S(2)}) collective-permute-start(bf16[512,128]{1,0:T(8,128)(2,1)S(1)} %get-tuple-element.55), channel_id=1, source_target_pairs={{4,0},{8,4},{12,8},{16,12},{20,16},{24,20},{28,24},{5,1},{9,5},{13... | collective-permute-start | bytes 393224 | tf_op jit(solution)/shard_map/ppermute | solution.py:32
  84.6 4.6 %collective-permute-start.12 = (bf16[2,8,1024]{2,1,0:T(8,128)(2,1)S(1)}, bf16[2,8,1024]{2,1,0:T(8,128)(2,1)S(1)}, u32[]{:S(2)}, u32[]{:S(2)}) collective-permute-start(bf16[2,8,1024]{2,1,0:T(8,128)(2,1)S(1)} %get-tuple-element.58), channel_id=1, source_target_pairs={{0,3},{4,7},{8,11},{12,15},{16,19},{20,23},{24,27},{28,31}} | collective-permute-start | bytes 98312 | tf_op jit(solution)/shard_map/ppermute | solution.py:32
  85.9 3.3 %collective-permute-start.11 = (bf16[2,8,1024]{2,1,0:T(8,128)(2,1)S(1)}, bf16[2,8,1024]{2,1,0:T(8,128)(2,1)S(1)}, u32[]{:S(2)}, u32[]{:S(2)}) collective-permute-start(bf16[2,8,1024]{2,1,0:T(8,128)(2,1)S(1)} %get-tuple-element.58), channel_id=1, source_target_pairs={{0,2},{1,3},{4,6},{5,7},{8,10},{9,11},{12,14},{13,15},{16,18},{17,... | collective-permute-start | bytes 98312 | tf_op jit(solution)/shard_map/ppermute | solution.py:32
  87.2 3.6 %collective-permute-start.10 = (bf16[2,8,1024]{2,1,0:T(8,128)(2,1)S(1)}, bf16[2,8,1024]{2,1,0:T(8,128)(2,1)S(1)}, u32[]{:S(2)}, u32[]{:S(2)}) collective-permute-start(bf16[2,8,1024]{2,1,0:T(8,128)(2,1)S(1)} %get-tuple-element.58), channel_id=1, source_target_pairs={{0,1},{1,2},{2,3},{4,5},{5,6},{6,7},{8,9},{9,10},{10,11},{12,13},{... | collective-permute-start | bytes 98312 | tf_op jit(solution)/shard_map/ppermute | solution.py:32

commit v2 on v1

--- a/solution.py
+++ b/solution.py
@@ -87,21 +87,9 @@
     return [(0, r, 0) for r in inner] + [(1, r, far) for r in inner]
 
 
-def fetch(pieces, pix_ref, dst_ref, sem):
-    width = dst_ref.shape[1]
-    copies = []
-    for n, (sec, row, col0) in enumerate(pieces):
-        copy = pltpu.make_async_copy(
-            pix_ref.at[sec, row, col0 : col0 + width, :], dst_ref.at[n], sem.at[n]
-        )
-        copy.start()
-        copies.append(copy)
-    return copies
-
-
-def pair_of(ref, n):
-    width, patch = ref.shape[1:]
-    return ref[n : n + 2].reshape(2 * width, patch)
+def pixel_pair(pix_ref, pieces, n, width):
+    rows = [pix_ref[sec, row, col0 : col0 + width, :] for sec, row, col0 in pieces[n : n + 2]]
+    return jnp.concatenate(rows, 0)
 
 
 def zero_sides(ref, cols):
@@ -120,44 +108,58 @@
 
 def encode_front_kernel(
     half, pix_ref, wh_in, wf_in, gain_in, pred_ref,
-    front_ref, odd_ref, next_ref, wh_ref, wf_ref, gain_ref, top_ref, bottom_ref,
-    pix_s, pre_s, sem, next_sem, more_sem,
+    front_ref, odd_ref, wh_ref, wf_ref, gain_ref, top_ref, bottom_ref,
+    pix_s, pre_s, sem, more_sem,
 ):
     rows, cols = pix_ref.shape[1:3]
     width = front_ref.shape[1]
-    far = cols - width
-    constants = [(wh_in, wh_ref), (wf_in, wf_ref), (gain_in, gain_ref)]
-    start_all(constants, more_sem)
-    copies = fetch(pieces_of("front", rows, far), pix_ref, pix_s, sem)
+    pieces = pieces_of("front", rows, cols - width)
+    loads = [
+        (pix_ref.at[sec, row, col0 : col0 + width, :], pix_s.at[n])
+        for n, (sec, row, col0) in enumerate(pieces)
+    ]
+    copies = copies_of(loads, sem)
+    constants = copies_of([(wh_in, wh_ref), (wf_in, wf_ref), (gain_in, gain_ref)], more_sem)
     edges = [(pred_ref.at[0:REACH], top_ref), (pred_ref.at[rows - REACH : rows], bottom_ref)]
-    start_all(edges, more_sem.at[len(constants) :])
-    following = fetch(pieces_of("border", rows, far), pix_ref, next_ref, next_sem)
+    edge_sem = more_sem.at[len(constants) :]
+    is_first = lax.axis_index("sec") == 0
+    for copy in copies[:2] + constants + copies[2:4]:
+        copy.start()
+
+    @pl.when(is_first)
+    def _():
+        start_all(edges, edge_sem)
+
     zero_sides(odd_ref, cols)
-    wait_all(constants, more_sem)
+    for copy in constants:
+        copy.wait()
 
     def pix_of(n):
+        for copy in copies[n + 4 : n + 6]:
+            copy.start()
         copies[n].wait()
         copies[n + 1].wait()
-        return pair_of(pix_s, n)
+        return pix_s[n : n + 2].reshape(2 * width, pix_s.shape[2])
 
     def store(n, value):
         front_ref[n] = value
         put_left(odd_ref, n, value, half)
 
-    encode_steps(pix_of, len(copies), width, store, wh_ref, wf_ref, gain_ref, pre_s)
-    wait_all(edges, more_sem.at[len(constants) :])
-    for copy in following:
-        copy.wait()
+    encode_steps(pix_of, len(pieces), width, store, wh_ref, wf_ref, gain_ref, pre_s)
+
+    @pl.when(is_first)
+    def _():
+        wait_all(edges, edge_sem)
 
 
 def encode_border_kernel(
-    half, pix_ref, wh_ref, wf_ref, gain_ref, own_ref, odd_in, off_ref, mask_ref,
-    odd_ref, even_ref, back_ref, up_ref, down_ref, next_ref, pre_s, next_sem,
+    half, pix_ref, wh_ref, wf_ref, gain_ref, odd_in, off_ref, mask_ref,
+    odd_ref, even_ref, back_ref, up_ref, down_ref, pre_s,
 ):
     rows, cols = pix_ref.shape[1:3]
-    width = own_ref.shape[1]
+    width = up_ref.shape[1] - cols
     border = border_rows(rows)
-    following = fetch(pieces_of("back", rows, cols - width), pix_ref, next_ref, next_sem)
+    pieces = pieces_of("border", rows, cols - width)
     zero_sides(even_ref, cols)
     first = half // LANES - 1
     for tile in range(cols // LANES - first):
@@ -183,35 +185,31 @@
             put_right(odd_ref, row, value, half)
             pack[m % REACH, cols : cols + width, :] = value
 
-    encode_steps(lambda n: pair_of(own_ref, n), own_ref.shape[0], width, store, wh_ref, wf_ref, gain_ref, pre_s)
-    for copy in following:
-        copy.wait()
-
-
-def encode_back_kernel(
-    half, pix_ref, wh_ref, wf_ref, gain_ref, own_ref, even_in, back_in,
-    even_ref, back_ref, next_ref, pre_s, next_sem,
-):
+    encode_steps(
+        lambda n: pixel_pair(pix_ref, pieces, n, width), len(pieces), width, store, wh_ref, wf_ref, gain_ref, pre_s
+    )
+
+
+def encode_back_kernel(half, pix_ref, wh_ref, wf_ref, gain_ref, even_in, back_in, even_ref, back_ref, pre_s):
     rows, cols = pix_ref.shape[1:3]
-    width = own_ref.shape[1]
+    width = pre_s.shape[1] // 2
     inner = inner_rows(rows)
-    following = fetch(pieces_of("inner", rows, cols - width), pix_ref, next_ref, next_sem)
+    pieces = pieces_of("back", rows, cols - width)
 
     def store(n, value):
         back_ref[inner[n] * width : (inner[n] + 1) * width, :] = value
         put_right(even_ref, inner[n], value, half)
 
-    encode_steps(lambda n: pair_of(own_ref, n), own_ref.shape[0], width, store, wh_ref, wf_ref, gain_ref, pre_s)
-    for copy in following:
-        copy.wait()
-
-
-def encode_inner_kernel(
-    half, wh_ref, wf_ref, gain_ref, own_ref, odd_in, even_in, odd_ref, even_ref, pre_s
-):
-    width = own_ref.shape[1]
-    rows = odd_ref.shape[0] - 2 * REACH
+    encode_steps(
+        lambda n: pixel_pair(pix_ref, pieces, n, width), len(pieces), width, store, wh_ref, wf_ref, gain_ref, pre_s
+    )
+
+
+def encode_inner_kernel(half, pix_ref, wh_ref, wf_ref, gain_ref, odd_in, even_in, odd_ref, even_ref, pre_s):
+    rows, cols = pix_ref.shape[1:3]
+    width = pre_s.shape[1] // 2
     inner = inner_rows(rows)
+    pieces = pieces_of("inner", rows, cols - width)
 
     def store(n, value):
         part, m = divmod(n, len(inner))
@@ -220,7 +218,9 @@
         else:
             put_right(odd_ref, inner[m], value, half)
 
-    encode_steps(lambda n: pair_of(own_ref, n), own_ref.shape[0], width, store, wh_ref, wf_ref, gain_ref, pre_s)
+    encode_steps(
+        lambda n: pixel_pair(pix_ref, pieces, n, width), len(pieces), width, store, wh_ref, wf_ref, gain_ref, pre_s
+    )
 
 
 def flops_of(nodes, patch, hid, feat):
@@ -231,7 +231,11 @@
 
 def align(band, first, lift, row):
     band = pltpu.roll(band, (2 * LANES - first - BASE + 2 + lift) % LANES, 1)
-    for shift in (1, 2, 4):
+    return jnp.where((row & 4) != 0, pltpu.roll(band, LANES - 4, 1), band)
+
+
+def settle(band, row):
+    for shift in (2, 1):
         band = jnp.where((row & shift) != 0, pltpu.roll(band, LANES - shift, 1), band)
     return band
 
@@ -280,7 +284,7 @@
     for i in range(low // 8, LANES // 8):
         one = align(m_s[r, 8 * i : 8 * i + 8, :], 8 * i, 0, row)
         two = align(m_s[r + 1, 8 * i : 8 * i + 8, :], 8 * i, 8, row)
-        groups.append(jnp.where((lane & 8) != 0, two, one))
+        groups.append(settle(jnp.where((lane & 8) != 0, two, one), row))
     turned = jnp.concatenate(groups, 0).T
     lanes = pl.ds(pl.multiple_of(k * LANES, LANES), LANES)
     for n in range(2):
@@ -300,16 +304,17 @@
 
     if low:
         columns(0, 0, low)
-    pairs, odd = (tiles - first) // 2, (tiles - first) % 2
+    step = m_s.shape[0]
+    whole, odd = (tiles - first) // step, (tiles - first) % step
 
     def body(n, carry):
-        for m in range(2):
-            columns(m, 2 * n + m + first, 0)
+        for m in range(step):
+            columns(m, step * n + m + first, 0)
         return carry
 
-    lax.fori_loop(0, pairs, body, 0)
-    if odd:
-        columns(0, tiles - 1, 0)
+    lax.fori_loop(0, whole, body, 0)
+    for m in range(odd):
+        columns(m, tiles - odd + m, 0)
 
 
 def padded_query(ref, tile0=0):
@@ -422,83 +427,113 @@
 
 
 def own_scores_kernel(
-    half, even_ref, odd_ref, up_ref, down_ref, off_ref, s_in, s_s, flow_ref, halo_s, m_s, sem
-):
-    rows = odd_ref.shape[0] - 2 * REACH
-    cols = 2 * half
-    halos = [
-        (up_ref.at[:, 0:cols, :], halo_s.at[0:REACH, PAD : PAD + cols, :]),
-        (down_ref.at[:, 0:cols, :], halo_s.at[REACH : 2 * REACH, PAD : PAD + cols, :]),
-    ]
-    start_all(halos, sem)
-    zero_sides(halo_s, cols)
-    wait_all(halos, sem)
-    score_job(
-        padded_query(odd_ref), padded_window(even_ref, halo_s), m_s, s_s, cols // LANES, 0,
-        ((0, REACH), (rows - REACH, rows)),
-    )
-    flows_of(s_s, off_ref.at[1], flow_ref, cols // LANES)
-
-
-def pairs_out(pack_ref, at, tops, bottoms):
-    for n, (top, bottom) in enumerate(zip(tops, bottoms)):
-        pack_ref[at + 16 * n : at + 16 * n + 16, :] = jnp.concatenate([top, bottom], 0).astype(BF16)
-    return at + 16 * len(tops)
-
-
-def cross_scores_kernel(
-    half, back_ref, odd_ref, up_ref, down_ref, front_ref, fup_ref, fdown_ref,
-    pred_ref, pup_ref, pdown_ref, even_ref, off_ref, mask_ref, flow1_ref, flow0_ref,
-    flow2_ref, flow_ref, pack_ref, halo_s, ref_s, s_s, m_s, sem, sem0,
+    half, even_ref, odd_ref, up_ref, down_ref, off_ref, s_in, front_ref, pred_ref,
+    s_s, flow_ref, ref_next, halo_next, halo_s, m_s, sem, next_sem, ref_sem,
 ):
     rows = odd_ref.shape[0] - 2 * REACH
     cols = 2 * half
     width = front_ref.shape[1]
     far = cols - width
     is_first = lax.axis_index("sec") == 0
+    halos = [
+        (up_ref.at[:, 0:cols, :], halo_s.at[0:REACH, PAD : PAD + cols, :]),
+        (down_ref.at[:, 0:cols, :], halo_s.at[REACH : 2 * REACH, PAD : PAD + cols, :]),
+    ]
+    start_all(halos, sem)
+    to = slice(PAD + far, PAD + cols)
+    beyond = [
+        (up_ref.at[:, cols : cols + width, :], halo_next.at[0:REACH, to, :]),
+        (down_ref.at[:, cols : cols + width, :], halo_next.at[REACH : 2 * REACH, to, :]),
+    ]
+    start_all(beyond, next_sem)
+    inside = ref_next.at[REACH : rows + REACH, PAD : PAD + width, :]
+    before = [(pred_ref.at[:, 0:width, :], inside)]
+    passed = [(front_ref, inside)]
+
+    @pl.when(is_first)
+    def _():
+        start_all(before, ref_sem)
+
+    @pl.when(jnp.logical_not(is_first))
+    def _():
+        start_all(passed, ref_sem)
+
+    zero_sides(halo_s, cols)
+    zero_sides(halo_next, cols)
+    ref_next[:, PAD - EDGE : PAD, :] = jnp.zeros((rows + 2 * REACH, EDGE, LANES), BF16)
+    wait_all(halos, sem)
+    score_job(
+        padded_query(odd_ref), padded_window(even_ref, halo_s), m_s, s_s, cols // LANES, 0,
+        ((0, REACH), (rows - REACH, rows)),
+    )
+    flows_of(s_s, off_ref.at[1], flow_ref, cols // LANES)
+    wait_all(beyond, next_sem)
+
+    @pl.when(is_first)
+    def _():
+        wait_all(before, ref_sem)
+
+    @pl.when(jnp.logical_not(is_first))
+    def _():
+        wait_all(passed, ref_sem)
+
+
+def front_scores_kernel(
+    half, even_ref, ref_in, fup_ref, fdown_ref, pup_ref, pdown_ref, off_ref, flow0_ref,
+    ref_s, flow_ref, s_s, m_s, sem,
+):
+    rows = even_ref.shape[0] - 2 * REACH
+    cols = 2 * half
+    width = fup_ref.shape[1]
+    is_first = lax.axis_index("sec") == 0
+    above = ref_s.at[0:REACH, PAD : PAD + width, :]
+    below = ref_s.at[rows + REACH : rows + 2 * REACH, PAD : PAD + width, :]
+    before = [(pup_ref.at[:, 0:width, :], above), (pdown_ref.at[:, 0:width, :], below)]
+    passed = [(fup_ref, above), (fdown_ref, below)]
+
+    @pl.when(is_first)
+    def _():
+        start_all(before, sem)
+        wait_all(before, sem)
+
+    @pl.when(jnp.logical_not(is_first))
+    def _():
+        start_all(passed, sem)
+        wait_all(passed, sem)
+
+    tiles = half // LANES
+    score_job(padded_query(even_ref), padded_window(ref_s), m_s, s_s, tiles)
+    flow_ref[:, :, half:cols] = flow0_ref[:, :, LANES:]
+    flows_of(s_s, off_ref.at[0], flow_ref, tiles)
+
+
+def pairs_out(pack_ref, at, tops, bottoms):
+    for n, (top, bottom) in enumerate(zip(tops, bottoms)):
+        pack_ref[at + 16 * n : at + 16 * n + 16, :] = jnp.concatenate([top, bottom], 0).astype(BF16)
+    return at + 16 * len(tops)
+
+
+def back_scores_kernel(
+    half, back_ref, odd_ref, halo_ref, mask_ref, flow1_ref, flow_ref,
+    flow2_ref, pack_ref, s_s, m_s,
+):
+    rows = odd_ref.shape[0] - 2 * REACH
+    cols = 2 * half
     tile0 = half // LANES - 1
     tiles = cols // LANES - tile0
-    pack = slice(cols, cols + width)
-    to = slice(PAD + far, PAD + cols)
-    span = slice(PAD, PAD + width)
-    above, below = slice(0, REACH), slice(rows + REACH, rows + 2 * REACH)
-    halos = [
-        (up_ref.at[:, pack, :], halo_s.at[0:REACH, to, :]),
-        (down_ref.at[:, pack, :], halo_s.at[REACH : 2 * REACH, to, :]),
-    ]
-    before = [
-        (pred_ref.at[:, 0:width, :], ref_s.at[REACH : rows + REACH, span, :]),
-        (pup_ref.at[:, 0:width, :], ref_s.at[above, span, :]),
-        (pdown_ref.at[:, 0:width, :], ref_s.at[below, span, :]),
-    ]
-    passed = [
-        (front_ref, ref_s.at[REACH : rows + REACH, span, :]),
-        (fup_ref, ref_s.at[above, span, :]),
-        (fdown_ref, ref_s.at[below, span, :]),
-    ]
-    start_all(halos, sem)
-
-    @pl.when(is_first)
-    def _():
-        start_all(before, sem0)
-
-    @pl.when(jnp.logical_not(is_first))
-    def _():
-        start_all(passed, sem0)
-
-    zero_sides(halo_s, cols)
-    wait_all(halos, sem)
+    width = (back_ref.shape[0] - 4 * rows * tiles) // rows
+    far = cols - width
 
     def query_of(r, k, low):
-        at = (k + tile0) * LANES + low - far
-        size = LANES - low
-        return back_ref[pl.ds(pl.multiple_of(at + r * width, 16), size), :]
-
-    score_job(query_of, padded_window(odd_ref, halo_s, tile0), m_s, s_s, tiles, LANES - EDGE)
+        at = (k + tile0) * LANES + low - far + r * width
+        return back_ref[pl.ds(pl.multiple_of(at, 16), LANES - low), :]
+
+    score_job(query_of, padded_window(odd_ref, halo_ref, tile0), m_s, s_s, tiles, LANES - EDGE)
 
     def body(k, carry):
         lanes = pl.ds(pl.multiple_of(k * LANES, LANES), LANES)
-        extra = back_ref[pl.ds(pl.multiple_of(k * 4 * rows + rows * width, 4 * rows), 4 * rows), :].astype(F32)
+        at = pl.multiple_of(k * 4 * rows + rows * width, 4 * rows)
+        extra = back_ref[pl.ds(at, 4 * rows), :].astype(F32)
         fy, fx = flow_tile(s_s, extra[:rows], extra[rows : 2 * rows], lanes)
         flow2_ref[0, :, lanes] = fy
         flow2_ref[1, :, lanes] = fx
@@ -506,20 +541,6 @@
         return carry
 
     lax.fori_loop(0, tiles, body, 0)
-
-    @pl.when(is_first)
-    def _():
-        wait_all(before, sem0)
-
-    @pl.when(jnp.logical_not(is_first))
-    def _():
-        wait_all(passed, sem0)
-
-    ref_s[:, PAD - EDGE : PAD, :] = jnp.zeros((rows + 2 * REACH, EDGE, LANES), BF16)
-    tiles = half // LANES
-    score_job(padded_query(even_ref), padded_window(ref_s), m_s, s_s, tiles)
-    flow_ref[:, :, half:cols] = flow0_ref[:, :, LANES:]
-    flows_of(s_s, off_ref.at[0], flow_ref, tiles)
 
     def tiles_of(ref, count):
         return [ref[:, n * LANES : (n + 1) * LANES] for n in range(count)]
@@ -621,7 +642,6 @@
     assert secs == 2 and rows == ITERS and feat == LANES and cols % (2 * LANES) == 0
     half = cols // 2
     width = half + 2 * EDGE
-    inner = rows - 2 * REACH
     span = half + LANES
     deep = rows + 2 * REACH
     tail = 4 * rows * (span // LANES)
@@ -645,49 +665,44 @@
             cost_estimate=cost,
         )(*ins)
 
-    def pixels_for(kind):
-        return shape((len(pieces_of(kind, rows, 0)), width, patch), BF16)
-
     def encode_cost(kind):
         return flops_of(len(pieces_of(kind, rows, 0)) * width, patch, hid, feat)
 
-    pixels, w_hidden, w_feature, gain, pred = (
-        pltpu.with_memory_space_constraint(x, pltpu.HBM) for x in (pixels, w_hidden, w_feature, gain, pred)
-    )
+    def in_place(value):
+        return pltpu.with_memory_space_constraint(value, pltpu.HBM)
+
     edges = shape((REACH, cols, feat), BF16)
-    front, odd, pix, wh, wf, gain, top, bottom = call(
+    front, odd, wh, wf, gain, top, bottom = call(
         encode_front_kernel,
-        (pixels, w_hidden, w_feature, gain, pred), [HBM] * 5,
+        (in_place(pixels), in_place(w_hidden), in_place(w_feature), in_place(gain), in_place(pred)), [HBM] * 5,
         (
-            shape((rows, width, feat), BF16), padded, pixels_for("border"),
+            shape((rows, width, feat), BF16), padded,
             shape(w_hidden.shape, BF16), shape(w_feature.shape, BF16), shape(gain.shape, F32), edges, edges,
         ),
-        [pltpu.VMEM((rows, width, patch), BF16), pre, dma((rows,)), dma((6 * REACH,)), dma((5,))],
+        [pltpu.VMEM((rows, width, patch), BF16), pre, dma((rows,)), dma((5,))],
         encode_cost("front"), 12,
     )
-    weights = (wh, wf, gain)
+    weights = (pixels, wh, wf, gain)
     front_in = hop(front, "sec", 1)
     pup = hop_plane(bottom, 1)
     pdown = hop_plane(top, -1)
     pack = shape((REACH, cols + width, feat), BF16)
-    odd, even, back, up, down, pix = call(
+    odd, even, back, up, down = call(
         encode_border_kernel,
-        (pixels, *weights, pix, odd, offsets, mask), [HBM] + [VMEM] * 7,
-        (padded, padded, shape((rows * width + tail, feat), BF16), pack, pack, pixels_for("back")),
-        [pre, dma((inner,))], encode_cost("border"), 12, {5: 0},
+        (*weights, odd, offsets, mask), [VMEM] * 7,
+        (padded, padded, shape((rows * width + tail, feat), BF16), pack, pack),
+        [pre], encode_cost("border"), 10, {4: 0},
     )
     up_in = hop(up, "tile", 1)
     down_in = hop(down, "tile", -1)
-    even, back, pix = call(
-        encode_back_kernel,
-        (pixels, *weights, pix, even, back), [HBM] + [VMEM] * 6,
-        (padded, shape(back.shape, BF16), pixels_for("inner")),
-        [pre, dma((2 * inner,))], encode_cost("back"), 12, {5: 0, 6: 1},
+    even, back = call(
+        encode_back_kernel, (*weights, even, back), [VMEM] * 6,
+        (padded, shape(back.shape, BF16)), [pre], encode_cost("back"), 10, {4: 0, 5: 1},
     )
     back_in = hop(back, "sec", -1)
     odd, even = call(
-        encode_inner_kernel, (*weights, pix, odd, even), [VMEM] * 6,
-        (padded, padded), [pre], encode_cost("inner"), 12, {4: 0, 5: 1},
+        encode_inner_kernel, (*weights, odd, even), [VMEM] * 6,
+        (padded, padded), [pre], encode_cost("inner"), 10, {4: 0, 5: 1},
     )
 
     bands = SEG * (2 * REACH + 1)
@@ -699,34 +714,36 @@
         )
 
     halo = pltpu.VMEM((2 * REACH, full, feat), BF16)
-    grids = pltpu.VMEM((rows, bands, cols), F32)
     turning = pltpu.VMEM((2, rows, LANES, LANES), F32)
+    turning4 = pltpu.VMEM((4, rows, LANES, LANES), F32)
     whole = pltpu.VMEM((deep, full, feat), BF16)
     flow0_shape = shape((2, rows, span), F32)
     scores, flow0 = call(
-        near_scores_kernel, (even, odd, pred, pup, pdown, offsets),
+        near_scores_kernel, (even, odd, in_place(pred), pup, pdown, offsets),
         [VMEM] * 2 + [HBM] + [VMEM] * 3, (shape((rows, bands, cols), F32), flow0_shape),
-        [whole, pltpu.VMEM((rows, bands, span), F32), turning, dma((3,))], score_cost(0.5), 16,
+        [whole, pltpu.VMEM((rows, bands, span), F32), turning4, dma((3,))], score_cost(0.5), 18,
     )
     fup_in = hop(front_in[rows - REACH :], "tile", 1)
     fdown_in = hop(front_in[:REACH], "tile", -1)
-    _, flow1 = call(
-        own_scores_kernel, (even, odd, up_in, down_in, offsets, scores), [VMEM] * 6,
-        (shape(scores.shape, F32), shape((2, rows, cols), F32)),
-        [halo, turning, dma((2,))], score_cost(0.5), 12, {5: 0},
+    ref_shape = shape((deep, half + 3 * PAD, feat), BF16)
+    _, flow1, ref, beyond = call(
+        own_scores_kernel, (even, odd, up_in, down_in, offsets, scores, front_in, in_place(pred)),
+        [VMEM] * 7 + [HBM],
+        (shape(scores.shape, F32), shape((2, rows, cols), F32), ref_shape, shape((2 * REACH, full, feat), BF16)),
+        [halo, turning4, dma((2,)), dma((2,)), dma((1,))], score_cost(0.5), 14, {5: 0},
+    )
+    _, flow3 = call(
+        front_scores_kernel, (even, ref, fup_in, fdown_in, pup, pdown, offsets, flow0),
+        [VMEM] * 8, (ref_shape, shape((2, rows, cols), F32)),
+        [pltpu.VMEM((rows, bands, half), F32), turning, dma((2,))], score_cost(0.5), 12, {1: 0},
     )
 
     tiles = 2 * (cols // LANES) + span // LANES
     pack_rows = 16 * tiles + 16 * ((tiles + 1) // 2)
-    flow2, flow3, pack = call(
-        cross_scores_kernel,
-        (
-            back_in, odd, up_in, down_in, front_in, fup_in, fdown_in,
-            pred, pup, pdown, even, offsets, mask, flow1, flow0,
-        ),
-        [VMEM] * 7 + [HBM] + [VMEM] * 7,
-        (shape((3, rows, span), F32), shape((2, rows, cols), F32), shape((pack_rows, LANES), BF16)),
-        [halo, whole, grids, turning, dma((2,)), dma((3,))], score_cost(1.0), 20,
+    flow2, pack = call(
+        back_scores_kernel, (back_in, odd, beyond, mask, flow1, flow3), [VMEM] * 6,
+        (shape((3, rows, span), F32), shape((pack_rows, LANES), BF16)),
+        [pltpu.VMEM((rows, bands, span), F32), turning], score_cost(0.55), 12,
     )
     pack_up = hop(pack, "tile", 1)
     pack_down = hop(pack, "tile", -1)

time: 93.1 us -> 88.7 us (0.953)
  Pallas kernels: 46.7 us -> 39.5 us
  waiting for transfers between devices: 10.9 us -> 12.7 us
  starting transfers between devices: 32.8 us -> 33.9 us
    pallas_call x7 -> x8, Pallas kernels: 44.1 us -> 36.9 us  [call(): pl.pallas_call(functools.partial(kernel, half), out_shape=outs, in_specs=...]
    ppermute x11, waiting for transfers between devices: 10.9 us -> 12.7 us  [hop(): return lax.ppermute(value, axis, pairs)]
    ppermute x11, starting transfers between devices: 26.3 us -> 27.5 us  [hop(): return lax.ppermute(value, axis, pairs)]
  transfers between devices with their start and end apart: 13 -> 13, of which waited for: 4 -> 4; matrix products, arithmetic and copies ran while one was open for 0% -> 0% of each run, Pallas kernels for 30% -> 31%
where the time goes in v2:
time: 88.7 us; the launch traced here: 87.1 us
  Pallas kernels  39.5 us (45%)
  starting transfers between devices  33.9 us (38%)
  waiting for transfers between devices  12.7 us (14%)
    pallas_call x8, Pallas kernels, call(): pl.pallas_call(functools.partial(kernel, half), out_shape=outs, in_specs=...  36.9 us
    ppermute x11, starting transfers between devices, hop(): return lax.ppermute(value, axis, pairs)  27.5 us
    ppermute x11, waiting for transfers between devices, hop(): return lax.ppermute(value, axis, pairs)  12.7 us
    ppermute x2, starting transfers between devices, hop_plane(): return lax.ppermute(value, ('tile', 'sec'), pairs)  6.46 us
    pallas_call x1, Pallas kernels, shards(): pl.pallas_call(functools.partial(relax_kernel, half), out_shape=(shape((2...  2.6 us
  transfers between devices with their start and end apart: 13, of which 4 were waited for; matrix products, arithmetic and copies ran while one was open for 0% of the time, Pallas kernels for 31%

profile of v2, /device:TPU:4, one launch (start us, length us, event | category | flops | bytes accessed | tf_op | source)
XLA Modules:
  0.0 87.1 jit_solution(5084871605259427193)
XLA Ops:
  0.0 4.9 %shard_map.82 = (bf16[8,544,128]{2,1,0:T(8,128)(2,1)S(1)}, bf16[12,1280,128]{2,1,0:T(8,128)(2,1)S(1)}, bf16[256,512]{1,0:T(8,128)(2,1)S(1)}, bf16[512,128]{1,0:T...) custom-call(bf16[2,8,1024,256]{3,2,1,0:T(8,128)(2,1)} %pix_ref.7, ...), custom_call_target="tpu_custom_call" | custom-call | flops 1711276032 | bytes 3342336 | tf_op jit(solution)/shard_map/pallas_call | solution.py:657
  4.9 3.5 %collective-permute-start.5 = (bf16[8,544,128]{2,1,0:T(8,128)(2,1)S(1)}, bf16[8,544,128]{2,1,0:T(8,128)(2,1)S(1)}, u32[]{:S(2)}, u32[]{:S(2)}) collective-permute-start(bf16[8,544,128]{2,1,0:T(8,128)(2,1)S(1)} %get-tuple-element.48), channel_id=1, source_target_pairs={{0,1},{1,2},{2,3},{4,5},{5,6},{6,7},{8,9},{9,10},{10,11},{12,13},{... | collective-permute-start | bytes 3342344 | tf_op jit(solution)/shard_map/ppermute | solution.py:32
  8.5 3.8 %shard_map.83 = (bf16[12,1280,128]{2,1,0:T(8,128)(2,1)S(1)}, bf16[12,1280,128]{2,1,0:T(8,128)(2,1)S(1)}, bf16[4512,128]{1,0:T(8,128)(2,1)S(1)}, bf16[2,1568,128]...) custom-call(bf16[2,8,1024,256]{3,2,1,0:T(8,128)(2,1)S(1)} %copy-done, ...), custom_call_target="tpu_custom_call", output_to_operand_aliasing={{0}: (4, {})} | custom-call | flops 2566914048 | bytes 5013504 | tf_op jit(solution)/shard_map/pallas_call | solution.py:657
  12.4 1.5 %shard_map.84 = (bf16[12,1280,128]{2,1,0:T(8,128)(2,1)S(1)}, bf16[4512,128]{1,0:T(8,128)(2,1)S(1)}) custom-call(bf16[2,8,1024,256]{3,2,1,0:T(8,128)(2,1)S(1)} %copy-done, bf16[256,512]{1,0:T(8,128)(2,1)S(1)} %get-tuple-element.32.wh_ref, bf16[512,128]{1,0:T(8,128)(2,1)S(1)} %get-tuple-element.33.wf_ref, ...), custom_call_target="tpu_custom_call", output_to_operand_aliasing={{0}: (4, {}), {1}: (5, {})} | custom-call | flops 855638016 | bytes 1671168 | tf_op jit(solution)/shard_map/pallas_call | solution.py:657
  13.9 1.3 %collective-permute-start = (bf16[4512,128]{1,0:T(8,128)(2,1)S(1)}, bf16[4512,128]{1,0:T(8,128)(2,1)S(1)}, u32[]{:S(2)}, u32[]{:S(2)}) collective-permute-start(bf16[4512,128]{1,0:T(8,128)(2,1)S(1)} %get-tuple-element.38), channel_id=1, source_target_pairs={{1,0},{2,1},{3,2},{5,4},{6,5},{7,6},{9,8},{10,9},{11,10},{13,12},{... | collective-permute-start | bytes 3465224 | tf_op jit(solution)/shard_map/ppermute | solution.py:32
  15.2 1.9 %collective-permute-start.3 = (bf16[2,1024,128]{2,1,0:T(8,128)(2,1)S(1)}, bf16[2,1024,128]{2,1,0:T(8,128)(2,1)S(1)}, u32[]{:S(2)}, u32[]{:S(2)}) collective-permute-start(bf16[2,1024,128]{2,1,0:T(8,128)(2,1)S(1)} %get-tuple-element.45), channel_id=1, source_target_pairs={{0,4},{4,8},{8,12},{12,16},{16,20},{20,24},{24,28}} | collective-permute-start | bytes 1572872 | tf_op jit(solution)/shard_map/ppermute | solution.py:39
  17.1 4.5 %collective-permute-start.4 = (bf16[2,1024,128]{2,1,0:T(8,128)(2,1)S(1)}, bf16[2,1024,128]{2,1,0:T(8,128)(2,1)S(1)}, u32[]{:S(2)}, u32[]{:S(2)}) collective-permute-start(bf16[2,1024,128]{2,1,0:T(8,128)(2,1)S(1)} %get-tuple-element.46), channel_id=1, source_target_pairs={{4,0},{8,4},{12,8},{16,12},{20,16},{24,20},{28,24}} | collective-permute-start | bytes 1572872 | tf_op jit(solution)/shard_map/ppermute | solution.py:39
  21.7 1.9 %collective-permute-start.1 = (bf16[2,1568,128]{2,1,0:T(8,128)(2,1)S(1)}, bf16[2,1568,128]{2,1,0:T(8,128)(2,1)S(1)}, u32[]{:S(2)}, u32[]{:S(2)}) collective-permute-start(bf16[2,1568,128]{2,1,0:T(8,128)(2,1)S(1)} %get-tuple-element.43), channel_id=1, source_target_pairs={{0,4},{4,8},{8,12},{12,16},{16,20},{20,24},{24,28},{1,5},{5,9},{9,... | collective-permute-start | bytes 2408456 | tf_op jit(solution)/shard_map/ppermute | solution.py:32
  23.6 8.6 %collective-permute-done.5.front_ref = bf16[8,544,128]{2,1,0:T(8,128)(2,1)S(1)} collective-permute-done((bf16[8,544,128]{2,1,0:T(8,128)(2,1)S(1)}, bf16[8,544,128]{2,1,0:T(8,128)(2,1)S(1)}, u32[]{:S(2)}, u32[]{:S(2)}) %collective-permute-start.5) | collective-permute-done | bytes 1114144 | tf_op jit(solution)/shard_map/ppermute | solution.py:32
  32.2 1.9 %collective-permute-start.2 = (bf16[2,1568,128]{2,1,0:T(8,128)(2,1)S(1)}, bf16[2,1568,128]{2,1,0:T(8,128)(2,1)S(1)}, u32[]{:S(2)}, u32[]{:S(2)}) collective-permute-start(bf16[2,1568,128]{2,1,0:T(8,128)(2,1)S(1)} %get-tuple-element.44), channel_id=1, source_target_pairs={{4,0},{8,4},{12,8},{16,12},{20,16},{24,20},{28,24},{5,1},{9,5},{13... | collective-permute-start | bytes 2408456 | tf_op jit(solution)/shard_map/ppermute | solution.py:32
  34.2 0.0 collective-permute-done.3.pup_ref
  34.2 2.4 %collective-permute-start.6 = (bf16[2,544,128]{2,1,0:T(8,128)(2,1)S(1)}, bf16[2,544,128]{2,1,0:T(8,128)(2,1)S(1)}, u32[]{:S(2)}, u32[]{:S(2)}) collective-permute-start(bf16[2,544,128]{2,1,0:T(8,128)(2,1)S(1)} %get-tuple-element.62), channel_id=1, source_target_pairs={{0,4},{4,8},{8,12},{12,16},{16,20},{20,24},{24,28},{1,5},{5,9},{9,... | collective-permute-start | bytes 835592 | tf_op jit(solution)/shard_map/ppermute | solution.py:32
  36.6 0.0 collective-permute-done.4.pdown_ref
  36.6 4.2 %collective-permute-start.7 = (bf16[2,544,128]{2,1,0:T(8,128)(2,1)S(1)}, bf16[2,544,128]{2,1,0:T(8,128)(2,1)S(1)}, u32[]{:S(2)}, u32[]{:S(2)}) collective-permute-start(bf16[2,544,128]{2,1,0:T(8,128)(2,1)S(1)} %get-tuple-element.61), channel_id=1, source_target_pairs={{4,0},{8,4},{12,8},{16,12},{20,16},{24,20},{28,24},{5,1},{9,5},{13... | collective-permute-start | bytes 835592 | tf_op jit(solution)/shard_map/ppermute | solution.py:32
  40.9 2.7 %shard_map.85 = (bf16[12,1280,128]{2,1,0:T(8,128)(2,1)S(1)}, bf16[12,1280,128]{2,1,0:T(8,128)(2,1)S(1)}) custom-call(bf16[2,8,1024,256]{3,2,1,0:T(8,128)(2,1)S(1)} %copy-done, bf16[256,512]{1,0:T(8,128)(2,1)S(1)} %get-tuple-element.32.wh_ref, bf16[512,128]{1,0:T(8,128)(2,1)S(1)} %get-tuple-element.33.wf_ref, ...), custom_call_target="tpu_custom_call", output_to_operand_aliasing={{0}: (4, {}), {1}: (5, {})} | custom-call | flops 1711276032 | bytes 3342336 | tf_op jit(solution)/shard_map/pallas_call | solution.py:657
  43.6 8.8 %shard_map.86 = (f32[8,80,1024]{2,1,0:T(8,128)S(1)}, f32[2,8,640]{2,1,0:T(8,128)S(1)}) custom-call(bf16[12,1280,128]{2,1,0:T(8,128)(2,1)S(1)} %get-tuple-element.42.even_ref, bf16[12,1280,128]{2,1,0:T(8,128)(2,1)S(1)} %get-tuple-element.41.odd_ref, bf16[8,1024,128]{2,1,0:T(8,128)(2,1)} %pred_ref.5, bf16[2,1024,128]{2,1,0:T(8,128)(2,1)S(1)} %collective-permute-done.3.pup_ref, ...), custom_call_target="tpu_custom_call" | custom-call | flops 1342177280 | bytes 2097152 | tf_op jit(solution)/shard_map/pallas_call | solution.py:657
  52.4 0.0 collective-permute-done.2.down_ref
  52.4 5.0 %shard_map.87 = (f32[8,80,1024]{2,1,0:T(8,128)S(1)}, f32[2,8,1024]{2,1,0:T(8,128)S(1)}, bf16[12,896,128]{2,1,0:T(8,128)(2,1)S(1)}, bf16[4,1280,128]{2,1,0:T(8,128)(2,1)S(1)}) custom-call(bf16[12,1280,128]{2,1,0:T(8,128)(2,1)S(1)} %get-tuple-element.42.even_ref, ...), custom_call_target="tpu_custom_call", output_to_operand_aliasing={{0}: (5, {})} | custom-call | flops 1342177280 | bytes 2097152 | tf_op jit(solution)/shard_map/pallas_call | solution.py:657
  57.4 0.0 collective-permute-done.6.fup_ref
  57.4 4.8 %shard_map.88 = (bf16[12,896,128]{2,1,0:T(8,128)(2,1)S(1)}, f32[2,8,1024]{2,1,0:T(8,128)S(1)}) custom-call(bf16[12,1280,128]{2,1,0:T(8,128)(2,1)S(1)} %get-tuple-element.42.even_ref, bf16[12,896,128]{2,1,0:T(8,128)(2,1)S(1)} %get-tuple-element.51.ref_in, bf16[2,544,128]{2,1,0:T(8,128)(2,1)S(1)} %collective-permute-done.6.fup_ref, ...), custom_call_target="tpu_custom_call", output_to_operand_aliasing={{0}: (1, {})} | custom-call | flops 1342177280 | bytes 2097152 | tf_op jit(solution)/shard_map/pallas_call | solution.py:657
  62.2 0.0 copy-start.3
  62.2 5.3 %shard_map.89 = (f32[3,8,640]{2,1,0:T(8,128)S(1)}, bf16[512,128]{1,0:T(8,128)(2,1)S(1)}) custom-call(bf16[4512,128]{1,0:T(8,128)(2,1)S(1)} %collective-permute-done.back_ref, bf16[12,1280,128]{2,1,0:T(8,128)(2,1)S(1)} %get-tuple-element.41.odd_ref, bf16[4,1280,128]{2,1,0:T(8,128)(2,1)S(1)} %get-tuple-element.49.halo_ref, s32[2,8,1024]{2,1,0:T(8,128)S(1)} %copy-done.2, ...), custom_call_target="tpu_custom_call" | custom-call | flops 1476395008 | bytes 2306867 | tf_op jit(solution)/shard_map/pallas_call | solution.py:657
  67.6 1.9 %collective-permute-start.8 = (bf16[512,128]{1,0:T(8,128)(2,1)S(1)}, bf16[512,128]{1,0:T(8,128)(2,1)S(1)}, u32[]{:S(2)}, u32[]{:S(2)}) collective-permute-start(bf16[512,128]{1,0:T(8,128)(2,1)S(1)} %get-tuple-element.54), channel_id=1, source_target_pairs={{0,4},{4,8},{8,12},{12,16},{16,20},{20,24},{24,28},{1,5},{5,9},{9,... | collective-permute-start | bytes 393224 | tf_op jit(solution)/shard_map/ppermute | solution.py:32
  69.5 4.5 %collective-permute-start.9 = (bf16[512,128]{1,0:T(8,128)(2,1)S(1)}, bf16[512,128]{1,0:T(8,128)(2,1)S(1)}, u32[]{:S(2)}, u32[]{:S(2)}) collective-permute-start(bf16[512,128]{1,0:T(8,128)(2,1)S(1)} %get-tuple-element.54), channel_id=1, source_target_pairs={{4,0},{8,4},{12,8},{16,12},{20,16},{24,20},{28,24},{5,1},{9,5},{13... | collective-permute-start | bytes 393224 | tf_op jit(solution)/shard_map/ppermute | solution.py:32
  74.0 0.7 collective-permute-done.8.up_ref
  74.8 1.8 %collective-permute-done.9.down_ref = bf16[512,128]{1,0:T(8,128)(2,1)S(1)} collective-permute-done((bf16[512,128]{1,0:T(8,128)(2,1)S(1)}, bf16[512,128]{1,0:T(8,128)(2,1)S(1)}, u32[]{:S(2)}, u32[]{:S(2)}) %collective-permute-start.9) | collective-permute-done | bytes 131104 | tf_op jit(solution)/shard_map/ppermute | solution.py:32
  76.5 2.6 %relax.1 = (f32[2,8,1024]{2,1,0:T(8,128)S(1)}, f32[2,8,1024]{2,1,0:T(8,128)S(1)}, bf16[2,8,1024]{2,1,0:T(8,128)(2,1)S(1)}) custom-call(bf16[512,128]{1,0:T(8,128)(2,1)S(1)} %collective-permute-done.8.up_ref, bf16[512,128]{1,0:T(8,128)(2,1)S(1)} %collective-permute-done.9.down_ref, f32[2,8,1024]{2,1,0:T(8,128)S(1)} %get-tuple-element.50.flow1_ref, ...), custom_call_target="tpu_custom_call" | custom-call | flops 18874368 | bytes 327680 | tf_op jit(solution)/shard_map/relax/pallas_call | solution.py:752
  79.2 1.9 %collective-permute-start.12 = (bf16[2,8,1024]{2,1,0:T(8,128)(2,1)S(1)}, bf16[2,8,1024]{2,1,0:T(8,128)(2,1)S(1)}, u32[]{:S(2)}, u32[]{:S(2)}) collective-permute-start(bf16[2,8,1024]{2,1,0:T(8,128)(2,1)S(1)} %get-tuple-element.56), channel_id=1, source_target_pairs={{0,3},{4,7},{8,11},{12,15},{16,19},{20,23},{24,27},{28,31}} | collective-permute-start | bytes 98312 | tf_op jit(solution)/shard_map/ppermute | solution.py:32
  81.1 1.3 %collective-permute-start.11 = (bf16[2,8,1024]{2,1,0:T(8,128)(2,1)S(1)}, bf16[2,8,1024]{2,1,0:T(8,128)(2,1)S(1)}, u32[]{:S(2)}, u32[]{:S(2)}) collective-permute-start(bf16[2,8,1024]{2,1,0:T(8,128)(2,1)S(1)} %get-tuple-element.56), channel_id=1, source_target_pairs={{0,2},{1,3},{4,6},{5,7},{8,10},{9,11},{12,14},{13,15},{16,18},{17,... | collective-permute-start | bytes 98312 | tf_op jit(solution)/shard_map/ppermute | solution.py:32
  82.4 2.5 %collective-permute-start.10 = (bf16[2,8,1024]{2,1,0:T(8,128)(2,1)S(1)}, bf16[2,8,1024]{2,1,0:T(8,128)(2,1)S(1)}, u32[]{:S(2)}, u32[]{:S(2)}) collective-permute-start(bf16[2,8,1024]{2,1,0:T(8,128)(2,1)S(1)} %get-tuple-element.56), channel_id=1, source_target_pairs={{0,1},{1,2},{2,3},{4,5},{5,6},{6,7},{8,9},{9,10},{10,11},{12,13},{... | collective-permute-start | bytes 98312 | tf_op jit(solution)/shard_map/ppermute | solution.py:32
  84.9 1.6 %collective-permute-done.10 = bf16[2,8,1024]{2,1,0:T(8,128)(2,1)S(1)} collective-permute-done((bf16[2,8,1024]{2,1,0:T(8,128)(2,1)S(1)}, bf16[2,8,1024]{2,1,0:T(8,128)(2,1)S(1)}, u32[]{:S(2)}, u32[]{:S(2)}) %collective-permute-start.10) | collective-permute-done | bytes 32800 | tf_op jit(solution)/shard_map/ppermute | solution.py:32
  86.5 0.7 pad_maximum_fusion
  (14 shorter events, 0.1 us)
Async XLA Ops:
  0.0 8.5 %copy-start = (bf16[2,8,1024,256]{3,2,1,0:T(8,128)(2,1)S(1)}, bf16[2,8,1024,256]{3,2,1,0:T(8,128)(2,1)}, u32[]{:S(2)}) copy-start(bf16[2,8,1024,256]{3,2,1,0:T(8,128)(2,1)} %pix_ref.7) | copy-start | bytes 25165828
  0.0 8.5 %copy-start.1 = (s32[2,2,8,1024]{3,2,1,0:T(8,128)S(1)}, s32[2,2,8,1024]{3,2,1,0:T(8,128)}, u32[]{:S(2)}) copy-start(s32[2,2,8,1024]{3,2,1,0:T(8,128)} %off_ref.7) | copy-start | bytes 393220
  0.0 8.5 %copy-start.2 = (s32[2,8,1024]{2,1,0:T(8,128)S(1)}, s32[2,8,1024]{2,1,0:T(8,128)}, u32[]{:S(2)}) copy-start(s32[2,8,1024]{2,1,0:T(8,128)} %mask_ref.5) | copy-start | bytes 196612
  4.9 27.3 %collective-permute-start.5 = (bf16[8,544,128]{2,1,0:T(8,128)(2,1)S(1)}, bf16[8,544,128]{2,1,0:T(8,128)(2,1)S(1)}, u32[]{:S(2)}, u32[]{:S(2)}) collective-permute-start(bf16[8,544,128]{2,1,0:T(8,128)(2,1)S(1)} %get-tuple-element.48), channel_id=1, source_target_pairs={{0,1},{1,2},{2,3},{4,5},{5,6},{6,7},{8,9},{9,10},{10,11},{12,13},{... | collective-permute-start | bytes 3342344 | tf_op jit(solution)/shard_map/ppermute | solution.py:32
  13.9 48.3 %collective-permute-start = (bf16[4512,128]{1,0:T(8,128)(2,1)S(1)}, bf16[4512,128]{1,0:T(8,128)(2,1)S(1)}, u32[]{:S(2)}, u32[]{:S(2)}) collective-permute-start(bf16[4512,128]{1,0:T(8,128)(2,1)S(1)} %get-tuple-element.38), channel_id=1, source_target_pairs={{1,0},{2,1},{3,2},{5,4},{6,5},{7,6},{9,8},{10,9},{11,10},{13,12},{... | collective-permute-start | bytes 3465224 | tf_op jit(solution)/shard_map/ppermute | solution.py:32
  15.2 19.0 %collective-permute-start.3 = (bf16[2,1024,128]{2,1,0:T(8,128)(2,1)S(1)}, bf16[2,1024,128]{2,1,0:T(8,128)(2,1)S(1)}, u32[]{:S(2)}, u32[]{:S(2)}) collective-permute-start(bf16[2,1024,128]{2,1,0:T(8,128)(2,1)S(1)} %get-tuple-element.45), channel_id=1, source_target_pairs={{0,4},{4,8},{8,12},{12,16},{16,20},{20,24},{24,28}} | collective-permute-start | bytes 1572872 | tf_op jit(solution)/shard_map/ppermute | solution.py:39
  17.1 19.5 %collective-permute-start.4 = (bf16[2,1024,128]{2,1,0:T(8,128)(2,1)S(1)}, bf16[2,1024,128]{2,1,0:T(8,128)(2,1)S(1)}, u32[]{:S(2)}, u32[]{:S(2)}) collective-permute-start(bf16[2,1024,128]{2,1,0:T(8,128)(2,1)S(1)} %get-tuple-element.46), channel_id=1, source_target_pairs={{4,0},{8,4},{12,8},{16,12},{20,16},{24,20},{28,24}} | collective-permute-start | bytes 1572872 | tf_op jit(solution)/shard_map/ppermute | solution.py:39
  21.7 30.7 %collective-permute-start.1 = (bf16[2,1568,128]{2,1,0:T(8,128)(2,1)S(1)}, bf16[2,1568,128]{2,1,0:T(8,128)(2,1)S(1)}, u32[]{:S(2)}, u32[]{:S(2)}) collective-permute-start(bf16[2,1568,128]{2,1,0:T(8,128)(2,1)S(1)} %get-tuple-element.43), channel_id=1, source_target_pairs={{0,4},{4,8},{8,12},{12,16},{16,20},{20,24},{24,28},{1,5},{5,9},{9,... | collective-permute-start | bytes 2408456 | tf_op jit(solution)/shard_map/ppermute | solution.py:32
  32.2 20.1 %collective-permute-start.2 = (bf16[2,1568,128]{2,1,0:T(8,128)(2,1)S(1)}, bf16[2,1568,128]{2,1,0:T(8,128)(2,1)S(1)}, u32[]{:S(2)}, u32[]{:S(2)}) collective-permute-start(bf16[2,1568,128]{2,1,0:T(8,128)(2,1)S(1)} %get-tuple-element.44), channel_id=1, source_target_pairs={{4,0},{8,4},{12,8},{16,12},{20,16},{24,20},{28,24},{5,1},{9,5},{13... | collective-permute-start | bytes 2408456 | tf_op jit(solution)/shard_map/ppermute | solution.py:32
  34.2 23.2 %collective-permute-start.6 = (bf16[2,544,128]{2,1,0:T(8,128)(2,1)S(1)}, bf16[2,544,128]{2,1,0:T(8,128)(2,1)S(1)}, u32[]{:S(2)}, u32[]{:S(2)}) collective-permute-start(bf16[2,544,128]{2,1,0:T(8,128)(2,1)S(1)} %get-tuple-element.62), channel_id=1, source_target_pairs={{0,4},{4,8},{8,12},{12,16},{16,20},{20,24},{24,28},{1,5},{5,9},{9,... | collective-permute-start | bytes 835592 | tf_op jit(solution)/shard_map/ppermute | solution.py:32
  36.6 20.8 %collective-permute-start.7 = (bf16[2,544,128]{2,1,0:T(8,128)(2,1)S(1)}, bf16[2,544,128]{2,1,0:T(8,128)(2,1)S(1)}, u32[]{:S(2)}, u32[]{:S(2)}) collective-permute-start(bf16[2,544,128]{2,1,0:T(8,128)(2,1)S(1)} %get-tuple-element.61), channel_id=1, source_target_pairs={{4,0},{8,4},{12,8},{16,12},{20,16},{24,20},{28,24},{5,1},{9,5},{13... | collective-permute-start | bytes 835592 | tf_op jit(solution)/shard_map/ppermute | solution.py:32
  62.2 24.2 %copy-start.3 = (f32[2,8,1024]{2,1,0:T(8,128)S(1)}, f32[2,8,1024]{2,1,0:T(8,128)}, u32[]{:S(2)}) copy-start(f32[2,8,1024]{2,1,0:T(8,128)} %param.12) | copy-start | bytes 196612
  67.6 7.2 %collective-permute-start.8 = (bf16[512,128]{1,0:T(8,128)(2,1)S(1)}, bf16[512,128]{1,0:T(8,128)(2,1)S(1)}, u32[]{:S(2)}, u32[]{:S(2)}) collective-permute-start(bf16[512,128]{1,0:T(8,128)(2,1)S(1)} %get-tuple-element.54), channel_id=1, source_target_pairs={{0,4},{4,8},{8,12},{12,16},{16,20},{20,24},{24,28},{1,5},{5,9},{9,... | collective-permute-start | bytes 393224 | tf_op jit(solution)/shard_map/ppermute | solution.py:32
  69.5 7.0 %collective-permute-start.9 = (bf16[512,128]{1,0:T(8,128)(2,1)S(1)}, bf16[512,128]{1,0:T(8,128)(2,1)S(1)}, u32[]{:S(2)}, u32[]{:S(2)}) collective-permute-start(bf16[512,128]{1,0:T(8,128)(2,1)S(1)} %get-tuple-element.54), channel_id=1, source_target_pairs={{4,0},{8,4},{12,8},{16,12},{20,16},{24,20},{28,24},{5,1},{9,5},{13... | collective-permute-start | bytes 393224 | tf_op jit(solution)/shard_map/ppermute | solution.py:32
  79.2 5.7 %collective-permute-start.12 = (bf16[2,8,1024]{2,1,0:T(8,128)(2,1)S(1)}, bf16[2,8,1024]{2,1,0:T(8,128)(2,1)S(1)}, u32[]{:S(2)}, u32[]{:S(2)}) collective-permute-start(bf16[2,8,1024]{2,1,0:T(8,128)(2,1)S(1)} %get-tuple-element.56), channel_id=1, source_target_pairs={{0,3},{4,7},{8,11},{12,15},{16,19},{20,23},{24,27},{28,31}} | collective-permute-start | bytes 98312 | tf_op jit(solution)/shard_map/ppermute | solution.py:32
  81.1 3.8 %collective-permute-start.11 = (bf16[2,8,1024]{2,1,0:T(8,128)(2,1)S(1)}, bf16[2,8,1024]{2,1,0:T(8,128)(2,1)S(1)}, u32[]{:S(2)}, u32[]{:S(2)}) collective-permute-start(bf16[2,8,1024]{2,1,0:T(8,128)(2,1)S(1)} %get-tuple-element.56), channel_id=1, source_target_pairs={{0,2},{1,3},{4,6},{5,7},{8,10},{9,11},{12,14},{13,15},{16,18},{17,... | collective-permute-start | bytes 98312 | tf_op jit(solution)/shard_map/ppermute | solution.py:32
  82.4 4.1 %collective-permute-start.10 = (bf16[2,8,1024]{2,1,0:T(8,128)(2,1)S(1)}, bf16[2,8,1024]{2,1,0:T(8,128)(2,1)S(1)}, u32[]{:S(2)}, u32[]{:S(2)}) collective-permute-start(bf16[2,8,1024]{2,1,0:T(8,128)(2,1)S(1)} %get-tuple-element.56), channel_id=1, source_target_pairs={{0,1},{1,2},{2,3},{4,5},{5,6},{6,7},{8,9},{9,10},{10,11},{12,13},{... | collective-permute-start | bytes 98312 | tf_op jit(solution)/shard_map/ppermute | solution.py:32

commit v3 on v2

--- a/solution.py
+++ b/solution.py
@@ -32,11 +32,19 @@
     return lax.ppermute(value, axis, pairs)
 
 
-def hop_plane(value, steps):
+def swap(value, first, plane=False):
     tiles = lax.axis_size("tile")
-    secs = lax.axis_size("sec")
-    pairs = [(i * secs, (i + steps) * secs) for i in range(tiles) if 0 <= i + steps < tiles]
-    return lax.ppermute(value, ("tile", "sec"), pairs)
+    stride = lax.axis_size("sec") if plane else 1
+    pairs = []
+    for i in range(first, tiles - 1, 2):
+        pairs += [(i * stride, (i + 1) * stride), ((i + 1) * stride, i * stride)]
+    return lax.ppermute(value, ("tile", "sec") if plane else "tile", pairs)
+
+
+def sides(rows):
+    last = rows - REACH
+    facing = jnp.where(lax.rem(lax.axis_index("tile"), 2) == 0, last, 0)
+    return facing, last - facing
 
 
 def params(limit):
@@ -68,20 +76,14 @@
     finish(steps - 1)
 
 
-def border_rows(rows):
-    return list(range(REACH)) + list(range(rows - REACH, rows))
-
-
 def inner_rows(rows):
     return list(range(REACH, rows - REACH))
 
 
 def pieces_of(kind, rows, far):
-    border, inner = border_rows(rows), inner_rows(rows)
+    inner = inner_rows(rows)
     if kind == "front":
         return [(1, r, 0) for r in range(rows)]
-    if kind == "border":
-        return [(0, r, far) for r in border] + [(0, r, 0) for r in border] + [(1, r, far) for r in border]
     if kind == "back":
         return [(0, r, far) for r in inner]
     return [(0, r, 0) for r in inner] + [(1, r, far) for r in inner]
@@ -108,7 +110,7 @@
 
 def encode_front_kernel(
     half, pix_ref, wh_in, wf_in, gain_in, pred_ref,
-    front_ref, odd_ref, wh_ref, wf_ref, gain_ref, top_ref, bottom_ref,
+    front_ref, odd_ref, wh_ref, wf_ref, gain_ref, pred_a_ref, pred_b_ref,
     pix_s, pre_s, sem, more_sem,
 ):
     rows, cols = pix_ref.shape[1:3]
@@ -120,7 +122,8 @@
     ]
     copies = copies_of(loads, sem)
     constants = copies_of([(wh_in, wh_ref), (wf_in, wf_ref), (gain_in, gain_ref)], more_sem)
-    edges = [(pred_ref.at[0:REACH], top_ref), (pred_ref.at[rows - REACH : rows], bottom_ref)]
+    side_a, side_b = sides(rows)
+    edges = [(pred_ref.at[pl.ds(side_a, REACH)], pred_a_ref), (pred_ref.at[pl.ds(side_b, REACH)], pred_b_ref)]
     edge_sem = more_sem.at[len(constants) :]
     is_first = lax.axis_index("sec") == 0
     for copy in copies[:2] + constants + copies[2:4]:
@@ -154,12 +157,14 @@
 
 def encode_border_kernel(
     half, pix_ref, wh_ref, wf_ref, gain_ref, odd_in, off_ref, mask_ref,
-    odd_ref, even_ref, back_ref, up_ref, down_ref, pre_s,
+    odd_ref, even_ref, back_ref, pack_a_ref, pack_b_ref, pre_s,
 ):
     rows, cols = pix_ref.shape[1:3]
-    width = up_ref.shape[1] - cols
-    border = border_rows(rows)
-    pieces = pieces_of("border", rows, cols - width)
+    width = pack_a_ref.shape[1] - cols
+    side_a, side_b = sides(rows)
+    border = [side_a + r for r in range(REACH)] + [side_b + r for r in range(REACH)]
+    far = cols - width
+    pieces = [(0, r, far) for r in border] + [(0, r, 0) for r in border] + [(1, r, far) for r in border]
     zero_sides(even_ref, cols)
     first = half // LANES - 1
     for tile in range(cols // LANES - first):
@@ -173,9 +178,9 @@
     def store(n, value):
         part, m = divmod(n, len(border))
         row = border[m]
-        pack = down_ref if m < REACH else up_ref
+        pack = pack_a_ref if m < REACH else pack_b_ref
         if part == 0:
-            back_ref[row * width : (row + 1) * width, :] = value
+            back_ref[pl.ds(pl.multiple_of(row * width, 16), width), :] = value
             put_right(even_ref, row, value, half)
             pack[m % REACH, half:cols, :] = value[width - half :]
         elif part == 1:
@@ -390,8 +395,21 @@
         copy.wait()
 
 
+def pick_kernel(half, front_ref, a_ref, b_ref):
+    side_a, side_b = sides(front_ref.shape[0])
+    for r in range(REACH):
+        a_ref[r] = front_ref[side_a + r]
+        b_ref[r] = front_ref[side_b + r]
+
+
+def beyond_rows(rows):
+    side_a, side_b = sides(rows)
+    below = rows + REACH
+    return jnp.where(side_a > 0, below, 0), jnp.where(side_b > 0, below, 0)
+
+
 def near_scores_kernel(
-    half, even_ref, odd_ref, pred_ref, pup_ref, pdown_ref, off_ref,
+    half, even_ref, odd_ref, pred_ref, pred_a_ref, pred_b_ref, off_ref,
     s_s, flow0_ref, ref0_s, s0_s, m_s, sem,
 ):
     rows = odd_ref.shape[0] - 2 * REACH
@@ -401,10 +419,11 @@
     tile0 = half // LANES - 1
     tiles = cols // LANES - tile0
     to = slice(PAD + far, PAD + cols)
+    beyond_a, beyond_b = beyond_rows(rows)
     before = [
         (pred_ref.at[:, far:cols, :], ref0_s.at[REACH : rows + REACH, to, :]),
-        (pup_ref.at[:, far:cols, :], ref0_s.at[0:REACH, to, :]),
-        (pdown_ref.at[:, far:cols, :], ref0_s.at[rows + REACH : rows + 2 * REACH, to, :]),
+        (pred_a_ref.at[:, far:cols, :], ref0_s.at[pl.ds(beyond_a, REACH), to, :]),
+        (pred_b_ref.at[:, far:cols, :], ref0_s.at[pl.ds(beyond_b, REACH), to, :]),
     ]
 
     @pl.when(is_first)
@@ -427,7 +446,7 @@
 
 
 def own_scores_kernel(
-    half, even_ref, odd_ref, up_ref, down_ref, off_ref, s_in, front_ref, pred_ref,
+    half, even_ref, odd_ref, pack_a_ref, pack_b_ref, off_ref, s_in, front_ref, pred_ref,
     s_s, flow_ref, ref_next, halo_next, halo_s, m_s, sem, next_sem, ref_sem,
 ):
     rows = odd_ref.shape[0] - 2 * REACH
@@ -435,15 +454,18 @@
     width = front_ref.shape[1]
     far = cols - width
     is_first = lax.axis_index("sec") == 0
+    side_a, _ = sides(rows)
+    half_a = jnp.where(side_a > 0, REACH, 0)
+    half_b = REACH - half_a
     halos = [
-        (up_ref.at[:, 0:cols, :], halo_s.at[0:REACH, PAD : PAD + cols, :]),
-        (down_ref.at[:, 0:cols, :], halo_s.at[REACH : 2 * REACH, PAD : PAD + cols, :]),
+        (pack_a_ref.at[:, 0:cols, :], halo_s.at[pl.ds(half_a, REACH), PAD : PAD + cols, :]),
+        (pack_b_ref.at[:, 0:cols, :], halo_s.at[pl.ds(half_b, REACH), PAD : PAD + cols, :]),
     ]
     start_all(halos, sem)
     to = slice(PAD + far, PAD + cols)
     beyond = [
-        (up_ref.at[:, cols : cols + width, :], halo_next.at[0:REACH, to, :]),
-        (down_ref.at[:, cols : cols + width, :], halo_next.at[REACH : 2 * REACH, to, :]),
+        (pack_a_ref.at[:, cols : cols + width, :], halo_next.at[pl.ds(half_a, REACH), to, :]),
+        (pack_b_ref.at[:, cols : cols + width, :], halo_next.at[pl.ds(half_b, REACH), to, :]),
     ]
     start_all(beyond, next_sem)
     inside = ref_next.at[REACH : rows + REACH, PAD : PAD + width, :]
@@ -479,17 +501,18 @@
 
 
 def front_scores_kernel(
-    half, even_ref, ref_in, fup_ref, fdown_ref, pup_ref, pdown_ref, off_ref, flow0_ref,
+    half, even_ref, ref_in, front_a_ref, front_b_ref, pred_a_ref, pred_b_ref, off_ref, flow0_ref,
     ref_s, flow_ref, s_s, m_s, sem,
 ):
     rows = even_ref.shape[0] - 2 * REACH
     cols = 2 * half
-    width = fup_ref.shape[1]
+    width = front_a_ref.shape[1]
     is_first = lax.axis_index("sec") == 0
-    above = ref_s.at[0:REACH, PAD : PAD + width, :]
-    below = ref_s.at[rows + REACH : rows + 2 * REACH, PAD : PAD + width, :]
-    before = [(pup_ref.at[:, 0:width, :], above), (pdown_ref.at[:, 0:width, :], below)]
-    passed = [(fup_ref, above), (fdown_ref, below)]
+    beyond_a, beyond_b = beyond_rows(rows)
+    to_a = ref_s.at[pl.ds(beyond_a, REACH), PAD : PAD + width, :]
+    to_b = ref_s.at[pl.ds(beyond_b, REACH), PAD : PAD + width, :]
+    before = [(pred_a_ref.at[:, 0:width, :], to_a), (pred_b_ref.at[:, 0:width, :], to_b)]
+    passed = [(front_a_ref, to_a), (front_b_ref, to_b)]
 
     @pl.when(is_first)
     def _():
@@ -557,7 +580,7 @@
 
 
 def relax_kernel(
-    half, up_ref, down_ref, flow1_ref, flow3_ref, flow2_ref, mask_ref, f1_ref, f3_ref, msg_ref,
+    half, pack_a_ref, pack_b_ref, flow1_ref, flow3_ref, flow2_ref, mask_ref, f1_ref, f3_ref, msg_ref,
     field_s, pull_s, keep_s,
 ):
     rows, cols = flow1_ref.shape[1:]
@@ -565,6 +588,7 @@
     place = lax.axis_index("tile")
     count = lax.axis_size("tile")
     glob = place * rows + lax.broadcasted_iota(jnp.int32, (deep, LANES), 0) - ITERS
+    a_below = lax.rem(place, 2) == 0
     inside = ((glob >= 0) & (glob < rows * count)).astype(F32)
     widths = (cols, cols, flow2_ref.shape[2])
     tiles = [w // LANES for w in widths]
@@ -579,10 +603,12 @@
             m_at = mask_at + 8 * (starts[job] + k)
             half_at = m_at // 16 * 16
             sub = slice(m_at - half_at, m_at - half_at + 8)
-            upper = up_ref[at : at + 16, :].astype(F32)
-            lower = down_ref[at : at + 16, :].astype(F32)
-            m_up = up_ref[half_at : half_at + 16, :].astype(F32)[sub]
-            m_down = down_ref[half_at : half_at + 16, :].astype(F32)[sub]
+            side_a = pack_a_ref[at : at + 16, :].astype(F32)
+            side_b = pack_b_ref[at : at + 16, :].astype(F32)
+            m_a = pack_a_ref[half_at : half_at + 16, :].astype(F32)[sub]
+            m_b = pack_b_ref[half_at : half_at + 16, :].astype(F32)[sub]
+            upper, lower = jnp.where(a_below, side_b, side_a), jnp.where(a_below, side_a, side_b)
+            m_up, m_down = jnp.where(a_below, m_b, m_a), jnp.where(a_below, m_a, m_b)
             weight = stiffness * jnp.concatenate(
                 [m_up, own_masks[job][:, lanes].astype(F32), m_down], 0
             )
@@ -672,7 +698,7 @@
         return pltpu.with_memory_space_constraint(value, pltpu.HBM)
 
     edges = shape((REACH, cols, feat), BF16)
-    front, odd, wh, wf, gain, top, bottom = call(
+    front, odd, wh, wf, gain, pred_a, pred_b = call(
         encode_front_kernel,
         (in_place(pixels), in_place(w_hidden), in_place(w_feature), in_place(gain), in_place(pred)), [HBM] * 5,
         (
@@ -684,17 +710,17 @@
     )
     weights = (pixels, wh, wf, gain)
     front_in = hop(front, "sec", 1)
-    pup = hop_plane(bottom, 1)
-    pdown = hop_plane(top, -1)
+    pred_a = swap(pred_a, 0, True)
+    pred_b = swap(pred_b, 1, True)
     pack = shape((REACH, cols + width, feat), BF16)
-    odd, even, back, up, down = call(
+    odd, even, back, pack_a, pack_b = call(
         encode_border_kernel,
         (*weights, odd, offsets, mask), [VMEM] * 7,
         (padded, padded, shape((rows * width + tail, feat), BF16), pack, pack),
-        [pre], encode_cost("border"), 10, {4: 0},
-    )
-    up_in = hop(up, "tile", 1)
-    down_in = hop(down, "tile", -1)
+        [pre], flops_of(6 * REACH * width, patch, hid, feat), 10, {4: 0},
+    )
+    pack_b = swap(pack_b, 1)
+    pack_a = swap(pack_a, 0)
     even, back = call(
         encode_back_kernel, (*weights, even, back), [VMEM] * 6,
         (padded, shape(back.shape, BF16)), [pre], encode_cost("back"), 10, {4: 0, 5: 1},
@@ -719,21 +745,26 @@
     whole = pltpu.VMEM((deep, full, feat), BF16)
     flow0_shape = shape((2, rows, span), F32)
     scores, flow0 = call(
-        near_scores_kernel, (even, odd, in_place(pred), pup, pdown, offsets),
+        near_scores_kernel, (even, odd, in_place(pred), pred_a, pred_b, offsets),
         [VMEM] * 2 + [HBM] + [VMEM] * 3, (shape((rows, bands, cols), F32), flow0_shape),
         [whole, pltpu.VMEM((rows, bands, span), F32), turning4, dma((3,))], score_cost(0.5), 18,
     )
-    fup_in = hop(front_in[rows - REACH :], "tile", 1)
-    fdown_in = hop(front_in[:REACH], "tile", -1)
+    edge = shape((REACH, width, feat), BF16)
+    front_a, front_b = call(
+        pick_kernel, (front_in,), [VMEM], (edge, edge), [],
+        pl.CostEstimate(flops=0, bytes_accessed=8 * REACH * width * feat, transcendentals=0), 4,
+    )
+    front_b = swap(front_b, 1)
+    front_a = swap(front_a, 0)
     ref_shape = shape((deep, half + 3 * PAD, feat), BF16)
     _, flow1, ref, beyond = call(
-        own_scores_kernel, (even, odd, up_in, down_in, offsets, scores, front_in, in_place(pred)),
+        own_scores_kernel, (even, odd, pack_a, pack_b, offsets, scores, front_in, in_place(pred)),
         [VMEM] * 7 + [HBM],
         (shape(scores.shape, F32), shape((2, rows, cols), F32), ref_shape, shape((2 * REACH, full, feat), BF16)),
         [halo, turning4, dma((2,)), dma((2,)), dma((1,))], score_cost(0.5), 14, {5: 0},
     )
     _, flow3 = call(
-        front_scores_kernel, (even, ref, fup_in, fdown_in, pup, pdown, offsets, flow0),
+        front_scores_kernel, (even, ref, front_a, front_b, pred_a, pred_b, offsets, flow0),
         [VMEM] * 8, (ref_shape, shape((2, rows, cols), F32)),
         [pltpu.VMEM((rows, bands, half), F32), turning, dma((2,))], score_cost(0.5), 12, {1: 0},
     )
@@ -745,8 +776,8 @@
         (shape((3, rows, span), F32), shape((pack_rows, LANES), BF16)),
         [pltpu.VMEM((rows, bands, span), F32), turning], score_cost(0.55), 12,
     )
-    pack_up = hop(pack, "tile", 1)
-    pack_down = hop(pack, "tile", -1)
+    flows_b = swap(pack, 1)
+    flows_a = swap(pack, 0)
 
     wide = rows + 2 * ITERS
     f1, f3, msg = pl.pallas_call(
@@ -762,7 +793,7 @@
         compiler_params=params(12),
         cost_estimate=pl.CostEstimate(flops=nodes * 24 * 12 * 8, bytes_accessed=nodes * 40, transcendentals=0),
         name="relax",
-    )(pack_up, pack_down, flow1, flow3, flow2, mask)
+    )(flows_a, flows_b, flow1, flow3, flow2, mask)
 
     prefix = base_shift
     for steps in range(1, lax.axis_size("sec")):

time: 88.7 us -> 93.8 us (1.057)
  waiting for transfers between devices: 12.7 us -> 23 us
  starting transfers between devices: 33.9 us -> 29.3 us
    ppermute x11 -> x5, starting transfers between devices: 27.5 us -> 15.1 us  [hop(): return lax.ppermute(value, axis, pairs)]
    ppermute x2 -> x8, waiting for transfers between devices: 0.01 us -> 9.97 us  [swap(): return lax.ppermute(value, ('tile', 'sec') if plane else 'tile', pairs)]
    ppermute x2 -> x8, starting transfers between devices: 6.46 us -> 14.2 us  [swap(): return lax.ppermute(value, ('tile', 'sec') if plane else 'tile', pairs)]
    ppermute x11 -> x5, waiting for transfers between devices: 12.7 us -> 13.1 us  [hop(): return lax.ppermute(value, axis, pairs)]
    pallas_call x8 -> x9, Pallas kernels: 36.9 us -> 36.9 us  [call(): pl.pallas_call(functools.partial(kernel, half), out_shape=outs, in_specs=...]
  transfers between devices with their start and end apart: 13 -> 13, of which waited for: 4 -> 5; matrix products, arithmetic and copies ran while one was open for 0% -> 0% of each run, Pallas kernels for 31% -> 29%
where the time goes in v3:
time: 93.8 us; the launch traced here: 92.8 us
  Pallas kernels  39.5 us (42%)
  starting transfers between devices  29.3 us (31%)
  waiting for transfers between devices  23 us (25%)
    pallas_call x9, Pallas kernels, call(): pl.pallas_call(functools.partial(kernel, half), out_shape=outs, in_specs=...  36.9 us
    ppermute x5, starting transfers between devices, hop(): return lax.ppermute(value, axis, pairs)  15.1 us
    ppermute x8, starting transfers between devices, swap(): return lax.ppermute(value, ('tile', 'sec') if plane else 'tile', pairs)  14.2 us
    ppermute x5, waiting for transfers between devices, hop(): return lax.ppermute(value, axis, pairs)  13.1 us
    ppermute x8, waiting for transfers between devices, swap(): return lax.ppermute(value, ('tile', 'sec') if plane else 'tile', pairs)  9.97 us
    pallas_call x1, Pallas kernels, shards(): pl.pallas_call(functools.partial(relax_kernel, half), out_shape=(shape((2...  2.61 us
  transfers between devices with their start and end apart: 13, of which 5 were waited for; matrix products, arithmetic and copies ran while one was open for 0% of the time, Pallas kernels for 29%

profile of v3, /device:TPU:4, one launch (start us, length us, event | category | flops | bytes accessed | tf_op | source)
XLA Modules:
  0.0 92.8 jit_solution(1041410834355615324)
XLA Ops:
  0.0 4.9 %shard_map.82 = (bf16[8,544,128]{2,1,0:T(8,128)(2,1)S(1)}, bf16[12,1280,128]{2,1,0:T(8,128)(2,1)S(1)}, bf16[256,512]{1,0:T(8,128)(2,1)S(1)}, bf16[512,128]{1,0:T...) custom-call(bf16[2,8,1024,256]{3,2,1,0:T(8,128)(2,1)} %pix_ref.7, ...), custom_call_target="tpu_custom_call" | custom-call | flops 1711276032 | bytes 3342336 | tf_op jit(solution)/shard_map/pallas_call | solution.py:683
  4.9 3.5 %collective-permute-start.5 = (bf16[8,544,128]{2,1,0:T(8,128)(2,1)S(1)}, bf16[8,544,128]{2,1,0:T(8,128)(2,1)S(1)}, u32[]{:S(2)}, u32[]{:S(2)}) collective-permute-start(bf16[8,544,128]{2,1,0:T(8,128)(2,1)S(1)} %get-tuple-element.50), channel_id=1, source_target_pairs={{0,1},{1,2},{2,3},{4,5},{5,6},{6,7},{8,9},{9,10},{10,11},{12,13},{... | collective-permute-start | bytes 3342344 | tf_op jit(solution)/shard_map/ppermute | solution.py:32
  8.5 3.8 %shard_map.83 = (bf16[12,1280,128]{2,1,0:T(8,128)(2,1)S(1)}, bf16[12,1280,128]{2,1,0:T(8,128)(2,1)S(1)}, bf16[4512,128]{1,0:T(8,128)(2,1)S(1)}, bf16[2,1568,128]...) custom-call(bf16[2,8,1024,256]{3,2,1,0:T(8,128)(2,1)S(1)} %copy-done, ...), custom_call_target="tpu_custom_call", output_to_operand_aliasing={{0}: (4, {})} | custom-call | flops 2566914048 | bytes 5013504 | tf_op jit(solution)/shard_map/pallas_call | solution.py:683
  12.4 1.5 %shard_map.84 = (bf16[12,1280,128]{2,1,0:T(8,128)(2,1)S(1)}, bf16[4512,128]{1,0:T(8,128)(2,1)S(1)}) custom-call(bf16[2,8,1024,256]{3,2,1,0:T(8,128)(2,1)S(1)} %copy-done, bf16[256,512]{1,0:T(8,128)(2,1)S(1)} %get-tuple-element.34.wh_ref, bf16[512,128]{1,0:T(8,128)(2,1)S(1)} %get-tuple-element.35.wf_ref, ...), custom_call_target="tpu_custom_call", output_to_operand_aliasing={{0}: (4, {}), {1}: (5, {})} | custom-call | flops 855638016 | bytes 1671168 | tf_op jit(solution)/shard_map/pallas_call | solution.py:683
  13.9 1.3 %collective-permute-start = (bf16[4512,128]{1,0:T(8,128)(2,1)S(1)}, bf16[4512,128]{1,0:T(8,128)(2,1)S(1)}, u32[]{:S(2)}, u32[]{:S(2)}) collective-permute-start(bf16[4512,128]{1,0:T(8,128)(2,1)S(1)} %get-tuple-element.40), channel_id=1, source_target_pairs={{1,0},{2,1},{3,2},{5,4},{6,5},{7,6},{9,8},{10,9},{11,10},{13,12},{... | collective-permute-start | bytes 3465224 | tf_op jit(solution)/shard_map/ppermute | solution.py:32
  15.2 1.9 %collective-permute-start.3 = (bf16[2,1024,128]{2,1,0:T(8,128)(2,1)S(1)}, bf16[2,1024,128]{2,1,0:T(8,128)(2,1)S(1)}, u32[]{:S(2)}, u32[]{:S(2)}) collective-permute-start(bf16[2,1024,128]{2,1,0:T(8,128)(2,1)S(1)} %get-tuple-element.47), channel_id=1, source_target_pairs={{0,4},{4,0},{8,12},{12,8},{16,20},{20,16},{24,28},{28,24}} | collective-permute-start | bytes 1572872 | tf_op jit(solution)/shard_map/ppermute | solution.py:41
  17.1 3.4 %collective-permute-start.4 = (bf16[2,1024,128]{2,1,0:T(8,128)(2,1)S(1)}, bf16[2,1024,128]{2,1,0:T(8,128)(2,1)S(1)}, u32[]{:S(2)}, u32[]{:S(2)}) collective-permute-start(bf16[2,1024,128]{2,1,0:T(8,128)(2,1)S(1)} %get-tuple-element.48), channel_id=1, source_target_pairs={{4,8},{8,4},{12,16},{16,12},{20,24},{24,20}} | collective-permute-start | bytes 1572872 | tf_op jit(solution)/shard_map/ppermute | solution.py:41
  20.6 0.1 collective-permute-start.1
  20.7 11.5 %collective-permute-done.5.front_ref = bf16[8,544,128]{2,1,0:T(8,128)(2,1)S(1)} collective-permute-done((bf16[8,544,128]{2,1,0:T(8,128)(2,1)S(1)}, bf16[8,544,128]{2,1,0:T(8,128)(2,1)S(1)}, u32[]{:S(2)}, u32[]{:S(2)}) %collective-permute-start.5) | collective-permute-done | bytes 1114144 | tf_op jit(solution)/shard_map/ppermute | solution.py:32
  32.2 1.9 %collective-permute-start.2 = (bf16[2,1568,128]{2,1,0:T(8,128)(2,1)S(1)}, bf16[2,1568,128]{2,1,0:T(8,128)(2,1)S(1)}, u32[]{:S(2)}, u32[]{:S(2)}) collective-permute-start(bf16[2,1568,128]{2,1,0:T(8,128)(2,1)S(1)} %get-tuple-element.46), channel_id=1, source_target_pairs={{4,8},{8,4},{12,16},{16,12},{20,24},{24,20},{5,9},{9,5},{13,17},{1... | collective-permute-start | bytes 2408456 | tf_op jit(solution)/shard_map/ppermute | solution.py:41
  34.2 0.1 shard_map.88
  34.2 0.0 collective-permute-done.3.pred_a_ref
  34.2 1.7 %collective-permute-start.6 = (bf16[2,544,128]{2,1,0:T(8,128)(2,1)S(1)}, bf16[2,544,128]{2,1,0:T(8,128)(2,1)S(1)}, u32[]{:S(2)}, u32[]{:S(2)}) collective-permute-start(bf16[2,544,128]{2,1,0:T(8,128)(2,1)S(1)} %get-tuple-element.54), channel_id=1, source_target_pairs={{0,4},{4,0},{8,12},{12,8},{16,20},{20,16},{24,28},{28,24},{1,5},{5... | collective-permute-start | bytes 835592 | tf_op jit(solution)/shard_map/ppermute | solution.py:41
  35.9 0.0 collective-permute-done.4.pred_b_ref
  35.9 3.1 %collective-permute-start.7 = (bf16[2,544,128]{2,1,0:T(8,128)(2,1)S(1)}, bf16[2,544,128]{2,1,0:T(8,128)(2,1)S(1)}, u32[]{:S(2)}, u32[]{:S(2)}) collective-permute-start(bf16[2,544,128]{2,1,0:T(8,128)(2,1)S(1)} %get-tuple-element.55), channel_id=1, source_target_pairs={{4,8},{8,4},{12,16},{16,12},{20,24},{24,20},{5,9},{9,5},{13,17},{1... | collective-permute-start | bytes 835592 | tf_op jit(solution)/shard_map/ppermute | solution.py:41
  39.0 2.7 %shard_map.85 = (bf16[12,1280,128]{2,1,0:T(8,128)(2,1)S(1)}, bf16[12,1280,128]{2,1,0:T(8,128)(2,1)S(1)}) custom-call(bf16[2,8,1024,256]{3,2,1,0:T(8,128)(2,1)S(1)} %copy-done, bf16[256,512]{1,0:T(8,128)(2,1)S(1)} %get-tuple-element.34.wh_ref, bf16[512,128]{1,0:T(8,128)(2,1)S(1)} %get-tuple-element.35.wf_ref, ...), custom_call_target="tpu_custom_call", output_to_operand_aliasing={{0}: (4, {}), {1}: (5, {})} | custom-call | flops 1711276032 | bytes 3342336 | tf_op jit(solution)/shard_map/pallas_call | solution.py:683
  41.7 8.8 %shard_map.86 = (f32[8,80,1024]{2,1,0:T(8,128)S(1)}, f32[2,8,640]{2,1,0:T(8,128)S(1)}) custom-call(bf16[12,1280,128]{2,1,0:T(8,128)(2,1)S(1)} %get-tuple-element.44.even_ref, bf16[12,1280,128]{2,1,0:T(8,128)(2,1)S(1)} %get-tuple-element.43.odd_ref, bf16[8,1024,128]{2,1,0:T(8,128)(2,1)} %pred_ref.5, ...), custom_call_target="tpu_custom_call" | custom-call | flops 1342177280 | bytes 2097152 | tf_op jit(solution)/shard_map/pallas_call | solution.py:683
  50.5 4.7 %collective-permute-done.2.pack_b_ref = bf16[2,1568,128]{2,1,0:T(8,128)(2,1)S(1)} collective-permute-done((bf16[2,1568,128]{2,1,0:T(8,128)(2,1)S(1)}, bf16[2,1568,128]{2,1,0:T(8,128)(2,1)S(1)}, u32[]{:S(2)}, u32[]{:S(2)}) %collective-permute-start.2) | collective-permute-done | bytes 802848 | tf_op jit(solution)/shard_map/ppermute | solution.py:41
  55.2 5.0 %shard_map.87 = (f32[8,80,1024]{2,1,0:T(8,128)S(1)}, f32[2,8,1024]{2,1,0:T(8,128)S(1)}, bf16[12,896,128]{2,1,0:T(8,128)(2,1)S(1)}, bf16[4,1280,128]{2,1,0:T(8,128)(2,1)S(1)}) custom-call(bf16[12,1280,128]{2,1,0:T(8,128)(2,1)S(1)} %get-tuple-element.44.even_ref, ...), custom_call_target="tpu_custom_call", output_to_operand_aliasing={{0}: (5, {})} | custom-call | flops 1342177280 | bytes 2097152 | tf_op jit(solution)/shard_map/pallas_call | solution.py:683
  60.2 0.1 collective-permute-done.7.front_b_ref
  60.3 4.8 %shard_map.89 = (bf16[12,896,128]{2,1,0:T(8,128)(2,1)S(1)}, f32[2,8,1024]{2,1,0:T(8,128)S(1)}) custom-call(bf16[12,1280,128]{2,1,0:T(8,128)(2,1)S(1)} %get-tuple-element.44.even_ref, bf16[12,896,128]{2,1,0:T(8,128)(2,1)S(1)} %get-tuple-element.53.ref_in, ...), custom_call_target="tpu_custom_call", output_to_operand_aliasing={{0}: (1, {})} | custom-call | flops 1342177280 | bytes 2097152 | tf_op jit(solution)/shard_map/pallas_call | solution.py:683
  65.1 0.0 copy-start.3
  65.1 5.3 %shard_map.90 = (f32[3,8,640]{2,1,0:T(8,128)S(1)}, bf16[512,128]{1,0:T(8,128)(2,1)S(1)}) custom-call(bf16[4512,128]{1,0:T(8,128)(2,1)S(1)} %collective-permute-done.back_ref, bf16[12,1280,128]{2,1,0:T(8,128)(2,1)S(1)} %get-tuple-element.43.odd_ref, bf16[4,1280,128]{2,1,0:T(8,128)(2,1)S(1)} %get-tuple-element.51.halo_ref, s32[2,8,1024]{2,1,0:T(8,128)S(1)} %copy-done.2, ...), custom_call_target="tpu_custom_call" | custom-call | flops 1476395008 | bytes 2306867 | tf_op jit(solution)/shard_map/pallas_call | solution.py:683
  70.4 0.1 collective-permute-start.8
  70.5 1.9 %collective-permute-start.9 = (bf16[512,128]{1,0:T(8,128)(2,1)S(1)}, bf16[512,128]{1,0:T(8,128)(2,1)S(1)}, u32[]{:S(2)}, u32[]{:S(2)}) collective-permute-start(bf16[512,128]{1,0:T(8,128)(2,1)S(1)} %get-tuple-element.58), channel_id=1, source_target_pairs={{4,8},{8,4},{12,16},{16,12},{20,24},{24,20},{5,9},{9,5},{13,17},{1... | collective-permute-start | bytes 393224 | tf_op jit(solution)/shard_map/ppermute | solution.py:41
  72.4 5.2 %collective-permute-done.9.pack_b_ref = bf16[512,128]{1,0:T(8,128)(2,1)S(1)} collective-permute-done((bf16[512,128]{1,0:T(8,128)(2,1)S(1)}, bf16[512,128]{1,0:T(8,128)(2,1)S(1)}, u32[]{:S(2)}, u32[]{:S(2)}) %collective-permute-start.9) | collective-permute-done | bytes 131104 | tf_op jit(solution)/shard_map/ppermute | solution.py:41
  77.7 2.6 %relax.1 = (f32[2,8,1024]{2,1,0:T(8,128)S(1)}, f32[2,8,1024]{2,1,0:T(8,128)S(1)}, bf16[2,8,1024]{2,1,0:T(8,128)(2,1)S(1)}) custom-call(bf16[512,128]{1,0:T(8,128)(2,1)S(1)} %collective-permute-done.8.pack_a_ref, bf16[512,128]{1,0:T(8,128)(2,1)S(1)} %collective-permute-done.9.pack_b_ref, f32[2,8,1024]{2,1,0:T(8,128)S(1)} %get-tuple-element.52.flow1_ref, ...), custom_call_target="tpu_custom_call" | custom-call | flops 18874368 | bytes 327680 | tf_op jit(solution)/shard_map/relax/pallas_call | solution.py:783
  80.3 6.5 %collective-permute-start.12 = (bf16[2,8,1024]{2,1,0:T(8,128)(2,1)S(1)}, bf16[2,8,1024]{2,1,0:T(8,128)(2,1)S(1)}, u32[]{:S(2)}, u32[]{:S(2)}) collective-permute-start(bf16[2,8,1024]{2,1,0:T(8,128)(2,1)S(1)} %get-tuple-element.60), channel_id=1, source_target_pairs={{0,3},{4,7},{8,11},{12,15},{16,19},{20,23},{24,27},{28,31}} | collective-permute-start | bytes 98312 | tf_op jit(solution)/shard_map/ppermute | solution.py:32
  86.8 1.3 %collective-permute-start.11 = (bf16[2,8,1024]{2,1,0:T(8,128)(2,1)S(1)}, bf16[2,8,1024]{2,1,0:T(8,128)(2,1)S(1)}, u32[]{:S(2)}, u32[]{:S(2)}) collective-permute-start(bf16[2,8,1024]{2,1,0:T(8,128)(2,1)S(1)} %get-tuple-element.60), channel_id=1, source_target_pairs={{0,2},{1,3},{4,6},{5,7},{8,10},{9,11},{12,14},{13,15},{16,18},{17,... | collective-permute-start | bytes 98312 | tf_op jit(solution)/shard_map/ppermute | solution.py:32
  88.1 2.5 %collective-permute-start.10 = (bf16[2,8,1024]{2,1,0:T(8,128)(2,1)S(1)}, bf16[2,8,1024]{2,1,0:T(8,128)(2,1)S(1)}, u32[]{:S(2)}, u32[]{:S(2)}) collective-permute-start(bf16[2,8,1024]{2,1,0:T(8,128)(2,1)S(1)} %get-tuple-element.60), channel_id=1, source_target_pairs={{0,1},{1,2},{2,3},{4,5},{5,6},{6,7},{8,9},{9,10},{10,11},{12,13},{... | collective-permute-start | bytes 98312 | tf_op jit(solution)/shard_map/ppermute | solution.py:32
  90.6 1.6 %collective-permute-done.10 = bf16[2,8,1024]{2,1,0:T(8,128)(2,1)S(1)} collective-permute-done((bf16[2,8,1024]{2,1,0:T(8,128)(2,1)S(1)}, bf16[2,8,1024]{2,1,0:T(8,128)(2,1)S(1)}, u32[]{:S(2)}, u32[]{:S(2)}) %collective-permute-start.10) | collective-permute-done | bytes 32800 | tf_op jit(solution)/shard_map/ppermute | solution.py:32
  92.1 0.7 pad_maximum_fusion
  (14 shorter events, 0.1 us)
Async XLA Ops:
  0.0 8.5 %copy-start = (bf16[2,8,1024,256]{3,2,1,0:T(8,128)(2,1)S(1)}, bf16[2,8,1024,256]{3,2,1,0:T(8,128)(2,1)}, u32[]{:S(2)}) copy-start(bf16[2,8,1024,256]{3,2,1,0:T(8,128)(2,1)} %pix_ref.7) | copy-start | bytes 25165828
  0.0 8.5 %copy-start.1 = (s32[2,2,8,1024]{3,2,1,0:T(8,128)S(1)}, s32[2,2,8,1024]{3,2,1,0:T(8,128)}, u32[]{:S(2)}) copy-start(s32[2,2,8,1024]{3,2,1,0:T(8,128)} %off_ref.7) | copy-start | bytes 393220
  0.0 8.5 %copy-start.2 = (s32[2,8,1024]{2,1,0:T(8,128)S(1)}, s32[2,8,1024]{2,1,0:T(8,128)}, u32[]{:S(2)}) copy-start(s32[2,8,1024]{2,1,0:T(8,128)} %mask_ref.5) | copy-start | bytes 196612
  4.9 27.3 %collective-permute-start.5 = (bf16[8,544,128]{2,1,0:T(8,128)(2,1)S(1)}, bf16[8,544,128]{2,1,0:T(8,128)(2,1)S(1)}, u32[]{:S(2)}, u32[]{:S(2)}) collective-permute-start(bf16[8,544,128]{2,1,0:T(8,128)(2,1)S(1)} %get-tuple-element.50), channel_id=1, source_target_pairs={{0,1},{1,2},{2,3},{4,5},{5,6},{6,7},{8,9},{9,10},{10,11},{12,13},{... | collective-permute-start | bytes 3342344 | tf_op jit(solution)/shard_map/ppermute | solution.py:32
  13.9 51.2 %collective-permute-start = (bf16[4512,128]{1,0:T(8,128)(2,1)S(1)}, bf16[4512,128]{1,0:T(8,128)(2,1)S(1)}, u32[]{:S(2)}, u32[]{:S(2)}) collective-permute-start(bf16[4512,128]{1,0:T(8,128)(2,1)S(1)} %get-tuple-element.40), channel_id=1, source_target_pairs={{1,0},{2,1},{3,2},{5,4},{6,5},{7,6},{9,8},{10,9},{11,10},{13,12},{... | collective-permute-start | bytes 3465224 | tf_op jit(solution)/shard_map/ppermute | solution.py:32
  15.2 19.0 %collective-permute-start.3 = (bf16[2,1024,128]{2,1,0:T(8,128)(2,1)S(1)}, bf16[2,1024,128]{2,1,0:T(8,128)(2,1)S(1)}, u32[]{:S(2)}, u32[]{:S(2)}) collective-permute-start(bf16[2,1024,128]{2,1,0:T(8,128)(2,1)S(1)} %get-tuple-element.47), channel_id=1, source_target_pairs={{0,4},{4,0},{8,12},{12,8},{16,20},{20,16},{24,28},{28,24}} | collective-permute-start | bytes 1572872 | tf_op jit(solution)/shard_map/ppermute | solution.py:41
  17.1 18.8 %collective-permute-start.4 = (bf16[2,1024,128]{2,1,0:T(8,128)(2,1)S(1)}, bf16[2,1024,128]{2,1,0:T(8,128)(2,1)S(1)}, u32[]{:S(2)}, u32[]{:S(2)}) collective-permute-start(bf16[2,1024,128]{2,1,0:T(8,128)(2,1)S(1)} %get-tuple-element.48), channel_id=1, source_target_pairs={{4,8},{8,4},{12,16},{16,12},{20,24},{24,20}} | collective-permute-start | bytes 1572872 | tf_op jit(solution)/shard_map/ppermute | solution.py:41
  20.6 29.9 %collective-permute-start.1 = (bf16[2,1568,128]{2,1,0:T(8,128)(2,1)S(1)}, bf16[2,1568,128]{2,1,0:T(8,128)(2,1)S(1)}, u32[]{:S(2)}, u32[]{:S(2)}) collective-permute-start(bf16[2,1568,128]{2,1,0:T(8,128)(2,1)S(1)} %get-tuple-element.45), channel_id=1, source_target_pairs={{0,4},{4,0},{8,12},{12,8},{16,20},{20,16},{24,28},{28,24},{1,5},{5... | collective-permute-start | bytes 2408456 | tf_op jit(solution)/shard_map/ppermute | solution.py:41
  32.2 23.0 %collective-permute-start.2 = (bf16[2,1568,128]{2,1,0:T(8,128)(2,1)S(1)}, bf16[2,1568,128]{2,1,0:T(8,128)(2,1)S(1)}, u32[]{:S(2)}, u32[]{:S(2)}) collective-permute-start(bf16[2,1568,128]{2,1,0:T(8,128)(2,1)S(1)} %get-tuple-element.46), channel_id=1, source_target_pairs={{4,8},{8,4},{12,16},{16,12},{20,24},{24,20},{5,9},{9,5},{13,17},{1... | collective-permute-start | bytes 2408456 | tf_op jit(solution)/shard_map/ppermute | solution.py:41
  34.2 26.0 %collective-permute-start.6 = (bf16[2,544,128]{2,1,0:T(8,128)(2,1)S(1)}, bf16[2,544,128]{2,1,0:T(8,128)(2,1)S(1)}, u32[]{:S(2)}, u32[]{:S(2)}) collective-permute-start(bf16[2,544,128]{2,1,0:T(8,128)(2,1)S(1)} %get-tuple-element.54), channel_id=1, source_target_pairs={{0,4},{4,0},{8,12},{12,8},{16,20},{20,16},{24,28},{28,24},{1,5},{5... | collective-permute-start | bytes 835592 | tf_op jit(solution)/shard_map/ppermute | solution.py:41
  35.9 24.4 %collective-permute-start.7 = (bf16[2,544,128]{2,1,0:T(8,128)(2,1)S(1)}, bf16[2,544,128]{2,1,0:T(8,128)(2,1)S(1)}, u32[]{:S(2)}, u32[]{:S(2)}) collective-permute-start(bf16[2,544,128]{2,1,0:T(8,128)(2,1)S(1)} %get-tuple-element.55), channel_id=1, source_target_pairs={{4,8},{8,4},{12,16},{16,12},{20,24},{24,20},{5,9},{9,5},{13,17},{1... | collective-permute-start | bytes 835592 | tf_op jit(solution)/shard_map/ppermute | solution.py:41
  65.1 27.0 %copy-start.3 = (f32[2,8,1024]{2,1,0:T(8,128)S(1)}, f32[2,8,1024]{2,1,0:T(8,128)}, u32[]{:S(2)}) copy-start(f32[2,8,1024]{2,1,0:T(8,128)} %param.12) | copy-start | bytes 196612
  70.4 2.0 %collective-permute-start.8 = (bf16[512,128]{1,0:T(8,128)(2,1)S(1)}, bf16[512,128]{1,0:T(8,128)(2,1)S(1)}, u32[]{:S(2)}, u32[]{:S(2)}) collective-permute-start(bf16[512,128]{1,0:T(8,128)(2,1)S(1)} %get-tuple-element.58), channel_id=1, source_target_pairs={{0,4},{4,0},{8,12},{12,8},{16,20},{20,16},{24,28},{28,24},{1,5},{5... | collective-permute-start | bytes 393224 | tf_op jit(solution)/shard_map/ppermute | solution.py:41
  70.5 7.2 %collective-permute-start.9 = (bf16[512,128]{1,0:T(8,128)(2,1)S(1)}, bf16[512,128]{1,0:T(8,128)(2,1)S(1)}, u32[]{:S(2)}, u32[]{:S(2)}) collective-permute-start(bf16[512,128]{1,0:T(8,128)(2,1)S(1)} %get-tuple-element.58), channel_id=1, source_target_pairs={{4,8},{8,4},{12,16},{16,12},{20,24},{24,20},{5,9},{9,5},{13,17},{1... | collective-permute-start | bytes 393224 | tf_op jit(solution)/shard_map/ppermute | solution.py:41
  80.3 10.2 %collective-permute-start.12 = (bf16[2,8,1024]{2,1,0:T(8,128)(2,1)S(1)}, bf16[2,8,1024]{2,1,0:T(8,128)(2,1)S(1)}, u32[]{:S(2)}, u32[]{:S(2)}) collective-permute-start(bf16[2,8,1024]{2,1,0:T(8,128)(2,1)S(1)} %get-tuple-element.60), channel_id=1, source_target_pairs={{0,3},{4,7},{8,11},{12,15},{16,19},{20,23},{24,27},{28,31}} | collective-permute-start | bytes 98312 | tf_op jit(solution)/shard_map/ppermute | solution.py:32
  86.8 3.8 %collective-permute-start.11 = (bf16[2,8,1024]{2,1,0:T(8,128)(2,1)S(1)}, bf16[2,8,1024]{2,1,0:T(8,128)(2,1)S(1)}, u32[]{:S(2)}, u32[]{:S(2)}) collective-permute-start(bf16[2,8,1024]{2,1,0:T(8,128)(2,1)S(1)} %get-tuple-element.60), channel_id=1, source_target_pairs={{0,2},{1,3},{4,6},{5,7},{8,10},{9,11},{12,14},{13,15},{16,18},{17,... | collective-permute-start | bytes 98312 | tf_op jit(solution)/shard_map/ppermute | solution.py:32
  88.1 4.1 %collective-permute-start.10 = (bf16[2,8,1024]{2,1,0:T(8,128)(2,1)S(1)}, bf16[2,8,1024]{2,1,0:T(8,128)(2,1)S(1)}, u32[]{:S(2)}, u32[]{:S(2)}) collective-permute-start(bf16[2,8,1024]{2,1,0:T(8,128)(2,1)S(1)} %get-tuple-element.60), channel_id=1, source_target_pairs={{0,1},{1,2},{2,3},{4,5},{5,6},{6,7},{8,9},{9,10},{10,11},{12,13},{... | collective-permute-start | bytes 98312 | tf_op jit(solution)/shard_map/ppermute | solution.py:32

commit v4 on v3

--- a/solution.py
+++ b/solution.py
@@ -84,8 +84,6 @@
     inner = inner_rows(rows)
     if kind == "front":
         return [(1, r, 0) for r in range(rows)]
-    if kind == "back":
-        return [(0, r, far) for r in inner]
     return [(0, r, 0) for r in inner] + [(1, r, far) for r in inner]
 
 
@@ -114,7 +112,8 @@
     pix_s, pre_s, sem, more_sem,
 ):
     rows, cols = pix_ref.shape[1:3]
-    width = front_ref.shape[1]
+    width = pix_s.shape[1]
+    lean = front_ref.shape[1]
     pieces = pieces_of("front", rows, cols - width)
     loads = [
         (pix_ref.at[sec, row, col0 : col0 + width, :], pix_s.at[n])
@@ -145,7 +144,7 @@
         return pix_s[n : n + 2].reshape(2 * width, pix_s.shape[2])
 
     def store(n, value):
-        front_ref[n] = value
+        front_ref[n] = value[:lean]
         put_left(odd_ref, n, value, half)
 
     encode_steps(pix_of, len(pieces), width, store, wh_ref, wf_ref, gain_ref, pre_s)
@@ -164,7 +163,10 @@
     side_a, side_b = sides(rows)
     border = [side_a + r for r in range(REACH)] + [side_b + r for r in range(REACH)]
     far = cols - width
+    lean = width - EDGE
+    inner = inner_rows(rows)
     pieces = [(0, r, far) for r in border] + [(0, r, 0) for r in border] + [(1, r, far) for r in border]
+    pieces += [(0, r, far) for r in inner]
     zero_sides(even_ref, cols)
     first = half // LANES - 1
     for tile in range(cols // LANES - first):
@@ -172,15 +174,18 @@
         extra = jnp.concatenate(
             [off_ref[0, 0, :, lanes], off_ref[0, 1, :, lanes], mask_ref[0, :, lanes], mask_ref[0, :, lanes]], 0
         )
-        at = rows * width + tile * 4 * rows
+        at = rows * lean + tile * 4 * rows
         back_ref[at : at + 4 * rows, :] = extra.astype(F32).astype(BF16)
 
     def store(n, value):
         part, m = divmod(n, len(border))
-        row = border[m]
+        row = border[m] if part < 3 else inner[n - 3 * len(border)]
         pack = pack_a_ref if m < REACH else pack_b_ref
-        if part == 0:
-            back_ref[pl.ds(pl.multiple_of(row * width, 16), width), :] = value
+        if part == 0 or part > 2:
+            back_ref[pl.ds(pl.multiple_of(row * lean, 16), lean), :] = value[EDGE:]
+        if part > 2:
+            put_right(even_ref, row, value, half)
+        elif part == 0:
             put_right(even_ref, row, value, half)
             pack[m % REACH, half:cols, :] = value[width - half :]
         elif part == 1:
@@ -189,21 +194,6 @@
         else:
             put_right(odd_ref, row, value, half)
             pack[m % REACH, cols : cols + width, :] = value
-
-    encode_steps(
-        lambda n: pixel_pair(pix_ref, pieces, n, width), len(pieces), width, store, wh_ref, wf_ref, gain_ref, pre_s
-    )
-
-
-def encode_back_kernel(half, pix_ref, wh_ref, wf_ref, gain_ref, even_in, back_in, even_ref, back_ref, pre_s):
-    rows, cols = pix_ref.shape[1:3]
-    width = pre_s.shape[1] // 2
-    inner = inner_rows(rows)
-    pieces = pieces_of("back", rows, cols - width)
-
-    def store(n, value):
-        back_ref[inner[n] * width : (inner[n] + 1) * width, :] = value
-        put_right(even_ref, inner[n], value, half)
 
     encode_steps(
         lambda n: pixel_pair(pix_ref, pieces, n, width), len(pieces), width, store, wh_ref, wf_ref, gain_ref, pre_s
@@ -451,7 +441,8 @@
 ):
     rows = odd_ref.shape[0] - 2 * REACH
     cols = 2 * half
-    width = front_ref.shape[1]
+    width = pack_a_ref.shape[1] - cols
+    lean = front_ref.shape[1]
     far = cols - width
     is_first = lax.axis_index("sec") == 0
     side_a, _ = sides(rows)
@@ -468,8 +459,9 @@
         (pack_b_ref.at[:, cols : cols + width, :], halo_next.at[pl.ds(half_b, REACH), to, :]),
     ]
     start_all(beyond, next_sem)
-    inside = ref_next.at[REACH : rows + REACH, PAD : PAD + width, :]
-    before = [(pred_ref.at[:, 0:width, :], inside)]
+    left = slice(PAD, PAD + lean)
+    inside = ref_next.at[REACH : rows + REACH, left, :]
+    before = [(pred_ref.at[:, 0:lean, :], inside)]
     passed = [(front_ref, inside)]
 
     @pl.when(is_first)
@@ -668,6 +660,7 @@
     assert secs == 2 and rows == ITERS and feat == LANES and cols % (2 * LANES) == 0
     half = cols // 2
     width = half + 2 * EDGE
+    lean = width - EDGE
     span = half + LANES
     deep = rows + 2 * REACH
     tail = 4 * rows * (span // LANES)
@@ -702,7 +695,7 @@
         encode_front_kernel,
         (in_place(pixels), in_place(w_hidden), in_place(w_feature), in_place(gain), in_place(pred)), [HBM] * 5,
         (
-            shape((rows, width, feat), BF16), padded,
+            shape((rows, lean, feat), BF16), padded,
             shape(w_hidden.shape, BF16), shape(w_feature.shape, BF16), shape(gain.shape, F32), edges, edges,
         ),
         [pltpu.VMEM((rows, width, patch), BF16), pre, dma((rows,)), dma((5,))],
@@ -716,15 +709,11 @@
     odd, even, back, pack_a, pack_b = call(
         encode_border_kernel,
         (*weights, odd, offsets, mask), [VMEM] * 7,
-        (padded, padded, shape((rows * width + tail, feat), BF16), pack, pack),
-        [pre], flops_of(6 * REACH * width, patch, hid, feat), 10, {4: 0},
+        (padded, padded, shape((rows * lean + tail, feat), BF16), pack, pack),
+        [pre], flops_of((rows + 4 * REACH) * width, patch, hid, feat), 10, {4: 0},
     )
     pack_b = swap(pack_b, 1)
     pack_a = swap(pack_a, 0)
-    even, back = call(
-        encode_back_kernel, (*weights, even, back), [VMEM] * 6,
-        (padded, shape(back.shape, BF16)), [pre], encode_cost("back"), 10, {4: 0, 5: 1},
-    )
     back_in = hop(back, "sec", -1)
     odd, even = call(
         encode_inner_kernel, (*weights, odd, even), [VMEM] * 6,
@@ -749,7 +738,7 @@
         [VMEM] * 2 + [HBM] + [VMEM] * 3, (shape((rows, bands, cols), F32), flow0_shape),
         [whole, pltpu.VMEM((rows, bands, span), F32), turning4, dma((3,))], score_cost(0.5), 18,
     )
-    edge = shape((REACH, width, feat), BF16)
+    edge = shape((REACH, lean, feat), BF16)
     front_a, front_b = call(
         pick_kernel, (front_in,), [VMEM], (edge, edge), [],
         pl.CostEstimate(flops=0, bytes_accessed=8 * REACH * width * feat, transcendentals=0), 4,

time: 93.8 us -> 92.9 us (level)
    pallas_call x9 -> x8, Pallas kernels: 36.9 us -> 36.5 us  [call(): pl.pallas_call(functools.partial(kernel, half), out_shape=outs, in_specs=...]
  transfers between devices with their start and end apart: 13 -> 13, of which waited for: 5 -> 4; matrix products, arithmetic and copies ran while one was open for 0% -> 0% of each run, Pallas kernels for 29% -> 29%
where the time goes in v4:
time: 92.9 us; the launch traced here: 91.9 us
  Pallas kernels  39.1 us (42%)
  starting transfers between devices  29.1 us (31%)
  waiting for transfers between devices  22.7 us (24%)
    pallas_call x8, Pallas kernels, call(): pl.pallas_call(functools.partial(kernel, half), out_shape=outs, in_specs=...  36.5 us
    ppermute x5, starting transfers between devices, hop(): return lax.ppermute(value, axis, pairs)  15.1 us
    ppermute x8, starting transfers between devices, swap(): return lax.ppermute(value, ('tile', 'sec') if plane else 'tile', pairs)  14 us
    ppermute x5, waiting for transfers between devices, hop(): return lax.ppermute(value, axis, pairs)  12.7 us
    ppermute x8, waiting for transfers between devices, swap(): return lax.ppermute(value, ('tile', 'sec') if plane else 'tile', pairs)  9.94 us
    pallas_call x1, Pallas kernels, shards(): pl.pallas_call(functools.partial(relax_kernel, half), out_shape=(shape((2...  2.61 us
  transfers between devices with their start and end apart: 13, of which 4 were waited for; matrix products, arithmetic and copies ran while one was open for 0% of the time, Pallas kernels for 29%

profile of v4, /device:TPU:4, one launch (start us, length us, event | category | flops | bytes accessed | tf_op | source)
XLA Modules:
  0.0 91.9 jit_solution(9292384448441758590)
XLA Ops:
  0.0 4.9 %shard_map.82 = (bf16[8,528,128]{2,1,0:T(8,128)(2,1)S(1)}, bf16[12,1280,128]{2,1,0:T(8,128)(2,1)S(1)}, bf16[256,512]{1,0:T(8,128)(2,1)S(1)}, bf16[512,128]{1,0:T...) custom-call(bf16[2,8,1024,256]{3,2,1,0:T(8,128)(2,1)} %pix_ref.5, ...), custom_call_target="tpu_custom_call" | custom-call | flops 1711276032 | bytes 3342336 | tf_op jit(solution)/shard_map/pallas_call | solution.py:676
  4.9 3.5 %collective-permute-start.5 = (bf16[8,528,128]{2,1,0:T(8,128)(2,1)S(1)}, bf16[8,528,128]{2,1,0:T(8,128)(2,1)S(1)}, u32[]{:S(2)}, u32[]{:S(2)}) collective-permute-start(bf16[8,528,128]{2,1,0:T(8,128)(2,1)S(1)} %get-tuple-element.46), channel_id=1, source_target_pairs={{0,1},{1,2},{2,3},{4,5},{5,6},{6,7},{8,9},{9,10},{10,11},{12,13},{... | collective-permute-start | bytes 3244040 | tf_op jit(solution)/shard_map/ppermute | solution.py:32
  8.5 5.0 %shard_map.83 = (bf16[12,1280,128]{2,1,0:T(8,128)(2,1)S(1)}, bf16[12,1280,128]{2,1,0:T(8,128)(2,1)S(1)}, bf16[4384,128]{1,0:T(8,128)(2,1)S(1)}, bf16[2,1568,128]...) custom-call(bf16[2,8,1024,256]{3,2,1,0:T(8,128)(2,1)S(1)} %copy-done, ...), custom_call_target="tpu_custom_call", output_to_operand_aliasing={{0}: (4, {})} | custom-call | flops 3422552064 | bytes 6684672 | tf_op jit(solution)/shard_map/pallas_call | solution.py:676
  13.5 1.3 %collective-permute-start = (bf16[4384,128]{1,0:T(8,128)(2,1)S(1)}, bf16[4384,128]{1,0:T(8,128)(2,1)S(1)}, u32[]{:S(2)}, u32[]{:S(2)}) collective-permute-start(bf16[4384,128]{1,0:T(8,128)(2,1)S(1)} %get-tuple-element.36), channel_id=1, source_target_pairs={{1,0},{2,1},{3,2},{5,4},{6,5},{7,6},{9,8},{10,9},{11,10},{13,12},{... | collective-permute-start | bytes 3366920 | tf_op jit(solution)/shard_map/ppermute | solution.py:32
  14.8 1.9 %collective-permute-start.3 = (bf16[2,1024,128]{2,1,0:T(8,128)(2,1)S(1)}, bf16[2,1024,128]{2,1,0:T(8,128)(2,1)S(1)}, u32[]{:S(2)}, u32[]{:S(2)}) collective-permute-start(bf16[2,1024,128]{2,1,0:T(8,128)(2,1)S(1)} %get-tuple-element.43), channel_id=1, source_target_pairs={{0,4},{4,0},{8,12},{12,8},{16,20},{20,16},{24,28},{28,24}} | collective-permute-start | bytes 1572872 | tf_op jit(solution)/shard_map/ppermute | solution.py:41
  16.8 3.4 %collective-permute-start.4 = (bf16[2,1024,128]{2,1,0:T(8,128)(2,1)S(1)}, bf16[2,1024,128]{2,1,0:T(8,128)(2,1)S(1)}, u32[]{:S(2)}, u32[]{:S(2)}) collective-permute-start(bf16[2,1024,128]{2,1,0:T(8,128)(2,1)S(1)} %get-tuple-element.44), channel_id=1, source_target_pairs={{4,8},{8,4},{12,16},{16,12},{20,24},{24,20}} | collective-permute-start | bytes 1572872 | tf_op jit(solution)/shard_map/ppermute | solution.py:41
  20.2 0.1 collective-permute-start.1
  20.3 11.2 %collective-permute-done.5.front_ref = bf16[8,528,128]{2,1,0:T(8,128)(2,1)S(1)} collective-permute-done((bf16[8,528,128]{2,1,0:T(8,128)(2,1)S(1)}, bf16[8,528,128]{2,1,0:T(8,128)(2,1)S(1)}, u32[]{:S(2)}, u32[]{:S(2)}) %collective-permute-start.5) | collective-permute-done | bytes 1081376 | tf_op jit(solution)/shard_map/ppermute | solution.py:32
  31.5 1.9 %collective-permute-start.2 = (bf16[2,1568,128]{2,1,0:T(8,128)(2,1)S(1)}, bf16[2,1568,128]{2,1,0:T(8,128)(2,1)S(1)}, u32[]{:S(2)}, u32[]{:S(2)}) collective-permute-start(bf16[2,1568,128]{2,1,0:T(8,128)(2,1)S(1)} %get-tuple-element.42), channel_id=1, source_target_pairs={{4,8},{8,4},{12,16},{16,12},{20,24},{24,20},{5,9},{9,5},{13,17},{1... | collective-permute-start | bytes 2408456 | tf_op jit(solution)/shard_map/ppermute | solution.py:41
  33.5 0.1 shard_map.87
  33.5 0.0 collective-permute-done.3.pred_a_ref
  33.5 1.7 %collective-permute-start.6 = (bf16[2,528,128]{2,1,0:T(8,128)(2,1)S(1)}, bf16[2,528,128]{2,1,0:T(8,128)(2,1)S(1)}, u32[]{:S(2)}, u32[]{:S(2)}) collective-permute-start(bf16[2,528,128]{2,1,0:T(8,128)(2,1)S(1)} %get-tuple-element.50), channel_id=1, source_target_pairs={{0,4},{4,0},{8,12},{12,8},{16,20},{20,16},{24,28},{28,24},{1,5},{5... | collective-permute-start | bytes 811016 | tf_op jit(solution)/shard_map/ppermute | solution.py:41
  35.2 0.0 collective-permute-done.4.pred_b_ref
  35.2 3.0 %collective-permute-start.7 = (bf16[2,528,128]{2,1,0:T(8,128)(2,1)S(1)}, bf16[2,528,128]{2,1,0:T(8,128)(2,1)S(1)}, u32[]{:S(2)}, u32[]{:S(2)}) collective-permute-start(bf16[2,528,128]{2,1,0:T(8,128)(2,1)S(1)} %get-tuple-element.51), channel_id=1, source_target_pairs={{4,8},{8,4},{12,16},{16,12},{20,24},{24,20},{5,9},{9,5},{13,17},{1... | collective-permute-start | bytes 811016 | tf_op jit(solution)/shard_map/ppermute | solution.py:41
  38.2 2.7 %shard_map.84 = (bf16[12,1280,128]{2,1,0:T(8,128)(2,1)S(1)}, bf16[12,1280,128]{2,1,0:T(8,128)(2,1)S(1)}) custom-call(bf16[2,8,1024,256]{3,2,1,0:T(8,128)(2,1)S(1)} %copy-done, bf16[256,512]{1,0:T(8,128)(2,1)S(1)} %get-tuple-element.32.wh_ref, bf16[512,128]{1,0:T(8,128)(2,1)S(1)} %get-tuple-element.33.wf_ref, ...), custom_call_target="tpu_custom_call", output_to_operand_aliasing={{0}: (4, {}), {1}: (5, {})} | custom-call | flops 1711276032 | bytes 3342336 | tf_op jit(solution)/shard_map/pallas_call | solution.py:676
  40.8 9.0 %shard_map.85 = (f32[8,80,1024]{2,1,0:T(8,128)S(1)}, f32[2,8,640]{2,1,0:T(8,128)S(1)}) custom-call(bf16[12,1280,128]{2,1,0:T(8,128)(2,1)S(1)} %get-tuple-element.40.even_ref, bf16[12,1280,128]{2,1,0:T(8,128)(2,1)S(1)} %get-tuple-element.39.odd_ref, bf16[8,1024,128]{2,1,0:T(8,128)(2,1)} %pred_ref.5, ...), custom_call_target="tpu_custom_call" | custom-call | flops 1342177280 | bytes 2097152 | tf_op jit(solution)/shard_map/pallas_call | solution.py:676
  49.8 4.7 %collective-permute-done.2.pack_b_ref = bf16[2,1568,128]{2,1,0:T(8,128)(2,1)S(1)} collective-permute-done((bf16[2,1568,128]{2,1,0:T(8,128)(2,1)S(1)}, bf16[2,1568,128]{2,1,0:T(8,128)(2,1)S(1)}, u32[]{:S(2)}, u32[]{:S(2)}) %collective-permute-start.2) | collective-permute-done | bytes 802848 | tf_op jit(solution)/shard_map/ppermute | solution.py:41
  54.5 5.0 %shard_map.86 = (f32[8,80,1024]{2,1,0:T(8,128)S(1)}, f32[2,8,1024]{2,1,0:T(8,128)S(1)}, bf16[12,896,128]{2,1,0:T(8,128)(2,1)S(1)}, bf16[4,1280,128]{2,1,0:T(8,128)(2,1)S(1)}) custom-call(bf16[12,1280,128]{2,1,0:T(8,128)(2,1)S(1)} %get-tuple-element.40.even_ref, ...), custom_call_target="tpu_custom_call", output_to_operand_aliasing={{0}: (5, {})} | custom-call | flops 1342177280 | bytes 2097152 | tf_op jit(solution)/shard_map/pallas_call | solution.py:676
  59.5 0.0 collective-permute-done.6.front_a_ref
  59.5 4.6 %shard_map.88 = (bf16[12,896,128]{2,1,0:T(8,128)(2,1)S(1)}, f32[2,8,1024]{2,1,0:T(8,128)S(1)}) custom-call(bf16[12,1280,128]{2,1,0:T(8,128)(2,1)S(1)} %get-tuple-element.40.even_ref, bf16[12,896,128]{2,1,0:T(8,128)(2,1)S(1)} %get-tuple-element.49.ref_in, ...), custom_call_target="tpu_custom_call", output_to_operand_aliasing={{0}: (1, {})} | custom-call | flops 1342177280 | bytes 2097152 | tf_op jit(solution)/shard_map/pallas_call | solution.py:676
  64.1 0.0 copy-start.3
  64.1 5.3 %shard_map.89 = (f32[3,8,640]{2,1,0:T(8,128)S(1)}, bf16[512,128]{1,0:T(8,128)(2,1)S(1)}) custom-call(bf16[4384,128]{1,0:T(8,128)(2,1)S(1)} %collective-permute-done.back_ref, bf16[12,1280,128]{2,1,0:T(8,128)(2,1)S(1)} %get-tuple-element.39.odd_ref, bf16[4,1280,128]{2,1,0:T(8,128)(2,1)S(1)} %get-tuple-element.47.halo_ref, s32[2,8,1024]{2,1,0:T(8,128)S(1)} %copy-done.2, ...), custom_call_target="tpu_custom_call" | custom-call | flops 1476395008 | bytes 2306867 | tf_op jit(solution)/shard_map/pallas_call | solution.py:676
  69.4 0.1 collective-permute-start.8
  69.5 1.9 %collective-permute-start.9 = (bf16[512,128]{1,0:T(8,128)(2,1)S(1)}, bf16[512,128]{1,0:T(8,128)(2,1)S(1)}, u32[]{:S(2)}, u32[]{:S(2)}) collective-permute-start(bf16[512,128]{1,0:T(8,128)(2,1)S(1)} %get-tuple-element.54), channel_id=1, source_target_pairs={{4,8},{8,4},{12,16},{16,12},{20,24},{24,20},{5,9},{9,5},{13,17},{1... | collective-permute-start | bytes 393224 | tf_op jit(solution)/shard_map/ppermute | solution.py:41
  71.5 5.2 %collective-permute-done.9.pack_b_ref = bf16[512,128]{1,0:T(8,128)(2,1)S(1)} collective-permute-done((bf16[512,128]{1,0:T(8,128)(2,1)S(1)}, bf16[512,128]{1,0:T(8,128)(2,1)S(1)}, u32[]{:S(2)}, u32[]{:S(2)}) %collective-permute-start.9) | collective-permute-done | bytes 131104 | tf_op jit(solution)/shard_map/ppermute | solution.py:41
  76.7 2.6 %relax.1 = (f32[2,8,1024]{2,1,0:T(8,128)S(1)}, f32[2,8,1024]{2,1,0:T(8,128)S(1)}, bf16[2,8,1024]{2,1,0:T(8,128)(2,1)S(1)}) custom-call(bf16[512,128]{1,0:T(8,128)(2,1)S(1)} %collective-permute-done.8.pack_a_ref, bf16[512,128]{1,0:T(8,128)(2,1)S(1)} %collective-permute-done.9.pack_b_ref, f32[2,8,1024]{2,1,0:T(8,128)S(1)} %get-tuple-element.48.flow1_ref, ...), custom_call_target="tpu_custom_call" | custom-call | flops 18874368 | bytes 327680 | tf_op jit(solution)/shard_map/relax/pallas_call | solution.py:772
  79.3 6.5 %collective-permute-start.12 = (bf16[2,8,1024]{2,1,0:T(8,128)(2,1)S(1)}, bf16[2,8,1024]{2,1,0:T(8,128)(2,1)S(1)}, u32[]{:S(2)}, u32[]{:S(2)}) collective-permute-start(bf16[2,8,1024]{2,1,0:T(8,128)(2,1)S(1)} %get-tuple-element.56), channel_id=1, source_target_pairs={{0,3},{4,7},{8,11},{12,15},{16,19},{20,23},{24,27},{28,31}} | collective-permute-start | bytes 98312 | tf_op jit(solution)/shard_map/ppermute | solution.py:32
  85.8 1.3 %collective-permute-start.11 = (bf16[2,8,1024]{2,1,0:T(8,128)(2,1)S(1)}, bf16[2,8,1024]{2,1,0:T(8,128)(2,1)S(1)}, u32[]{:S(2)}, u32[]{:S(2)}) collective-permute-start(bf16[2,8,1024]{2,1,0:T(8,128)(2,1)S(1)} %get-tuple-element.56), channel_id=1, source_target_pairs={{0,2},{1,3},{4,6},{5,7},{8,10},{9,11},{12,14},{13,15},{16,18},{17,... | collective-permute-start | bytes 98312 | tf_op jit(solution)/shard_map/ppermute | solution.py:32
  87.1 2.5 %collective-permute-start.10 = (bf16[2,8,1024]{2,1,0:T(8,128)(2,1)S(1)}, bf16[2,8,1024]{2,1,0:T(8,128)(2,1)S(1)}, u32[]{:S(2)}, u32[]{:S(2)}) collective-permute-start(bf16[2,8,1024]{2,1,0:T(8,128)(2,1)S(1)} %get-tuple-element.56), channel_id=1, source_target_pairs={{0,1},{1,2},{2,3},{4,5},{5,6},{6,7},{8,9},{9,10},{10,11},{12,13},{... | collective-permute-start | bytes 98312 | tf_op jit(solution)/shard_map/ppermute | solution.py:32
  89.6 0.0 collective-permute-done.12
  89.6 1.6 %collective-permute-done.10 = bf16[2,8,1024]{2,1,0:T(8,128)(2,1)S(1)} collective-permute-done((bf16[2,8,1024]{2,1,0:T(8,128)(2,1)S(1)}, bf16[2,8,1024]{2,1,0:T(8,128)(2,1)S(1)}, u32[]{:S(2)}, u32[]{:S(2)}) %collective-permute-start.10) | collective-permute-done | bytes 32800 | tf_op jit(solution)/shard_map/ppermute | solution.py:32
  91.2 0.7 pad_maximum_fusion
  (13 shorter events, 0.1 us)
Async XLA Ops:
  0.0 8.5 %copy-start = (bf16[2,8,1024,256]{3,2,1,0:T(8,128)(2,1)S(1)}, bf16[2,8,1024,256]{3,2,1,0:T(8,128)(2,1)}, u32[]{:S(2)}) copy-start(bf16[2,8,1024,256]{3,2,1,0:T(8,128)(2,1)} %pix_ref.5) | copy-start | bytes 25165828
  0.0 8.5 %copy-start.1 = (s32[2,2,8,1024]{3,2,1,0:T(8,128)S(1)}, s32[2,2,8,1024]{3,2,1,0:T(8,128)}, u32[]{:S(2)}) copy-start(s32[2,2,8,1024]{3,2,1,0:T(8,128)} %off_ref.7) | copy-start | bytes 393220
  0.0 8.5 %copy-start.2 = (s32[2,8,1024]{2,1,0:T(8,128)S(1)}, s32[2,8,1024]{2,1,0:T(8,128)}, u32[]{:S(2)}) copy-start(s32[2,8,1024]{2,1,0:T(8,128)} %mask_ref.5) | copy-start | bytes 196612
  4.9 26.6 %collective-permute-start.5 = (bf16[8,528,128]{2,1,0:T(8,128)(2,1)S(1)}, bf16[8,528,128]{2,1,0:T(8,128)(2,1)S(1)}, u32[]{:S(2)}, u32[]{:S(2)}) collective-permute-start(bf16[8,528,128]{2,1,0:T(8,128)(2,1)S(1)} %get-tuple-element.46), channel_id=1, source_target_pairs={{0,1},{1,2},{2,3},{4,5},{5,6},{6,7},{8,9},{9,10},{10,11},{12,13},{... | collective-permute-start | bytes 3244040 | tf_op jit(solution)/shard_map/ppermute | solution.py:32
  13.5 50.6 %collective-permute-start = (bf16[4384,128]{1,0:T(8,128)(2,1)S(1)}, bf16[4384,128]{1,0:T(8,128)(2,1)S(1)}, u32[]{:S(2)}, u32[]{:S(2)}) collective-permute-start(bf16[4384,128]{1,0:T(8,128)(2,1)S(1)} %get-tuple-element.36), channel_id=1, source_target_pairs={{1,0},{2,1},{3,2},{5,4},{6,5},{7,6},{9,8},{10,9},{11,10},{13,12},{... | collective-permute-start | bytes 3366920 | tf_op jit(solution)/shard_map/ppermute | solution.py:32
  14.8 18.7 %collective-permute-start.3 = (bf16[2,1024,128]{2,1,0:T(8,128)(2,1)S(1)}, bf16[2,1024,128]{2,1,0:T(8,128)(2,1)S(1)}, u32[]{:S(2)}, u32[]{:S(2)}) collective-permute-start(bf16[2,1024,128]{2,1,0:T(8,128)(2,1)S(1)} %get-tuple-element.43), channel_id=1, source_target_pairs={{0,4},{4,0},{8,12},{12,8},{16,20},{20,16},{24,28},{28,24}} | collective-permute-start | bytes 1572872 | tf_op jit(solution)/shard_map/ppermute | solution.py:41
  16.8 18.4 %collective-permute-start.4 = (bf16[2,1024,128]{2,1,0:T(8,128)(2,1)S(1)}, bf16[2,1024,128]{2,1,0:T(8,128)(2,1)S(1)}, u32[]{:S(2)}, u32[]{:S(2)}) collective-permute-start(bf16[2,1024,128]{2,1,0:T(8,128)(2,1)S(1)} %get-tuple-element.44), channel_id=1, source_target_pairs={{4,8},{8,4},{12,16},{16,12},{20,24},{24,20}} | collective-permute-start | bytes 1572872 | tf_op jit(solution)/shard_map/ppermute | solution.py:41
  20.2 29.6 %collective-permute-start.1 = (bf16[2,1568,128]{2,1,0:T(8,128)(2,1)S(1)}, bf16[2,1568,128]{2,1,0:T(8,128)(2,1)S(1)}, u32[]{:S(2)}, u32[]{:S(2)}) collective-permute-start(bf16[2,1568,128]{2,1,0:T(8,128)(2,1)S(1)} %get-tuple-element.41), channel_id=1, source_target_pairs={{0,4},{4,0},{8,12},{12,8},{16,20},{20,16},{24,28},{28,24},{1,5},{5... | collective-permute-start | bytes 2408456 | tf_op jit(solution)/shard_map/ppermute | solution.py:41
  31.5 23.0 %collective-permute-start.2 = (bf16[2,1568,128]{2,1,0:T(8,128)(2,1)S(1)}, bf16[2,1568,128]{2,1,0:T(8,128)(2,1)S(1)}, u32[]{:S(2)}, u32[]{:S(2)}) collective-permute-start(bf16[2,1568,128]{2,1,0:T(8,128)(2,1)S(1)} %get-tuple-element.42), channel_id=1, source_target_pairs={{4,8},{8,4},{12,16},{16,12},{20,24},{24,20},{5,9},{9,5},{13,17},{1... | collective-permute-start | bytes 2408456 | tf_op jit(solution)/shard_map/ppermute | solution.py:41
  33.5 26.0 %collective-permute-start.6 = (bf16[2,528,128]{2,1,0:T(8,128)(2,1)S(1)}, bf16[2,528,128]{2,1,0:T(8,128)(2,1)S(1)}, u32[]{:S(2)}, u32[]{:S(2)}) collective-permute-start(bf16[2,528,128]{2,1,0:T(8,128)(2,1)S(1)} %get-tuple-element.50), channel_id=1, source_target_pairs={{0,4},{4,0},{8,12},{12,8},{16,20},{20,16},{24,28},{28,24},{1,5},{5... | collective-permute-start | bytes 811016 | tf_op jit(solution)/shard_map/ppermute | solution.py:41
  35.2 24.3 %collective-permute-start.7 = (bf16[2,528,128]{2,1,0:T(8,128)(2,1)S(1)}, bf16[2,528,128]{2,1,0:T(8,128)(2,1)S(1)}, u32[]{:S(2)}, u32[]{:S(2)}) collective-permute-start(bf16[2,528,128]{2,1,0:T(8,128)(2,1)S(1)} %get-tuple-element.51), channel_id=1, source_target_pairs={{4,8},{8,4},{12,16},{16,12},{20,24},{24,20},{5,9},{9,5},{13,17},{1... | collective-permute-start | bytes 811016 | tf_op jit(solution)/shard_map/ppermute | solution.py:41
  64.1 27.1 %copy-start.3 = (f32[2,8,1024]{2,1,0:T(8,128)S(1)}, f32[2,8,1024]{2,1,0:T(8,128)}, u32[]{:S(2)}) copy-start(f32[2,8,1024]{2,1,0:T(8,128)} %param.12) | copy-start | bytes 196612
  69.4 2.0 %collective-permute-start.8 = (bf16[512,128]{1,0:T(8,128)(2,1)S(1)}, bf16[512,128]{1,0:T(8,128)(2,1)S(1)}, u32[]{:S(2)}, u32[]{:S(2)}) collective-permute-start(bf16[512,128]{1,0:T(8,128)(2,1)S(1)} %get-tuple-element.54), channel_id=1, source_target_pairs={{0,4},{4,0},{8,12},{12,8},{16,20},{20,16},{24,28},{28,24},{1,5},{5... | collective-permute-start | bytes 393224 | tf_op jit(solution)/shard_map/ppermute | solution.py:41
  69.5 7.2 %collective-permute-start.9 = (bf16[512,128]{1,0:T(8,128)(2,1)S(1)}, bf16[512,128]{1,0:T(8,128)(2,1)S(1)}, u32[]{:S(2)}, u32[]{:S(2)}) collective-permute-start(bf16[512,128]{1,0:T(8,128)(2,1)S(1)} %get-tuple-element.54), channel_id=1, source_target_pairs={{4,8},{8,4},{12,16},{16,12},{20,24},{24,20},{5,9},{9,5},{13,17},{1... | collective-permute-start | bytes 393224 | tf_op jit(solution)/shard_map/ppermute | solution.py:41
  79.3 10.3 %collective-permute-start.12 = (bf16[2,8,1024]{2,1,0:T(8,128)(2,1)S(1)}, bf16[2,8,1024]{2,1,0:T(8,128)(2,1)S(1)}, u32[]{:S(2)}, u32[]{:S(2)}) collective-permute-start(bf16[2,8,1024]{2,1,0:T(8,128)(2,1)S(1)} %get-tuple-element.56), channel_id=1, source_target_pairs={{0,3},{4,7},{8,11},{12,15},{16,19},{20,23},{24,27},{28,31}} | collective-permute-start | bytes 98312 | tf_op jit(solution)/shard_map/ppermute | solution.py:32
  85.8 3.8 %collective-permute-start.11 = (bf16[2,8,1024]{2,1,0:T(8,128)(2,1)S(1)}, bf16[2,8,1024]{2,1,0:T(8,128)(2,1)S(1)}, u32[]{:S(2)}, u32[]{:S(2)}) collective-permute-start(bf16[2,8,1024]{2,1,0:T(8,128)(2,1)S(1)} %get-tuple-element.56), channel_id=1, source_target_pairs={{0,2},{1,3},{4,6},{5,7},{8,10},{9,11},{12,14},{13,15},{16,18},{17,... | collective-permute-start | bytes 98312 | tf_op jit(solution)/shard_map/ppermute | solution.py:32
  87.1 4.1 %collective-permute-start.10 = (bf16[2,8,1024]{2,1,0:T(8,128)(2,1)S(1)}, bf16[2,8,1024]{2,1,0:T(8,128)(2,1)S(1)}, u32[]{:S(2)}, u32[]{:S(2)}) collective-permute-start(bf16[2,8,1024]{2,1,0:T(8,128)(2,1)S(1)} %get-tuple-element.56), channel_id=1, source_target_pairs={{0,1},{1,2},{2,3},{4,5},{5,6},{6,7},{8,9},{9,10},{10,11},{12,13},{... | collective-permute-start | bytes 98312 | tf_op jit(solution)/shard_map/ppermute | solution.py:32

commit v5 on v4

--- a/solution.py
+++ b/solution.py
@@ -729,7 +729,6 @@
         )
 
     halo = pltpu.VMEM((2 * REACH, full, feat), BF16)
-    turning = pltpu.VMEM((2, rows, LANES, LANES), F32)
     turning4 = pltpu.VMEM((4, rows, LANES, LANES), F32)
     whole = pltpu.VMEM((deep, full, feat), BF16)
     flow0_shape = shape((2, rows, span), F32)
@@ -755,7 +754,7 @@
     _, flow3 = call(
         front_scores_kernel, (even, ref, front_a, front_b, pred_a, pred_b, offsets, flow0),
         [VMEM] * 8, (ref_shape, shape((2, rows, cols), F32)),
-        [pltpu.VMEM((rows, bands, half), F32), turning, dma((2,))], score_cost(0.5), 12, {1: 0},
+        [pltpu.VMEM((rows, bands, half), F32), turning4, dma((2,))], score_cost(0.5), 14, {1: 0},
     )
 
     tiles = 2 * (cols // LANES) + span // LANES
@@ -763,7 +762,7 @@
     flow2, pack = call(
         back_scores_kernel, (back_in, odd, beyond, mask, flow1, flow3), [VMEM] * 6,
         (shape((3, rows, span), F32), shape((pack_rows, LANES), BF16)),
-        [pltpu.VMEM((rows, bands, span), F32), turning], score_cost(0.55), 12,
+        [pltpu.VMEM((rows, bands, span), F32), turning4], score_cost(0.55), 14,
     )
     flows_b = swap(pack, 1)
     flows_a = swap(pack, 0)

time: 92.9 us -> 91.9 us (0.989)
  Pallas kernels: 39.1 us -> 38.1 us
    pallas_call x8, Pallas kernels: 36.5 us -> 35.5 us  [call(): pl.pallas_call(functools.partial(kernel, half), out_shape=outs, in_specs=...]
where the time goes in v5:
time: 91.9 us; the launch traced here: 90.8 us
  Pallas kernels  38.1 us (41%)
  starting transfers between devices  29.1 us (32%)
  waiting for transfers between devices  22.7 us (25%)
    pallas_call x8, Pallas kernels, call(): pl.pallas_call(functools.partial(kernel, half), out_shape=outs, in_specs=...  35.5 us
    ppermute x5, starting transfers between devices, hop(): return lax.ppermute(value, axis, pairs)  15.1 us
    ppermute x8, starting transfers between devices, swap(): return lax.ppermute(value, ('tile', 'sec') if plane else 'tile', pairs)  14 us
    ppermute x5, waiting for transfers between devices, hop(): return lax.ppermute(value, axis, pairs)  12.7 us
    ppermute x8, waiting for transfers between devices, swap(): return lax.ppermute(value, ('tile', 'sec') if plane else 'tile', pairs)  9.94 us
    pallas_call x1, Pallas kernels, shards(): pl.pallas_call(functools.partial(relax_kernel, half), out_shape=(shape((2...  2.61 us
  transfers between devices with their start and end apart: 13, of which 4 were waited for; matrix products, arithmetic and copies ran while one was open for 0% of the time, Pallas kernels for 29%

profile of v5, /device:TPU:4, one launch (start us, length us, event | category | flops | bytes accessed | tf_op | source)
XLA Modules:
  0.0 90.8 jit_solution(12464170554820011338)
XLA Ops:
  0.0 4.9 %shard_map.82 = (bf16[8,528,128]{2,1,0:T(8,128)(2,1)S(1)}, bf16[12,1280,128]{2,1,0:T(8,128)(2,1)S(1)}, bf16[256,512]{1,0:T(8,128)(2,1)S(1)}, bf16[512,128]{1,0:T...) custom-call(bf16[2,8,1024,256]{3,2,1,0:T(8,128)(2,1)} %pix_ref.5, ...), custom_call_target="tpu_custom_call" | custom-call | flops 1711276032 | bytes 3342336 | tf_op jit(solution)/shard_map/pallas_call | solution.py:676
  4.9 3.5 %collective-permute-start.5 = (bf16[8,528,128]{2,1,0:T(8,128)(2,1)S(1)}, bf16[8,528,128]{2,1,0:T(8,128)(2,1)S(1)}, u32[]{:S(2)}, u32[]{:S(2)}) collective-permute-start(bf16[8,528,128]{2,1,0:T(8,128)(2,1)S(1)} %get-tuple-element.46), channel_id=1, source_target_pairs={{0,1},{1,2},{2,3},{4,5},{5,6},{6,7},{8,9},{9,10},{10,11},{12,13},{... | collective-permute-start | bytes 3244040 | tf_op jit(solution)/shard_map/ppermute | solution.py:32
  8.5 5.0 %shard_map.83 = (bf16[12,1280,128]{2,1,0:T(8,128)(2,1)S(1)}, bf16[12,1280,128]{2,1,0:T(8,128)(2,1)S(1)}, bf16[4384,128]{1,0:T(8,128)(2,1)S(1)}, bf16[2,1568,128]...) custom-call(bf16[2,8,1024,256]{3,2,1,0:T(8,128)(2,1)S(1)} %copy-done, ...), custom_call_target="tpu_custom_call", output_to_operand_aliasing={{0}: (4, {})} | custom-call | flops 3422552064 | bytes 6684672 | tf_op jit(solution)/shard_map/pallas_call | solution.py:676
  13.5 1.3 %collective-permute-start = (bf16[4384,128]{1,0:T(8,128)(2,1)S(1)}, bf16[4384,128]{1,0:T(8,128)(2,1)S(1)}, u32[]{:S(2)}, u32[]{:S(2)}) collective-permute-start(bf16[4384,128]{1,0:T(8,128)(2,1)S(1)} %get-tuple-element.36), channel_id=1, source_target_pairs={{1,0},{2,1},{3,2},{5,4},{6,5},{7,6},{9,8},{10,9},{11,10},{13,12},{... | collective-permute-start | bytes 3366920 | tf_op jit(solution)/shard_map/ppermute | solution.py:32
  14.8 1.9 %collective-permute-start.3 = (bf16[2,1024,128]{2,1,0:T(8,128)(2,1)S(1)}, bf16[2,1024,128]{2,1,0:T(8,128)(2,1)S(1)}, u32[]{:S(2)}, u32[]{:S(2)}) collective-permute-start(bf16[2,1024,128]{2,1,0:T(8,128)(2,1)S(1)} %get-tuple-element.43), channel_id=1, source_target_pairs={{0,4},{4,0},{8,12},{12,8},{16,20},{20,16},{24,28},{28,24}} | collective-permute-start | bytes 1572872 | tf_op jit(solution)/shard_map/ppermute | solution.py:41
  16.8 3.4 %collective-permute-start.4 = (bf16[2,1024,128]{2,1,0:T(8,128)(2,1)S(1)}, bf16[2,1024,128]{2,1,0:T(8,128)(2,1)S(1)}, u32[]{:S(2)}, u32[]{:S(2)}) collective-permute-start(bf16[2,1024,128]{2,1,0:T(8,128)(2,1)S(1)} %get-tuple-element.44), channel_id=1, source_target_pairs={{4,8},{8,4},{12,16},{16,12},{20,24},{24,20}} | collective-permute-start | bytes 1572872 | tf_op jit(solution)/shard_map/ppermute | solution.py:41
  20.2 0.1 collective-permute-start.1
  20.3 11.2 %collective-permute-done.5.front_ref = bf16[8,528,128]{2,1,0:T(8,128)(2,1)S(1)} collective-permute-done((bf16[8,528,128]{2,1,0:T(8,128)(2,1)S(1)}, bf16[8,528,128]{2,1,0:T(8,128)(2,1)S(1)}, u32[]{:S(2)}, u32[]{:S(2)}) %collective-permute-start.5) | collective-permute-done | bytes 1081376 | tf_op jit(solution)/shard_map/ppermute | solution.py:32
  31.5 1.9 %collective-permute-start.2 = (bf16[2,1568,128]{2,1,0:T(8,128)(2,1)S(1)}, bf16[2,1568,128]{2,1,0:T(8,128)(2,1)S(1)}, u32[]{:S(2)}, u32[]{:S(2)}) collective-permute-start(bf16[2,1568,128]{2,1,0:T(8,128)(2,1)S(1)} %get-tuple-element.42), channel_id=1, source_target_pairs={{4,8},{8,4},{12,16},{16,12},{20,24},{24,20},{5,9},{9,5},{13,17},{1... | collective-permute-start | bytes 2408456 | tf_op jit(solution)/shard_map/ppermute | solution.py:41
  33.4 0.1 shard_map.87
  33.5 0.0 collective-permute-done.3.pred_a_ref
  33.5 1.7 %collective-permute-start.6 = (bf16[2,528,128]{2,1,0:T(8,128)(2,1)S(1)}, bf16[2,528,128]{2,1,0:T(8,128)(2,1)S(1)}, u32[]{:S(2)}, u32[]{:S(2)}) collective-permute-start(bf16[2,528,128]{2,1,0:T(8,128)(2,1)S(1)} %get-tuple-element.50), channel_id=1, source_target_pairs={{0,4},{4,0},{8,12},{12,8},{16,20},{20,16},{24,28},{28,24},{1,5},{5... | collective-permute-start | bytes 811016 | tf_op jit(solution)/shard_map/ppermute | solution.py:41
  35.2 3.0 %collective-permute-start.7 = (bf16[2,528,128]{2,1,0:T(8,128)(2,1)S(1)}, bf16[2,528,128]{2,1,0:T(8,128)(2,1)S(1)}, u32[]{:S(2)}, u32[]{:S(2)}) collective-permute-start(bf16[2,528,128]{2,1,0:T(8,128)(2,1)S(1)} %get-tuple-element.51), channel_id=1, source_target_pairs={{4,8},{8,4},{12,16},{16,12},{20,24},{24,20},{5,9},{9,5},{13,17},{1... | collective-permute-start | bytes 811016 | tf_op jit(solution)/shard_map/ppermute | solution.py:41
  38.2 2.7 %shard_map.84 = (bf16[12,1280,128]{2,1,0:T(8,128)(2,1)S(1)}, bf16[12,1280,128]{2,1,0:T(8,128)(2,1)S(1)}) custom-call(bf16[2,8,1024,256]{3,2,1,0:T(8,128)(2,1)S(1)} %copy-done, bf16[256,512]{1,0:T(8,128)(2,1)S(1)} %get-tuple-element.32.wh_ref, bf16[512,128]{1,0:T(8,128)(2,1)S(1)} %get-tuple-element.33.wf_ref, ...), custom_call_target="tpu_custom_call", output_to_operand_aliasing={{0}: (4, {}), {1}: (5, {})} | custom-call | flops 1711276032 | bytes 3342336 | tf_op jit(solution)/shard_map/pallas_call | solution.py:676
  40.8 9.0 %shard_map.85 = (f32[8,80,1024]{2,1,0:T(8,128)S(1)}, f32[2,8,640]{2,1,0:T(8,128)S(1)}) custom-call(bf16[12,1280,128]{2,1,0:T(8,128)(2,1)S(1)} %get-tuple-element.40.even_ref, bf16[12,1280,128]{2,1,0:T(8,128)(2,1)S(1)} %get-tuple-element.39.odd_ref, bf16[8,1024,128]{2,1,0:T(8,128)(2,1)} %pred_ref.5, ...), custom_call_target="tpu_custom_call" | custom-call | flops 1342177280 | bytes 2097152 | tf_op jit(solution)/shard_map/pallas_call | solution.py:676
  49.8 4.7 %collective-permute-done.2.pack_b_ref = bf16[2,1568,128]{2,1,0:T(8,128)(2,1)S(1)} collective-permute-done((bf16[2,1568,128]{2,1,0:T(8,128)(2,1)S(1)}, bf16[2,1568,128]{2,1,0:T(8,128)(2,1)S(1)}, u32[]{:S(2)}, u32[]{:S(2)}) %collective-permute-start.2) | collective-permute-done | bytes 802848 | tf_op jit(solution)/shard_map/ppermute | solution.py:41
  54.5 5.0 %shard_map.86 = (f32[8,80,1024]{2,1,0:T(8,128)S(1)}, f32[2,8,1024]{2,1,0:T(8,128)S(1)}, bf16[12,896,128]{2,1,0:T(8,128)(2,1)S(1)}, bf16[4,1280,128]{2,1,0:T(8,128)(2,1)S(1)}) custom-call(bf16[12,1280,128]{2,1,0:T(8,128)(2,1)S(1)} %get-tuple-element.40.even_ref, ...), custom_call_target="tpu_custom_call", output_to_operand_aliasing={{0}: (5, {})} | custom-call | flops 1342177280 | bytes 2097152 | tf_op jit(solution)/shard_map/pallas_call | solution.py:676
  59.5 0.0 collective-permute-done.6.front_a_ref
  59.5 4.4 %shard_map.88 = (bf16[12,896,128]{2,1,0:T(8,128)(2,1)S(1)}, f32[2,8,1024]{2,1,0:T(8,128)S(1)}) custom-call(bf16[12,1280,128]{2,1,0:T(8,128)(2,1)S(1)} %get-tuple-element.40.even_ref, bf16[12,896,128]{2,1,0:T(8,128)(2,1)S(1)} %get-tuple-element.49.ref_in, ...), custom_call_target="tpu_custom_call", output_to_operand_aliasing={{0}: (1, {})} | custom-call | flops 1342177280 | bytes 2097152 | tf_op jit(solution)/shard_map/pallas_call | solution.py:676
  63.9 0.0 collective-permute-done.back_ref
  63.9 0.0 copy-start.3
  63.9 4.4 %shard_map.89 = (f32[3,8,640]{2,1,0:T(8,128)S(1)}, bf16[512,128]{1,0:T(8,128)(2,1)S(1)}) custom-call(bf16[4384,128]{1,0:T(8,128)(2,1)S(1)} %collective-permute-done.back_ref, bf16[12,1280,128]{2,1,0:T(8,128)(2,1)S(1)} %get-tuple-element.39.odd_ref, bf16[4,1280,128]{2,1,0:T(8,128)(2,1)S(1)} %get-tuple-element.47.halo_ref, s32[2,8,1024]{2,1,0:T(8,128)S(1)} %copy-done.2, ...), custom_call_target="tpu_custom_call" | custom-call | flops 1476395008 | bytes 2306867 | tf_op jit(solution)/shard_map/pallas_call | solution.py:676
  68.4 0.1 collective-permute-start.8
  68.5 1.9 %collective-permute-start.9 = (bf16[512,128]{1,0:T(8,128)(2,1)S(1)}, bf16[512,128]{1,0:T(8,128)(2,1)S(1)}, u32[]{:S(2)}, u32[]{:S(2)}) collective-permute-start(bf16[512,128]{1,0:T(8,128)(2,1)S(1)} %get-tuple-element.54), channel_id=1, source_target_pairs={{4,8},{8,4},{12,16},{16,12},{20,24},{24,20},{5,9},{9,5},{13,17},{1... | collective-permute-start | bytes 393224 | tf_op jit(solution)/shard_map/ppermute | solution.py:41
  70.4 5.2 %collective-permute-done.9.pack_b_ref = bf16[512,128]{1,0:T(8,128)(2,1)S(1)} collective-permute-done((bf16[512,128]{1,0:T(8,128)(2,1)S(1)}, bf16[512,128]{1,0:T(8,128)(2,1)S(1)}, u32[]{:S(2)}, u32[]{:S(2)}) %collective-permute-start.9) | collective-permute-done | bytes 131104 | tf_op jit(solution)/shard_map/ppermute | solution.py:41
  75.7 2.6 %relax.1 = (f32[2,8,1024]{2,1,0:T(8,128)S(1)}, f32[2,8,1024]{2,1,0:T(8,128)S(1)}, bf16[2,8,1024]{2,1,0:T(8,128)(2,1)S(1)}) custom-call(bf16[512,128]{1,0:T(8,128)(2,1)S(1)} %collective-permute-done.8.pack_a_ref, bf16[512,128]{1,0:T(8,128)(2,1)S(1)} %collective-permute-done.9.pack_b_ref, f32[2,8,1024]{2,1,0:T(8,128)S(1)} %get-tuple-element.48.flow1_ref, ...), custom_call_target="tpu_custom_call" | custom-call | flops 18874368 | bytes 327680 | tf_op jit(solution)/shard_map/relax/pallas_call | solution.py:771
  78.3 6.5 %collective-permute-start.12 = (bf16[2,8,1024]{2,1,0:T(8,128)(2,1)S(1)}, bf16[2,8,1024]{2,1,0:T(8,128)(2,1)S(1)}, u32[]{:S(2)}, u32[]{:S(2)}) collective-permute-start(bf16[2,8,1024]{2,1,0:T(8,128)(2,1)S(1)} %get-tuple-element.56), channel_id=1, source_target_pairs={{0,3},{4,7},{8,11},{12,15},{16,19},{20,23},{24,27},{28,31}} | collective-permute-start | bytes 98312 | tf_op jit(solution)/shard_map/ppermute | solution.py:32
  84.8 1.3 %collective-permute-start.11 = (bf16[2,8,1024]{2,1,0:T(8,128)(2,1)S(1)}, bf16[2,8,1024]{2,1,0:T(8,128)(2,1)S(1)}, u32[]{:S(2)}, u32[]{:S(2)}) collective-permute-start(bf16[2,8,1024]{2,1,0:T(8,128)(2,1)S(1)} %get-tuple-element.56), channel_id=1, source_target_pairs={{0,2},{1,3},{4,6},{5,7},{8,10},{9,11},{12,14},{13,15},{16,18},{17,... | collective-permute-start | bytes 98312 | tf_op jit(solution)/shard_map/ppermute | solution.py:32
  86.1 2.5 %collective-permute-start.10 = (bf16[2,8,1024]{2,1,0:T(8,128)(2,1)S(1)}, bf16[2,8,1024]{2,1,0:T(8,128)(2,1)S(1)}, u32[]{:S(2)}, u32[]{:S(2)}) collective-permute-start(bf16[2,8,1024]{2,1,0:T(8,128)(2,1)S(1)} %get-tuple-element.56), channel_id=1, source_target_pairs={{0,1},{1,2},{2,3},{4,5},{5,6},{6,7},{8,9},{9,10},{10,11},{12,13},{... | collective-permute-start | bytes 98312 | tf_op jit(solution)/shard_map/ppermute | solution.py:32
  88.6 0.0 collective-permute-done.11
  88.6 1.6 %collective-permute-done.10 = bf16[2,8,1024]{2,1,0:T(8,128)(2,1)S(1)} collective-permute-done((bf16[2,8,1024]{2,1,0:T(8,128)(2,1)S(1)}, bf16[2,8,1024]{2,1,0:T(8,128)(2,1)S(1)}, u32[]{:S(2)}, u32[]{:S(2)}) %collective-permute-start.10) | collective-permute-done | bytes 32800 | tf_op jit(solution)/shard_map/ppermute | solution.py:32
  90.2 0.7 pad_maximum_fusion
  (13 shorter events, 0.1 us)
Async XLA Ops:
  0.0 8.5 %copy-start = (bf16[2,8,1024,256]{3,2,1,0:T(8,128)(2,1)S(1)}, bf16[2,8,1024,256]{3,2,1,0:T(8,128)(2,1)}, u32[]{:S(2)}) copy-start(bf16[2,8,1024,256]{3,2,1,0:T(8,128)(2,1)} %pix_ref.5) | copy-start | bytes 25165828
  0.0 8.5 %copy-start.1 = (s32[2,2,8,1024]{3,2,1,0:T(8,128)S(1)}, s32[2,2,8,1024]{3,2,1,0:T(8,128)}, u32[]{:S(2)}) copy-start(s32[2,2,8,1024]{3,2,1,0:T(8,128)} %off_ref.7) | copy-start | bytes 393220
  0.0 8.5 %copy-start.2 = (s32[2,8,1024]{2,1,0:T(8,128)S(1)}, s32[2,8,1024]{2,1,0:T(8,128)}, u32[]{:S(2)}) copy-start(s32[2,8,1024]{2,1,0:T(8,128)} %mask_ref.5) | copy-start | bytes 196612
  4.9 26.6 %collective-permute-start.5 = (bf16[8,528,128]{2,1,0:T(8,128)(2,1)S(1)}, bf16[8,528,128]{2,1,0:T(8,128)(2,1)S(1)}, u32[]{:S(2)}, u32[]{:S(2)}) collective-permute-start(bf16[8,528,128]{2,1,0:T(8,128)(2,1)S(1)} %get-tuple-element.46), channel_id=1, source_target_pairs={{0,1},{1,2},{2,3},{4,5},{5,6},{6,7},{8,9},{9,10},{10,11},{12,13},{... | collective-permute-start | bytes 3244040 | tf_op jit(solution)/shard_map/ppermute | solution.py:32
  13.5 50.4 %collective-permute-start = (bf16[4384,128]{1,0:T(8,128)(2,1)S(1)}, bf16[4384,128]{1,0:T(8,128)(2,1)S(1)}, u32[]{:S(2)}, u32[]{:S(2)}) collective-permute-start(bf16[4384,128]{1,0:T(8,128)(2,1)S(1)} %get-tuple-element.36), channel_id=1, source_target_pairs={{1,0},{2,1},{3,2},{5,4},{6,5},{7,6},{9,8},{10,9},{11,10},{13,12},{... | collective-permute-start | bytes 3366920 | tf_op jit(solution)/shard_map/ppermute | solution.py:32
  14.8 18.7 %collective-permute-start.3 = (bf16[2,1024,128]{2,1,0:T(8,128)(2,1)S(1)}, bf16[2,1024,128]{2,1,0:T(8,128)(2,1)S(1)}, u32[]{:S(2)}, u32[]{:S(2)}) collective-permute-start(bf16[2,1024,128]{2,1,0:T(8,128)(2,1)S(1)} %get-tuple-element.43), channel_id=1, source_target_pairs={{0,4},{4,0},{8,12},{12,8},{16,20},{20,16},{24,28},{28,24}} | collective-permute-start | bytes 1572872 | tf_op jit(solution)/shard_map/ppermute | solution.py:41
  16.8 18.4 %collective-permute-start.4 = (bf16[2,1024,128]{2,1,0:T(8,128)(2,1)S(1)}, bf16[2,1024,128]{2,1,0:T(8,128)(2,1)S(1)}, u32[]{:S(2)}, u32[]{:S(2)}) collective-permute-start(bf16[2,1024,128]{2,1,0:T(8,128)(2,1)S(1)} %get-tuple-element.44), channel_id=1, source_target_pairs={{4,8},{8,4},{12,16},{16,12},{20,24},{24,20}} | collective-permute-start | bytes 1572872 | tf_op jit(solution)/shard_map/ppermute | solution.py:41
  20.2 29.6 %collective-permute-start.1 = (bf16[2,1568,128]{2,1,0:T(8,128)(2,1)S(1)}, bf16[2,1568,128]{2,1,0:T(8,128)(2,1)S(1)}, u32[]{:S(2)}, u32[]{:S(2)}) collective-permute-start(bf16[2,1568,128]{2,1,0:T(8,128)(2,1)S(1)} %get-tuple-element.41), channel_id=1, source_target_pairs={{0,4},{4,0},{8,12},{12,8},{16,20},{20,16},{24,28},{28,24},{1,5},{5... | collective-permute-start | bytes 2408456 | tf_op jit(solution)/shard_map/ppermute | solution.py:41
  31.5 23.0 %collective-permute-start.2 = (bf16[2,1568,128]{2,1,0:T(8,128)(2,1)S(1)}, bf16[2,1568,128]{2,1,0:T(8,128)(2,1)S(1)}, u32[]{:S(2)}, u32[]{:S(2)}) collective-permute-start(bf16[2,1568,128]{2,1,0:T(8,128)(2,1)S(1)} %get-tuple-element.42), channel_id=1, source_target_pairs={{4,8},{8,4},{12,16},{16,12},{20,24},{24,20},{5,9},{9,5},{13,17},{1... | collective-permute-start | bytes 2408456 | tf_op jit(solution)/shard_map/ppermute | solution.py:41
  33.5 26.0 %collective-permute-start.6 = (bf16[2,528,128]{2,1,0:T(8,128)(2,1)S(1)}, bf16[2,528,128]{2,1,0:T(8,128)(2,1)S(1)}, u32[]{:S(2)}, u32[]{:S(2)}) collective-permute-start(bf16[2,528,128]{2,1,0:T(8,128)(2,1)S(1)} %get-tuple-element.50), channel_id=1, source_target_pairs={{0,4},{4,0},{8,12},{12,8},{16,20},{20,16},{24,28},{28,24},{1,5},{5... | collective-permute-start | bytes 811016 | tf_op jit(solution)/shard_map/ppermute | solution.py:41
  35.2 24.3 %collective-permute-start.7 = (bf16[2,528,128]{2,1,0:T(8,128)(2,1)S(1)}, bf16[2,528,128]{2,1,0:T(8,128)(2,1)S(1)}, u32[]{:S(2)}, u32[]{:S(2)}) collective-permute-start(bf16[2,528,128]{2,1,0:T(8,128)(2,1)S(1)} %get-tuple-element.51), channel_id=1, source_target_pairs={{4,8},{8,4},{12,16},{16,12},{20,24},{24,20},{5,9},{9,5},{13,17},{1... | collective-permute-start | bytes 811016 | tf_op jit(solution)/shard_map/ppermute | solution.py:41
  63.9 26.2 %copy-start.3 = (f32[2,8,1024]{2,1,0:T(8,128)S(1)}, f32[2,8,1024]{2,1,0:T(8,128)}, u32[]{:S(2)}) copy-start(f32[2,8,1024]{2,1,0:T(8,128)} %param.12) | copy-start | bytes 196612
  68.4 2.0 %collective-permute-start.8 = (bf16[512,128]{1,0:T(8,128)(2,1)S(1)}, bf16[512,128]{1,0:T(8,128)(2,1)S(1)}, u32[]{:S(2)}, u32[]{:S(2)}) collective-permute-start(bf16[512,128]{1,0:T(8,128)(2,1)S(1)} %get-tuple-element.54), channel_id=1, source_target_pairs={{0,4},{4,0},{8,12},{12,8},{16,20},{20,16},{24,28},{28,24},{1,5},{5... | collective-permute-start | bytes 393224 | tf_op jit(solution)/shard_map/ppermute | solution.py:41
  68.5 7.2 %collective-permute-start.9 = (bf16[512,128]{1,0:T(8,128)(2,1)S(1)}, bf16[512,128]{1,0:T(8,128)(2,1)S(1)}, u32[]{:S(2)}, u32[]{:S(2)}) collective-permute-start(bf16[512,128]{1,0:T(8,128)(2,1)S(1)} %get-tuple-element.54), channel_id=1, source_target_pairs={{4,8},{8,4},{12,16},{16,12},{20,24},{24,20},{5,9},{9,5},{13,17},{1... | collective-permute-start | bytes 393224 | tf_op jit(solution)/shard_map/ppermute | solution.py:41
  78.3 10.3 %collective-permute-start.12 = (bf16[2,8,1024]{2,1,0:T(8,128)(2,1)S(1)}, bf16[2,8,1024]{2,1,0:T(8,128)(2,1)S(1)}, u32[]{:S(2)}, u32[]{:S(2)}) collective-permute-start(bf16[2,8,1024]{2,1,0:T(8,128)(2,1)S(1)} %get-tuple-element.56), channel_id=1, source_target_pairs={{0,3},{4,7},{8,11},{12,15},{16,19},{20,23},{24,27},{28,31}} | collective-permute-start | bytes 98312 | tf_op jit(solution)/shard_map/ppermute | solution.py:32
  84.8 3.8 %collective-permute-start.11 = (bf16[2,8,1024]{2,1,0:T(8,128)(2,1)S(1)}, bf16[2,8,1024]{2,1,0:T(8,128)(2,1)S(1)}, u32[]{:S(2)}, u32[]{:S(2)}) collective-permute-start(bf16[2,8,1024]{2,1,0:T(8,128)(2,1)S(1)} %get-tuple-element.56), channel_id=1, source_target_pairs={{0,2},{1,3},{4,6},{5,7},{8,10},{9,11},{12,14},{13,15},{16,18},{17,... | collective-permute-start | bytes 98312 | tf_op jit(solution)/shard_map/ppermute | solution.py:32
  86.1 4.1 %collective-permute-start.10 = (bf16[2,8,1024]{2,1,0:T(8,128)(2,1)S(1)}, bf16[2,8,1024]{2,1,0:T(8,128)(2,1)S(1)}, u32[]{:S(2)}, u32[]{:S(2)}) collective-permute-start(bf16[2,8,1024]{2,1,0:T(8,128)(2,1)S(1)} %get-tuple-element.56), channel_id=1, source_target_pairs={{0,1},{1,2},{2,3},{4,5},{5,6},{6,7},{8,9},{9,10},{10,11},{12,13},{... | collective-permute-start | bytes 98312 | tf_op jit(solution)/shard_map/ppermute | solution.py:32
